TPU v7x, 32 devices: a whole 2x2x4 slice. The times are simulated.
32 devices in a mesh: tensor: 4 (over y, x), sub: 2 (over core), group: 4 (over z).
Axes of the slice: x: 2, y: 2, z: 4, core: 2. Of those that a mesh axis runs over, the one named last changes fastest.
Arguments:
- frames: bfloat16 [8, 1024, 1536], P(('sub', 'group'), 'tensor'), may hold values from -6 to 6
- text_states: bfloat16 [8, 64, 1536], P(('sub', 'group')), may hold values from -6 to 6
- selfgain: float32 [1536], replicated, may hold values from 0.5 to 1.5
- selfbias: float32 [1536], replicated, may hold values from -1.5 to 1.5
- selfqkv: bfloat16 [1536, 3, 1536], P(None, None, 'tensor'), may hold values from -0.15625 to 0.15625
- selfout: bfloat16 [1536, 1536], P('tensor'), may hold values from -0.625 to 0.625
- crossgain: float32 [1536], replicated, may hold values from 0.5 to 1.5
- crossbias: float32 [1536], replicated, may hold values from -1.5 to 1.5
- crossquery: bfloat16 [1536, 1536], P(None, 'tensor'), may hold values from -0.15625 to 0.15625
- crosskv: bfloat16 [1536, 2, 1536], P(None, None, 'tensor'), may hold values from -0.15625 to 0.15625
- crossout: bfloat16 [1536, 1536], P('tensor'), may hold values from -0.4375 to 0.4375
- feedgain: float32 [1536], replicated, may hold values from 0.5 to 1.5
- feedbias: float32 [1536], replicated, may hold values from -1.5 to 1.5
- feedup: bfloat16 [1536, 6144], P(None, 'tensor'), may hold values from -0.15625 to 0.15625
- feeddown: bfloat16 [6144, 1536], P('tensor'), may hold values from -0.078125 to 0.078125
- cotangent: float32 [8, 1024, 1536], P(('sub', 'group'), 'tensor'), may hold values from -6 to 6
Outputs:
- layer_output: float32 [8, 1024, 1536], P(('sub', 'group'), 'tensor')
- frame_grad: float32 [8, 1024, 1536], P(('sub', 'group'), 'tensor')
- text_grad: float32 [8, 64, 1536], P(('sub', 'group'))
- selfgain_grad: float32 [1536], P('sub')
- selfbias_grad: float32 [1536], P('sub')
- selfqkv_grad: float32 [1536, 3, 1536], P('sub', None, 'tensor')
- selfout_grad: float32 [1536, 1536], P(('tensor', 'sub'))
- crossgain_grad: float32 [1536], P('sub')
- crossbias_grad: float32 [1536], P('sub')
- crossquery_grad: float32 [1536, 1536], P('sub', 'tensor')
- crosskv_grad: float32 [1536, 2, 1536], P('sub', None, 'tensor')
- crossout_grad: float32 [1536, 1536], P(('tensor', 'sub'))
- feedgain_grad: float32 [1536], P('sub')
- feedbias_grad: float32 [1536], P('sub')
- feedup_grad: float32 [1536, 6144], P('sub', 'tensor')
- feeddown_grad: float32 [6144, 1536], P(('tensor', 'sub'))
All inputs are finite; a program needn't handle non-finite values.
Results may differ from a plain program's by a relative error of at most 0.035.
Values may be sent and summed in bfloat16 or wider, within the bound.
A program may use at most 256 MiB of HBM per device.

v0:
```python
from functools import partial

import jax
import jax.numpy as jnp
from jax import lax
from jax.sharding import PartitionSpec as P

HEAD = 64


EPSILON = 1e-05
NEG_BIG = -1e30


def layer_norm(values, gain_row, bias_row):
    centre = values - jnp.mean(values, -1, keepdims=True)
    variance = jnp.mean(centre * centre, -1, keepdims=True)
    inverse = lax.rsqrt(variance + EPSILON)
    normed = centre * inverse
    return (normed * gain_row + bias_row, normed, inverse)


def norm_back(grad_out, normed, inverse, gain_row):
    scaled = grad_out * gain_row
    first_mean = jnp.mean(scaled, -1, keepdims=True)
    second_mean = jnp.mean(scaled * normed, -1, keepdims=True)
    grad_in = inverse * (scaled - first_mean - normed * second_mean)
    return (grad_in, jnp.sum(grad_out * normed, 0), jnp.sum(grad_out, 0))


def inner_rows(left_side, right_side):
    return lax.dot_general(
        left_side, right_side, (((0,), (0,)), ((), ())), preferred_element_type=jnp.float32
    )


def outer_cols(left_side, right_side):
    return lax.dot_general(
        left_side, right_side, (((1,), (1,)), ((), ())), preferred_element_type=jnp.float32
    )


def gather_rows(values):
    return lax.all_gather(values, "tensor", axis=0, tiled=True)


def gather_grads(values):
    return lax.all_gather(values, "tensor", axis=0, tiled=True)


def project_rows(left_side, weight):

    def partial_term(offset, count):
        return jnp.dot(left_side, weight, preferred_element_type=jnp.float32)

    return lax.psum_scatter(
        partial_term(
            jnp.int32(0), left_side.shape[0] // lax.axis_size("tensor") * lax.axis_size("tensor")
        ).astype(jnp.bfloat16),
        "tensor",
        scatter_dimension=0,
        tiled=True,
    ).astype(jnp.float32)


def project_back(grad_left, weight):

    def partial_term(offset, count):
        return outer_cols(grad_left, weight)

    return lax.psum_scatter(
        partial_term(
            jnp.int32(0), grad_left.shape[0] // lax.axis_size("tensor") * lax.axis_size("tensor")
        ).astype(jnp.bfloat16),
        "tensor",
        scatter_dimension=0,
        tiled=True,
    ).astype(jnp.float32)


def block_scores(query_block, key_vals, offset, causal):
    scaling = query_block.shape[-1] ** (-0.5)
    scores = (
        jnp.einsum("qhd,khd->hqk", query_block, key_vals, preferred_element_type=jnp.float32)
        * scaling
    )
    if causal:
        row_pos = offset + jnp.arange(scores.shape[1])
        key_pos = jnp.arange(scores.shape[2])
        scores = jnp.where(key_pos[None, None, :] <= row_pos[None, :, None], scores, NEG_BIG)
    return scores


def attend_forward(queries, key_vals, value_vals, causal):
    total_rows = queries.shape[0]
    block_rows = min(512, total_rows)
    outputs = []
    logsums = []
    for offset in range(0, total_rows, block_rows):
        scores = block_scores(queries[offset : offset + block_rows], key_vals, offset, causal)
        row_peak = jnp.max(scores, -1, keepdims=True)
        exponent = jnp.exp(scores - row_peak)
        totals = jnp.sum(exponent, -1, keepdims=True)
        weights = (exponent / totals).astype(jnp.bfloat16)
        outputs.append(
            jnp.einsum(
                "hqk,khd->qhd", weights, value_vals, preferred_element_type=jnp.float32
            ).astype(jnp.bfloat16)
        )
        logsums.append(row_peak + jnp.log(totals))
    return (jnp.concatenate(outputs, 0), jnp.concatenate(logsums, 1))


def attend_backward(queries, key_vals, value_vals, logsums, grad_heads, causal):
    total_rows = queries.shape[0]
    block_rows = min(512, total_rows)
    scaling = queries.shape[-1] ** (-0.5)
    grad_queries = []
    grad_keys = jnp.zeros(key_vals.shape, jnp.float32)
    grad_values = jnp.zeros(value_vals.shape, jnp.float32)
    for offset in range(0, total_rows, block_rows):
        query_block = queries[offset : offset + block_rows]
        grad_block = grad_heads[offset : offset + block_rows]
        scores = block_scores(query_block, key_vals, offset, causal)
        probs = jnp.exp(scores - logsums[:, offset : offset + block_rows])
        grad_probs = jnp.einsum(
            "qhd,khd->hqk", grad_block, value_vals, preferred_element_type=jnp.float32
        )
        centred = jnp.sum(grad_probs * probs, -1, keepdims=True)
        grad_scores = (probs * (grad_probs - centred)).astype(jnp.bfloat16)
        grad_queries.append(
            jnp.einsum("hqk,khd->qhd", grad_scores, key_vals, preferred_element_type=jnp.float32)
            * scaling
        )
        grad_keys = (
            grad_keys
            + jnp.einsum(
                "hqk,qhd->khd", grad_scores, query_block, preferred_element_type=jnp.float32
            )
            * scaling
        )
        grad_values = grad_values + jnp.einsum(
            "hqk,qhd->khd",
            probs.astype(jnp.bfloat16),
            grad_block,
            preferred_element_type=jnp.float32,
        )
    return (jnp.concatenate(grad_queries, 0), grad_keys, grad_values)


def local(
    frames,
    text_states,
    selfgain,
    selfbias,
    selfqkv,
    selfout,
    crossgain,
    crossbias,
    crossquery,
    crosskv,
    crossout,
    feedgain,
    feedbias,
    feedup,
    feeddown,
    cotangent,
):
    bfloat = jnp.bfloat16
    residual = frames[0].astype(jnp.float32)
    memory_rows = text_states[0]
    model_width = residual.shape[1]
    local_width = selfout.shape[0]
    head_size = HEAD
    local_heads = local_width // head_size
    text_rows = memory_rows.shape[0]
    qkv_flat = selfqkv.reshape(model_width, 3 * local_width)
    memory_flat = crosskv.reshape(model_width, 2 * local_width)
    normed_self, hat_self, inverse_self = layer_norm(residual, selfgain, selfbias)
    self_rows = gather_rows(normed_self.astype(bfloat))
    all_rows = self_rows.shape[0]
    triple = jnp.dot(self_rows, qkv_flat, preferred_element_type=jnp.float32).astype(bfloat)
    triple = triple.reshape(all_rows, 3, local_heads, head_size)
    self_heads, self_logsums = attend_forward(triple[:, 0], triple[:, 1], triple[:, 2], True)
    self_flat = self_heads.reshape(all_rows, local_width)
    after_self = residual + project_rows(self_flat, selfout)
    normed_cross, hat_cross, inverse_cross = layer_norm(after_self, crossgain, crossbias)
    cross_rows = gather_rows(normed_cross.astype(bfloat))
    cross_queries = jnp.dot(cross_rows, crossquery, preferred_element_type=jnp.float32).astype(
        bfloat
    )
    cross_queries = cross_queries.reshape(all_rows, local_heads, head_size)
    memory = jnp.dot(memory_rows, memory_flat, preferred_element_type=jnp.float32).astype(bfloat)
    memory = memory.reshape(text_rows, 2, local_heads, head_size)
    cross_heads, cross_logsums = attend_forward(cross_queries, memory[:, 0], memory[:, 1], False)
    cross_flat = cross_heads.reshape(all_rows, local_width)
    after_cross = after_self + project_rows(cross_flat, crossout)
    normed_feed, hat_feed, inverse_feed = layer_norm(after_cross, feedgain, feedbias)
    feed_rows = gather_rows(normed_feed.astype(bfloat))
    hidden_pre = jnp.dot(feed_rows, feedup, preferred_element_type=jnp.float32)
    hidden_act = jax.nn.gelu(hidden_pre, approximate=False).astype(bfloat)
    layer_output = after_cross + project_rows(hidden_act, feeddown)
    grad_top = cotangent[0]
    grad_feed = gather_grads(grad_top.astype(bfloat))
    feeddown_grad = inner_rows(hidden_act, grad_feed)
    grad_act = outer_cols(grad_feed, feeddown)
    unused_value, gelu_back = jax.vjp(partial(jax.nn.gelu, approximate=False), hidden_pre)
    grad_pre = gelu_back(grad_act)[0].astype(bfloat)
    feedup_grad = inner_rows(feed_rows, grad_pre)
    grad_norm_feed = project_back(grad_pre, feedup)
    grad_in_feed, feedgain_part, feedbias_part = norm_back(
        grad_norm_feed, hat_feed, inverse_feed, feedgain
    )
    grad_cross_out = grad_top + grad_in_feed
    grad_cross = gather_grads(grad_cross_out.astype(bfloat))
    crossout_grad = inner_rows(cross_flat, grad_cross)
    grad_cross_heads = (
        outer_cols(grad_cross, crossout).astype(bfloat).reshape(all_rows, local_heads, head_size)
    )
    grad_cq, grad_ck, grad_cv = attend_backward(
        cross_queries, memory[:, 0], memory[:, 1], cross_logsums, grad_cross_heads, False
    )
    grad_cq_flat = grad_cq.astype(bfloat).reshape(all_rows, local_width)
    grad_memory = (
        jnp.stack([grad_ck, grad_cv], 1).astype(bfloat).reshape(text_rows, 2 * local_width)
    )
    crossquery_grad = inner_rows(cross_rows, grad_cq_flat)
    crosskv_grad = inner_rows(memory_rows, grad_memory).reshape(model_width, 2, local_width)
    text_partial = outer_cols(grad_memory, memory_flat)
    grad_norm_cross = project_back(grad_cq_flat, crossquery)
    grad_in_cross, crossgain_part, crossbias_part = norm_back(
        grad_norm_cross, hat_cross, inverse_cross, crossgain
    )
    grad_self_out = grad_cross_out + grad_in_cross
    grad_self = gather_grads(grad_self_out.astype(bfloat))
    selfout_grad = inner_rows(self_flat, grad_self)
    grad_self_heads = (
        outer_cols(grad_self, selfout).astype(bfloat).reshape(all_rows, local_heads, head_size)
    )
    grad_sq, grad_sk, grad_sv = attend_backward(
        triple[:, 0], triple[:, 1], triple[:, 2], self_logsums, grad_self_heads, True
    )
    grad_triple = (
        jnp.stack([grad_sq, grad_sk, grad_sv], 1).astype(bfloat).reshape(all_rows, 3 * local_width)
    )
    selfqkv_grad = inner_rows(self_rows, grad_triple).reshape(model_width, 3, local_width)
    grad_norm_self = project_back(grad_triple, qkv_flat)
    grad_in_self, selfgain_part, selfbias_part = norm_back(
        grad_norm_self, hat_self, inverse_self, selfgain
    )
    frame_grad = grad_self_out + grad_in_self
    summed = (
        lax.psum(text_partial.astype(jnp.bfloat16), "tensor").astype(jnp.float32),
        lax.psum(selfgain_part.astype(jnp.bfloat16), "tensor").astype(jnp.float32),
        lax.psum(selfbias_part.astype(jnp.bfloat16), "tensor").astype(jnp.float32),
        lax.psum(crossgain_part.astype(jnp.bfloat16), "tensor").astype(jnp.float32),
        lax.psum(crossbias_part.astype(jnp.bfloat16), "tensor").astype(jnp.float32),
        lax.psum(feedgain_part.astype(jnp.bfloat16), "tensor").astype(jnp.float32),
        lax.psum(feedbias_part.astype(jnp.bfloat16), "tensor").astype(jnp.float32),
    )
    gradients = (
        summed[1],
        summed[2],
        selfqkv_grad,
        selfout_grad,
        summed[3],
        summed[4],
        crossquery_grad,
        crosskv_grad,
        crossout_grad,
        summed[5],
        summed[6],
        feedup_grad,
        feeddown_grad,
    )
    shards = (
        lax.psum_scatter(
            gradients[0].astype(jnp.bfloat16), "sub", scatter_dimension=0, tiled=True
        ).astype(jnp.float32),
        lax.psum_scatter(
            gradients[1].astype(jnp.bfloat16), "sub", scatter_dimension=0, tiled=True
        ).astype(jnp.float32),
        lax.psum_scatter(
            gradients[2].astype(jnp.bfloat16), "sub", scatter_dimension=0, tiled=True
        ).astype(jnp.float32),
        lax.psum_scatter(
            gradients[3].astype(jnp.bfloat16), "sub", scatter_dimension=0, tiled=True
        ).astype(jnp.float32),
        lax.psum_scatter(
            gradients[4].astype(jnp.bfloat16), "sub", scatter_dimension=0, tiled=True
        ).astype(jnp.float32),
        lax.psum_scatter(
            gradients[5].astype(jnp.bfloat16), "sub", scatter_dimension=0, tiled=True
        ).astype(jnp.float32),
        lax.psum_scatter(
            gradients[6].astype(jnp.bfloat16), "sub", scatter_dimension=0, tiled=True
        ).astype(jnp.float32),
        lax.psum_scatter(
            gradients[7].astype(jnp.bfloat16), "sub", scatter_dimension=0, tiled=True
        ).astype(jnp.float32),
        lax.psum_scatter(
            gradients[8].astype(jnp.bfloat16), "sub", scatter_dimension=0, tiled=True
        ).astype(jnp.float32),
        lax.psum_scatter(
            gradients[9].astype(jnp.bfloat16), "sub", scatter_dimension=0, tiled=True
        ).astype(jnp.float32),
        lax.psum_scatter(
            gradients[10].astype(jnp.bfloat16), "sub", scatter_dimension=0, tiled=True
        ).astype(jnp.float32),
        lax.psum_scatter(
            gradients[11].astype(jnp.bfloat16), "sub", scatter_dimension=0, tiled=True
        ).astype(jnp.float32),
        lax.psum_scatter(
            gradients[12].astype(jnp.bfloat16), "sub", scatter_dimension=0, tiled=True
        ).astype(jnp.float32),
    )
    reduced = (
        lax.psum(shards[0].astype(jnp.bfloat16), "group").astype(jnp.float32),
        lax.psum(shards[1].astype(jnp.bfloat16), "group").astype(jnp.float32),
        lax.psum(shards[2].astype(jnp.bfloat16), "group").astype(jnp.float32),
        lax.psum(shards[3].astype(jnp.bfloat16), "group").astype(jnp.float32),
        lax.psum(shards[4].astype(jnp.bfloat16), "group").astype(jnp.float32),
        lax.psum(shards[5].astype(jnp.bfloat16), "group").astype(jnp.float32),
        lax.psum(shards[6].astype(jnp.bfloat16), "group").astype(jnp.float32),
        lax.psum(shards[7].astype(jnp.bfloat16), "group").astype(jnp.float32),
        lax.psum(shards[8].astype(jnp.bfloat16), "group").astype(jnp.float32),
        lax.psum(shards[9].astype(jnp.bfloat16), "group").astype(jnp.float32),
        lax.psum(shards[10].astype(jnp.bfloat16), "group").astype(jnp.float32),
        lax.psum(shards[11].astype(jnp.bfloat16), "group").astype(jnp.float32),
        lax.psum(shards[12].astype(jnp.bfloat16), "group").astype(jnp.float32),
    )
    return (
        layer_output[None],
        frame_grad[None],
        summed[0][None],
        reduced[0],
        reduced[1],
        reduced[2],
        reduced[3],
        reduced[4],
        reduced[5],
        reduced[6],
        reduced[7],
        reduced[8],
        reduced[9],
        reduced[10],
        reduced[11],
        reduced[12],
    )


def solution(mesh):
    placed = (
        P(("sub", "group"), "tensor", None),
        P(("sub", "group"), None, None),
        P(),
        P(),
        P(None, None, "tensor"),
        P("tensor", None),
        P(),
        P(),
        P(None, "tensor"),
        P(None, None, "tensor"),
        P("tensor", None),
        P(),
        P(),
        P(None, "tensor"),
        P("tensor", None),
        P(("sub", "group"), "tensor", None),
    )
    return jax.shard_map(
        local,
        mesh=mesh,
        in_specs=placed,
        out_specs=(
            P(("sub", "group"), "tensor", None),
            P(("sub", "group"), "tensor", None),
            P(("sub", "group"), None, None),
            P("sub"),
            P("sub"),
            P("sub", None, "tensor"),
            P(("tensor", "sub"), None),
            P("sub"),
            P("sub"),
            P("sub", "tensor"),
            P("sub", None, "tensor"),
            P(("tensor", "sub"), None),
            P("sub"),
            P("sub"),
            P("sub", "tensor"),
            P(("tensor", "sub"), None),
        ),
        check_vma=False,
    )
```

profile of v0, /device:TPU:0, one launch (start us, length us, event | category | flops | bytes accessed | tf_op | source)
XLA Modules:
  0.0 1176.1 jit_solution(11678007954476885735)
XLA Ops:
  12.6 6.0 copy.54
  19.2 40.1 %all-gather.7.cloned.1.call-done = bf16[1024,1536]{1,0:T(8,128)(2,1)} async-done(((bf16[256,1536]{1,0:T(8,128)(2,1)}), bf16[1024,1536]{1,0:T(8,128)(2,1)}) %all-gather.7.cloned.1.call-update) | async-done | bytes 3145744 | tf_op jit(solution)/shard_map/all_gather | solution.py:44
  59.3 8.7 convolution_convert_fusion.8
  99.6 44.0 %reduce-scatter.13.cloned.1.call-done = bf16[256,1536]{1,0:T(8,128)(2,1)} async-done(((bf16[1024,1536]{1,0:T(8,128)(2,1)}), bf16[256,1536]{1,0:T(8,128)(2,1)}) %reduce-scatter.13.cloned.1.call-update) | async-done | bytes 786448 | tf_op jit(solution)/shard_map/reduce_scatter | solution.py:56
  153.2 39.4 %all-gather.9.cloned.1.call-done = bf16[1024,1536]{1,0:T(8,128)(2,1)} async-done(((bf16[256,1536]{1,0:T(8,128)(2,1)}), bf16[1024,1536]{1,0:T(8,128)(2,1)}) %all-gather.9.cloned.1.call-update) | async-done | bytes 3145744 | tf_op jit(solution)/shard_map/all_gather | solution.py:44
  203.6 44.0 %reduce-scatter.15.cloned.1.call-done = bf16[256,1536]{1,0:T(8,128)(2,1)} async-done(((bf16[1024,1536]{1,0:T(8,128)(2,1)}), bf16[256,1536]{1,0:T(8,128)(2,1)}) %reduce-scatter.15.cloned.1.call-update) | async-done | bytes 786448 | tf_op jit(solution)/shard_map/reduce_scatter | solution.py:56
  254.1 41.5 %all-gather.11.cloned.1.call-done = bf16[1024,1536]{1,0:T(8,128)(2,1)} async-done(((bf16[256,1536]{1,0:T(8,128)(2,1)}), bf16[1024,1536]{1,0:T(8,128)(2,1)}) %all-gather.11.cloned.1.call-update) | async-done | bytes 3145744 | tf_op jit(solution)/shard_map/all_gather | solution.py:44
  295.6 10.1 fusion.108
  305.7 36.0 %all-gather.13.cloned.1.call-done = bf16[1024,1536]{1,0:T(8,128)(2,1)} async-done(((bf16[256,1536]{1,0:T(8,128)(2,1)}), bf16[1024,1536]{1,0:T(8,128)(2,1)}) %all-gather.13.cloned.1.call-update) | async-done | bytes 3145744 | tf_op jit(solution)/shard_map/all_gather | solution.py:48
  341.7 24.5 %add_convert_fusion = (bf16[1024,1536]{1,0:T(8,128)(2,1)S(1)}, f32[1024,1536]{1,0:T(8,128)}) fusion(f32[1024,1536]{1,0:T(8,128)} %fusion.108, bf16[1024,1536]{1,0:T(8,128)(2,1)} %all-gather.13.cloned.1.call-done, bf16[1536,1536]{1,0:T(8,128)(2,1)} %param.30), kind=kOutput, calls=%fused_computation.24 | convolution fusion | flops 4945084416 | bytes 23592960 | tf_op jit(solution)/shard_map/dot_general | solution.py:38
  367.9 8.8 convolution_convert_fusion.4
  376.7 6.2 multiply_convert_fusion.2
  384.6 8.7 convolution_convert_fusion.5
  393.6 27.2 %reduce-scatter.19.cloned.1.call-done = bf16[256,1536]{1,0:T(8,128)(2,1)} async-done(((bf16[1024,1536]{1,0:T(8,128)(2,1)}), bf16[256,1536]{1,0:T(8,128)(2,1)}) %reduce-scatter.19.cloned.1.call-update) | async-done | bytes 786448 | tf_op jit(solution)/shard_map/reduce_scatter | solution.py:71
  423.7 44.6 %reduce-scatter.17.cloned.1.call-done = bf16[256,1536]{1,0:T(8,128)(2,1)} async-done(((bf16[1024,1536]{1,0:T(8,128)(2,1)}), bf16[256,1536]{1,0:T(8,128)(2,1)}) %reduce-scatter.17.cloned.1.call-update) | async-done | bytes 786448 | tf_op jit(solution)/shard_map/reduce_scatter | solution.py:56
  475.0 41.8 %all-gather.15.cloned.1.call-done = bf16[1024,1536]{1,0:T(8,128)(2,1)} async-done(((bf16[256,1536]{1,0:T(8,128)(2,1)}), bf16[1024,1536]{1,0:T(8,128)(2,1)}) %all-gather.15.cloned.1.call-update) | async-done | bytes 3145744 | tf_op jit(solution)/shard_map/all_gather | solution.py:48
  526.8 44.0 %reduce-scatter.21.cloned.1.call-done = bf16[256,1536]{1,0:T(8,128)(2,1)} async-done(((bf16[1024,1536]{1,0:T(8,128)(2,1)}), bf16[256,1536]{1,0:T(8,128)(2,1)}) %reduce-scatter.21.cloned.1.call-update) | async-done | bytes 786448 | tf_op jit(solution)/shard_map/reduce_scatter | solution.py:71
  583.4 6.9 copy.63
  590.4 9.1 convolution_convert_fusion
  600.0 9.7 convolution_convert_fusion.1
  624.2 11.0 multiply_reduce_fusion.1
  637.7 10.5 multiply_convert_fusion.1
  657.9 6.7 multiply_reduce_fusion
  667.1 11.7 multiply_convert_fusion
  685.0 6.4 fusion.5
  691.4 6.1 add_bitcast_fusion
  710.4 9.1 convolution_convert_fusion.9
  731.2 46.1 %all-reduce.15.cloned.1.call-done = bf16[1,64,1536]{2,1,0:T(8,128)(2,1)} async-done(((bf16[1,64,1536]{2,1,0:T(8,128)(2,1)}), bf16[1,64,1536]{2,1,0:T(8,128)(2,1)}) %all-reduce.15.cloned.1.call-update) | async-done | bytes 196624 | tf_op jit(solution)/shard_map/psum | solution.py:253
  779.1 44.9 %reduce-scatter.23.cloned.1.call-done = bf16[256,1536]{1,0:T(8,128)(2,1)} async-done(((bf16[1024,1536]{1,0:T(8,128)(2,1)}), bf16[256,1536]{1,0:T(8,128)(2,1)}) %reduce-scatter.23.cloned.1.call-update) | async-done | bytes 786448 | tf_op jit(solution)/shard_map/reduce_scatter | solution.py:71
  831.2 15.4 %all-reduce.9 = (bf16[768]{0:T(1024)(128)(2,1)S(1)}, bf16[768]{0:T(1024)(128)(2,1)S(1)}, bf16[768]{0:T(1024)(128)(2,1)S(1)}, bf16[768]{0:T(1024)(128)(2,1)S(1)},...) all-reduce(bf16[768]{0:T(1024)(128)(2,1)S(1)} %dynamic-slice.1, ...), channel_id=1, replica_groups=mesh['tensor'=4,'sub'=2,'group'=4] {'tensor'}, use_global_device_ids=true, to_apply=%region_32.33 | all-reduce | flops 4608 | bytes 18432 | tf_op jit(solution)/shard_map/psum | solution.py:254
  846.5 20.2 %all-reduce.7 = (bf16[768]{0:T(1024)(128)(2,1)S(1)}, bf16[768]{0:T(1024)(128)(2,1)S(1)}, bf16[768]{0:T(1024)(128)(2,1)S(1)}, bf16[768]{0:T(1024)(128)(2,1)S(1)},...) all-reduce(bf16[768]{0:T(1024)(128)(2,1)S(1)} %get-tuple-element.38, ...), channel_id=1, replica_groups=mesh['tensor'=4,'sub'=2,'group'=4] {'group'}, use_global_device_ids=true, to_apply=%region_34.35 | all-reduce | flops 4608 | bytes 18432 | tf_op jit(solution)/shard_map/psum | solution.py:318
  873.1 280.3 %all-reduce.19.cloned.1.call-done = (bf16[768,3,384]{2,0,1:T(8,128)(2,1)}, bf16[192,1536]{1,0:T(8,128)(2,1)}, bf16[768,384]{1,0:T(8,128)(2,1)}, bf16[768,2,384]{...) async-done(((bf16[768,3,384]{2,0,1:T(8,128)(2,1)}, bf16[192,1536]{1,0:T(8,128)(2,1)}, ...) | async-done | bytes 9437200 | tf_op jit(solution)/shard_map/psum | solution.py:320
  (338 shorter events, 190.2 us)
Async XLA Ops:
  7.2 192.8 %copy-start = (bf16[384,1536]{1,0:T(8,128)(2,1)S(1)}, bf16[384,1536]{1,0:T(8,128)(2,1)}, u32[]{:S(2)}) copy-start(bf16[384,1536]{1,0:T(8,128)(2,1)} %param.26) | copy-start | bytes 3538948
  7.2 52.1 %all-gather.7.cloned.1.call-start = ((), (), s32[]{:S(2)}) async-start(), calls=%async_computation.12 | async-start | bytes 3932160 | tf_op jit(solution)/shard_map/all_gather | solution.py:44
  12.6 131.1 %reduce-scatter.13.cloned.1.call-start = ((), (), s32[]{:S(2)}) async-start(), calls=%async_computation.13 | async-start | bytes 3932160 | tf_op jit(solution)/shard_map/reduce_scatter | solution.py:56
  99.6 47.7 %copy-start.57 = (f32[1536]{0:T(1024)S(1)}, f32[1536]{0:T(1024)}, u32[]{:S(2)}) copy-start(f32[1536]{0:T(1024)} %param.22) | copy-start | bytes 18436
  99.6 47.7 %copy-start.73 = (f32[1536]{0:T(1024)S(1)}, f32[1536]{0:T(1024)}, u32[]{:S(2)}) copy-start(f32[1536]{0:T(1024)} %param.23) | copy-start | bytes 18436
  99.6 93.0 %all-gather.9.cloned.1.call-start = ((), (), s32[]{:S(2)}) async-start(), calls=%async_computation.14 | async-start | bytes 3932160 | tf_op jit(solution)/shard_map/all_gather | solution.py:44
  148.6 98.9 %reduce-scatter.15.cloned.1.call-start = ((), (), s32[]{:S(2)}) async-start(), calls=%async_computation.15 | async-start | bytes 3932160 | tf_op jit(solution)/shard_map/reduce_scatter | solution.py:56
  203.5 46.1 %copy-start.56 = (f32[1536]{0:T(1024)S(1)}, f32[1536]{0:T(1024)}, u32[]{:S(2)}) copy-start(f32[1536]{0:T(1024)} %param.27) | copy-start | bytes 18436
  203.5 92.1 %all-gather.11.cloned.1.call-start = ((), (), s32[]{:S(2)}) async-start(), calls=%async_computation.16 | async-start | bytes 3932160 | tf_op jit(solution)/shard_map/all_gather | solution.py:44
  251.6 90.1 %all-gather.13.cloned.1.call-start = ((), (), s32[]{:S(2)}) async-start(), calls=%async_computation.18 | async-start | bytes 3932160 | tf_op jit(solution)/shard_map/all_gather | solution.py:48
  254.0 166.7 %reduce-scatter.19.cloned.1.call-start = ((), (), s32[]{:S(2)}) async-start(), calls=%async_computation.19 | async-start | bytes 3932160 | tf_op jit(solution)/shard_map/reduce_scatter | solution.py:71
  376.7 91.6 %reduce-scatter.17.cloned.1.call-start = ((), (), s32[]{:S(2)}) async-start(), calls=%async_computation.17 | async-start | bytes 3932160 | tf_op jit(solution)/shard_map/reduce_scatter | solution.py:56
  393.3 123.5 %all-gather.15.cloned.1.call-start = ((), (), s32[]{:S(2)}) async-start(), calls=%async_computation.20 | async-start | bytes 3932160 | tf_op jit(solution)/shard_map/all_gather | solution.py:48
  472.8 97.9 %reduce-scatter.21.cloned.1.call-start = ((), (), s32[]{:S(2)}) async-start(), calls=%async_computation.21 | async-start | bytes 3932160 | tf_op jit(solution)/shard_map/reduce_scatter | solution.py:71
  526.7 94.1 %all-gather.17.cloned.1.call-start = ((), (), s32[]{:S(2)}) async-start(), calls=%async_computation.22 | async-start | bytes 3932160 | tf_op jit(solution)/shard_map/all_gather | solution.py:48
  576.8 144.5 %all-reduce.17.cloned.1.call-start = ((), (), s32[]{:S(2)}) async-start(), calls=%async_computation.31 | async-start | bytes 4718592
  590.4 134.1 %reduce-scatter.35.cloned.1.call-start = ((), (), s32[]{:S(2)}) async-start(), calls=%async_computation.30 | async-start | bytes 7077888 | tf_op jit(solution)/shard_map/reduce_scatter | solution.py:313
  599.6 124.9 %reduce-scatter.33.cloned.1.call-start = ((), (), s32[]{:S(2)}) async-start(), calls=%async_computation.29 | async-start | bytes 7077888 | tf_op jit(solution)/shard_map/reduce_scatter | solution.py:310
  609.8 114.7 %reduce-scatter.31.cloned.1.call-start = ((), (), s32[]{:S(2)}) async-start(), calls=%async_computation.28 | async-start | bytes 1769472 | tf_op jit(solution)/shard_map/reduce_scatter | solution.py:301
  615.1 109.3 %reduce-scatter.29.cloned.1.call-start = ((), (), s32[]{:S(2)}) async-start(), calls=%async_computation.27 | async-start | bytes 1769472 | tf_op jit(solution)/shard_map/reduce_scatter | solution.py:295
  620.7 103.8 %reduce-scatter.27.cloned.1.call-start = ((), (), s32[]{:S(2)}) async-start(), calls=%async_computation.26 | async-start | bytes 1769472 | tf_op jit(solution)/shard_map/reduce_scatter | solution.py:286
  683.7 46.2 %reduce-scatter.25.cloned.1.call-start = ((), (), s32[]{:S(2)}) async-start(), calls=%async_computation.25 | async-start | bytes 5308416 | tf_op jit(solution)/shard_map/reduce_scatter | solution.py:283
  706.2 71.1 %all-reduce.15.cloned.1.call-start = ((), (), s32[]{:S(2)}) async-start(), calls=%async_computation.24 | async-start | bytes 393216 | tf_op jit(solution)/shard_map/psum | solution.py:253
  710.3 113.8 %reduce-scatter.23.cloned.1.call-start = ((), (), s32[]{:S(2)}) async-start(), calls=%async_computation.23 | async-start | bytes 3932160 | tf_op jit(solution)/shard_map/reduce_scatter | solution.py:71
  719.5 434.0 %all-reduce.19.cloned.1.call-start = ((), (), s32[]{:S(2)}) async-start(), calls=%async_computation.32 | async-start | bytes 18874368 | tf_op jit(solution)/shard_map/psum | solution.py:320
  729.9 49.1 %copy-start.16 = (bf16[256,1536]{1,0:T(8,128)(2,1)S(1)}, bf16[256,1536]{1,0:T(8,128)(2,1)}, u32[]{:S(2)}) copy-start(bf16[256,1536]{1,0:T(8,128)(2,1)} %reduce-scatter.21.cloned.1.call-done) | copy-start | bytes 2359300
  729.9 95.4 %copy-start.58 = (f32[1536]{0:T(1024)S(1)}, f32[1536]{0:T(1024)}, u32[]{:S(2)}) copy-start(f32[1536]{0:T(1024)} %param.18) | copy-start | bytes 18436
  729.9 95.4 %copy-start.66 = (f32[256]{0:T(256)S(1)}, f32[256]{0:T(256)}, u32[]{:S(2)}) copy-start(f32[256]{0:T(256)} %copy-done.65) | copy-start | bytes 3076
  729.9 95.4 %copy-start.71 = (f32[256]{0:T(256)S(1)}, f32[256]{0:T(256)}, u32[]{:S(2)}) copy-start(f32[256]{0:T(256)} %copy-done.70) | copy-start | bytes 3076
  731.1 96.1 %copy-start.68 = (bf16[1536]{0:T(1024)(128)(2,1)S(1)}, bf16[1536]{0:T(1024)(128)(2,1)}, u32[]{:S(2)}) copy-start(bf16[1536]{0:T(1024)(128)(2,1)} %get-tuple-element.16) | copy-start | bytes 9220
  731.1 96.2 %copy-start.69 = (bf16[1536]{0:T(1024)(128)(2,1)S(1)}, bf16[1536]{0:T(1024)(128)(2,1)}, u32[]{:S(2)}) copy-start(bf16[1536]{0:T(1024)(128)(2,1)} %get-tuple-element.18) | copy-start | bytes 9220
  779.1 91.1 %copy-start.18 = (f32[256,1536]{1,0:T(8,128)S(1)}, f32[256,1536]{1,0:T(8,128)}, u32[]{:S(2)}) copy-start(f32[256,1536]{1,0:T(8,128)} %get-tuple-element.51) | copy-start | bytes 4718596
  (76 other events, 533.1 us)
Sparse Core Ops, SparseCore 0:
  12.7 46.5 all-gather.6
  99.7 43.8 reduce-scatter.12
  148.8 43.8 all-gather.8
  203.6 43.8 reduce-scatter.14
  251.7 43.8 all-gather.10
  297.9 43.8 all-gather.12
  376.8 43.8 reduce-scatter.18
  424.3 43.8 reduce-scatter.16
  472.9 43.8 all-gather.14
  526.8 43.8 reduce-scatter.20
  576.9 43.8 all-gather.16
  623.0 21.7 all-reduce.16
  647.7 13.7 reduce-scatter.34
  664.1 13.8 reduce-scatter.32
  680.1 9.7 reduce-scatter.30
  692.6 9.8 reduce-scatter.28
  705.1 9.7 reduce-scatter.26
  717.1 12.8 reduce-scatter.24
  733.4 43.8 all-reduce.14
  780.1 43.8 reduce-scatter.22
  828.1 325.3 all-reduce.18
where the time goes:
time: 1190 us; the launch traced here: 1180 us
  waiting for transfers between devices  780 us (66%)
  matrix products  196 us (16%)
  other arithmetic  96 us (8%)
  local copies, waits for them, and re-layouts  46.8 us (4%)
  blocking collectives  39 us (3%)
  between operations  16.3 us (1%)
    psum x1, waiting for transfers between devices, local(): lax.psum(shards[2].astype(jnp.bfloat16), 'group').astype(jnp.float32)  280 us
    reduce_scatter x3, waiting for transfers between devices, project_rows(): lax.psum_scatter(partial_term(jnp.int32(0), left_side.shape[0] // lax.axi...  133 us
    all_gather x3, waiting for transfers between devices, gather_rows(): return lax.all_gather(values, 'tensor', axis=0, tiled=True)  121 us
    reduce_scatter x3, waiting for transfers between devices, project_back(): lax.psum_scatter(partial_term(jnp.int32(0), grad_left.shape[0] // lax.axi...  116 us
    all_gather x3, waiting for transfers between devices, gather_grads(): return lax.all_gather(values, 'tensor', axis=0, tiled=True)  77.9 us
    dot_general x7, matrix products, outer_cols(): lax.dot_general(left_side, right_side, (((1,), (1,)), ((), ())), preferre...  55.6 us
    psum x1, waiting for transfers between devices, local(): lax.psum(text_partial.astype(jnp.bfloat16), 'tensor').astype(jnp.float32)  46.1 us
    dot_general x7, matrix products, inner_rows(): lax.dot_general(left_side, right_side, (((0,), (0,)), ((), ())), preferre...  38.2 us
  transfers between devices with their start and end apart: 21, of which 14 were waited for; matrix products, arithmetic and copies ran while one was open for 16% of the time, Pallas kernels for 0%

commit v1 on v0

v1 whole, which is shorter than its diff:
```python
from functools import partial

import jax
import jax.numpy as jnp
from jax import lax
from jax.experimental import pallas as pl
from jax.experimental.pallas import tpu as pltpu
from jax.sharding import PartitionSpec as P

HEAD = 64
EPSILON = 1e-05
NEG_BIG = -1e30
LOG2E = 1.4426950408889634
MESH = pl.DeviceIdType.MESH
F32 = jnp.float32
BF = jnp.bfloat16
ANY = pl.BlockSpec(memory_space=pl.ANY)
VMEM_LIMIT = 63 << 20


def neighbours():
    t = lax.axis_index("tensor")
    return t, t + 1 - 2 * (t % 2), (t + 2) % 4, 3 - t


def greet(targets):
    barrier = pltpu.get_barrier_semaphore()
    for target in targets:
        pl.semaphore_signal(barrier, inc=1, device_id=target, device_id_type=MESH)
    pl.semaphore_wait(barrier, len(targets))


def dot(a, b):
    return lax.dot_general(a, b, (((1,), (0,)), ((), ())), preferred_element_type=F32)


def dot_t(a, b):
    return lax.dot_general(a, b, (((1,), (1,)), ((), ())), preferred_element_type=F32)


def dot_c(a, b):
    return lax.dot_general(a, b, (((0,), (0,)), ((), ())), preferred_element_type=F32)


def cols(j, width):
    return pl.ds(pl.multiple_of(j * width, width), width)


def rows_at(j, height):
    return pl.ds(pl.multiple_of(j * height, height), height)


def split(count):
    first = (count // 2 + 15) // 16 * 16
    return pl.ds(0, first), pl.ds(first, count - first)


class Gather:
    def __init__(self, own, dst, send, recv, base, halves=None):
        self.own, self.dst, self.send, self.recv, self.base = own, dst, send, recv, base
        self.halves = halves or split(own.shape[0])

    def copy(self, k):
        t, x, y, _ = neighbours()
        first, second = self.halves
        half = (first, second, second, first, first, second)[k]
        place = (t, t, t, t, x, y)[k]
        target = (x, y, x, y, y, x)[k]
        source = self.own.at[half] if k < 4 else self.dst.at[place, half]
        return pltpu.make_async_remote_copy(
            source,
            self.dst.at[place, half],
            self.send.at[self.base + k],
            self.recv.at[self.base + k],
            device_id={"tensor": target},
            device_id_type=MESH,
        )

    def start(self):
        for k in range(4):
            self.copy(k).start()

    def relay_x(self):
        self.copy(0).wait_recv()
        self.copy(4).start()

    def relay_y(self):
        self.copy(1).wait_recv()
        self.copy(5).start()

    def have_x(self):
        self.copy(2).wait_recv()

    def have_y(self):
        self.copy(3).wait_recv()

    def have_d(self):
        self.copy(4).wait_recv()
        self.copy(5).wait_recv()

    def drain(self):
        for k in range(6):
            self.copy(k).wait_send()


class Scatter:
    def __init__(self, part, land, stage, send, recv, base):
        self.part, self.land, self.stage = part, land, stage
        self.send, self.recv, self.base = send, recv, base
        self.half = part.shape[1] // 2

    def copy(self, k):
        t, x, y, d = neighbours()
        low, high = pl.ds(0, self.half), pl.ds(self.half, self.half)
        source = (
            self.part.at[d, low],
            self.part.at[d, high],
            self.part.at[x, low],
            self.stage.at[1],
            self.part.at[y, high],
            self.stage.at[0],
        )[k]
        target = (x, y, x, x, y, y)[k]
        return pltpu.make_async_remote_copy(
            source,
            self.land.at[k],
            self.send.at[self.base + k],
            self.recv.at[self.base + k],
            device_id={"tensor": target},
            device_id_type=MESH,
        )

    def diagonal(self):
        self.copy(0).start()
        self.copy(1).start()

    def along_x(self):
        self.copy(2).start()

    def along_y(self):
        self.copy(4).start()

    def relay(self):
        t, x, y, d = neighbours()
        low, high = pl.ds(0, self.half), pl.ds(self.half, self.half)
        self.copy(0).wait_recv()
        self.stage[0] = (self.part[y, low].astype(F32) + self.land[0].astype(F32)).astype(BF)
        self.copy(5).start()
        self.copy(1).wait_recv()
        self.stage[1] = (self.part[x, high].astype(F32) + self.land[1].astype(F32)).astype(BF)
        self.copy(3).start()

    def finish(self, take, step):
        t, x, y, d = neighbours()
        for k in (2, 4, 5, 3):
            self.copy(k).wait_recv()
        for base, a, b in ((0, 2, 5), (self.half, 4, 3)):

            def block(i, carry, base=base, a=a, b=b):
                here = rows_at(i, step)
                rows = pl.ds(pl.multiple_of(base + i * step, step), step)
                take(
                    rows,
                    self.part[t, rows].astype(F32)
                    + self.land[a, here].astype(F32)
                    + self.land[b, here].astype(F32),
                )
                return carry

            lax.fori_loop(0, self.half // step, block, 0)

    def drain(self):
        for k in range(6):
            self.copy(k).wait_send()


def normed_rows(values):
    centre = values - jnp.mean(values, -1, keepdims=True)
    inverse = lax.rsqrt(jnp.mean(centre * centre, -1, keepdims=True) + EPSILON)
    return centre * inverse, inverse


def params(cid, **more):
    return pltpu.CompilerParams(
        collective_id=cid, has_side_effects=True, vmem_limit_bytes=VMEM_LIMIT, **more
    )


def dma(count):
    return pltpu.SemaphoreType.DMA((count,))


def shape(*dims, kind=BF):
    return jax.ShapeDtypeStruct(dims, kind)


def enter_kernel(
    frames, gain, bias, qkv, text, kv, o_rows, o_triple, o_memory,
    v_frames, v_gain, v_bias, v_qkv, v_text, v_kv, rows, triple, memory, load, store, send, recv,
):
    t, x, y, d = neighbours()
    loads = [
        pltpu.make_async_copy(a, b, load.at[i])
        for i, (a, b) in enumerate(
            ((frames, v_frames), (gain, v_gain), (bias, v_bias), (qkv, v_qkv), (text, v_text), (kv, v_kv))
        )
    ]
    for copy in loads:
        copy.start()
    greet([{"tensor": x}, {"tensor": y}])
    for copy in loads[:3]:
        copy.wait()
    count, width = v_qkv.shape
    block = 384

    def norm_block(i, carry):
        here = rows_at(i, 64)
        hat, _ = normed_rows(v_frames[here].astype(F32))
        rows[t, here] = (hat * v_gain[...] + v_bias[...]).astype(BF)
        return carry

    lax.fori_loop(0, v_frames.shape[0] // 64, norm_block, 0)
    gather = Gather(rows.at[t], rows, send, recv, 0)
    gather.start()
    texts = Gather(memory.at[t], memory, send, recv, 6)

    def project(place):
        def step(j, carry):
            triple[place, :, cols(j, block)] = dot(rows[place], v_qkv[:, cols(j, block)]).astype(BF)
            return carry

        lax.fori_loop(0, width // block, step, 0)

    def put(k, place):
        a = pltpu.make_async_copy(rows.at[place], o_rows.at[place], store.at[2 * k])
        b = pltpu.make_async_copy(triple.at[place], o_triple.at[place], store.at[2 * k + 1])
        a.start()
        b.start()
        return [a, b]

    loads[4].wait()
    loads[5].wait()

    def texts_step(j, carry):
        memory[t, :, cols(j, block)] = dot(v_text[...], v_kv[:, cols(j, block)]).astype(BF)
        return carry

    lax.fori_loop(0, v_kv.shape[1] // block, texts_step, 0)
    texts.start()
    loads[3].wait()
    project(t)
    stores = put(0, t)
    gather.relay_x()
    gather.relay_y()
    gather.have_x()
    project(x)
    stores += put(1, x)
    gather.have_y()
    project(y)
    stores += put(2, y)
    texts.relay_x()
    texts.relay_y()
    texts.have_x()
    texts.have_y()
    gather.have_d()
    project(d)
    stores += put(3, d)
    texts.have_d()
    last = pltpu.make_async_copy(memory, o_memory, store.at[8])
    last.start()
    gather.drain()
    texts.drain()
    for copy in stores:
        copy.wait()
    last.wait()


def enter(frames, gain, bias, qkv, text, kv):
    n, m = frames.shape
    width, texts, kvw = qkv.shape[1], text.shape[0], kv.shape[1]
    return pl.pallas_call(
        enter_kernel,
        name="enter",
        out_shape=[shape(4, n, m), shape(4, n, width), shape(4, texts, kvw)],
        in_specs=[ANY] * 6,
        out_specs=[ANY] * 3,
        scratch_shapes=[
            pltpu.VMEM((n, m), frames.dtype), pltpu.VMEM((1, m), F32), pltpu.VMEM((1, m), F32),
            pltpu.VMEM(qkv.shape, BF), pltpu.VMEM(text.shape, BF), pltpu.VMEM(kv.shape, BF),
            pltpu.VMEM((4, n, m), BF), pltpu.VMEM((4, n, width), BF), pltpu.VMEM((4, texts, kvw), BF),
            dma(6), dma(9), dma(12), dma(12),
        ],
        compiler_params=params(1),
    )(frames, gain, bias, qkv, text, kv)


def head_lanes(rows):
    return lax.broadcasted_iota(jnp.int32, (rows, 128), 1)


def attend_rows(triple, place, blocks, heads, flat, sums):
    n = triple.shape[1]
    width = heads * HEAD
    scale = HEAD ** (-0.5) * LOG2E
    lanes = head_lanes(n)

    def pair(p, stats):
        here = pl.ds(pl.multiple_of(p * 128, 128), 128)
        key_cols = pl.ds(pl.multiple_of(width + p * 128, 128), 128)
        value_cols = pl.ds(pl.multiple_of(2 * width + p * 128, 128), 128)
        query = triple[place, :, here]
        keys = triple[0:blocks, :, key_cols].reshape(blocks * n, 128)
        values = triple[0:blocks, :, value_cols].reshape(blocks * n, 128)
        outs = []
        for h in range(2):
            mine = (lanes < HEAD) if h == 0 else (lanes >= HEAD)
            scores = dot_t(jnp.where(mine, query, jnp.zeros_like(query)), keys)
            row = lax.broadcasted_iota(jnp.int32, scores.shape, 0)
            col = lax.broadcasted_iota(jnp.int32, scores.shape, 1)
            scores = jnp.where(col <= row + (blocks - 1) * n, scores, NEG_BIG)
            peak = jnp.max(scores, -1, keepdims=True) * scale
            exponent = jnp.exp2(scores * scale - peak)
            total = jnp.sum(exponent, -1, keepdims=True)
            outs.append(dot(exponent.astype(BF), values) / total)
            stats = jnp.where(lanes == 2 * p + h, peak + jnp.log2(total), stats)
        flat[place, :, here] = jnp.where(lanes < HEAD, outs[0], outs[1]).astype(BF)
        return stats

    sums[place] = lax.fori_loop(0, heads // 2, pair, jnp.zeros((n, 128), F32))


def attend_kernel(
    triple_in, out_in, frames_in, wq, wo, o_flat, o_sums, o_after, o_wq, o_wo,
    triple, v_out, v_frames, flat, sums, after, part, land, stage, v_wq, v_wo, load, store, send, recv, side,
):
    t, x, y, d = neighbours()
    s = lax.axis_index("sub")
    subs = lax.axis_size("sub")
    n = triple.shape[1]
    m = v_out.shape[1]
    heads = v_out.shape[0] // HEAD
    loads = [
        pltpu.make_async_copy(a, b, load.at[i])
        for i, (a, b) in enumerate(
            ((triple_in, triple), (out_in, v_out), (frames_in, v_frames), (wq, v_wq), (wo, v_wo))
        )
    ]
    for copy in loads:
        copy.start()
    greet(
        [{"tensor": x}, {"tensor": y}]
        + [{"sub": (s + k) % subs} for k in range(1, subs)]
    )
    scatter = Scatter(part, land, stage, send, recv, 0)
    gathers = []
    for i, (weight, full) in enumerate(((wq, o_wq), (wo, o_wo))):
        piece = weight.shape[0] // subs
        first, second = split(piece)
        offset = pl.multiple_of(s * piece, piece)
        halves = (
            pl.ds(offset, first.size),
            pl.ds(pl.multiple_of(offset + first.size, 16), second.size),
        )
        gathers.append((Gather(weight, full, send, recv, 6 + 6 * i, halves), full, pl.ds(offset, piece)))

    def shared(i, j, k):
        _, full, piece = gathers[i]
        place = (x, y, d)[j]
        slot = (i * 3 + j) * (subs - 1) + k - 1
        return pltpu.make_async_remote_copy(
            full.at[place, piece], full.at[place, piece],
            send.at[18 + slot], recv.at[18 + slot],
            device_id={"sub": (s + k) % subs}, device_id_type=MESH,
        )

    for gather, _, _ in gathers:
        gather.start()
    for copy in loads[:2]:
        copy.wait()

    def one(i, carry):
        far_y = 1 - i // 2
        far_x = 1 - i % 2
        place = (t // 2 + far_y - 2 * (t // 2) * far_y) * 2 + (t % 2 + far_x - 2 * (t % 2) * far_x)
        for blocks in range(1, 5):

            @pl.when(place == blocks - 1)
            def _(blocks=blocks):
                attend_rows(triple, blocks - 1, blocks, heads, flat, sums)

        def out_step(j, carry):
            part[place, :, cols(j, 512)] = dot(flat[place], v_out[:, cols(j, 512)]).astype(BF)
            return carry

        lax.fori_loop(0, m // 512, out_step, 0)

        @pl.when(i == 0)
        def _():
            scatter.diagonal()

        @pl.when(i == 1)
        def _():
            scatter.along_y()

        @pl.when(i == 2)
        def _():
            scatter.along_x()

        return carry

    lax.fori_loop(0, 4, one, 0)
    for gather, _, _ in gathers:
        gather.relay_x()
        gather.relay_y()
    stores = [
        pltpu.make_async_copy(flat, o_flat, store.at[0]),
        pltpu.make_async_copy(sums, o_sums, store.at[1]),
    ]
    loads[3].wait()
    loads[4].wait()
    stores += [
        pltpu.make_async_copy(v_wq, o_wq.at[t], store.at[2]),
        pltpu.make_async_copy(v_wo, o_wo.at[t], store.at[3]),
    ]
    for copy in stores:
        copy.start()
    scatter.relay()
    for i, (gather, _, _) in enumerate(gathers):
        gather.have_x()
        gather.have_y()
        gather.have_d()
        for j in range(3):
            for k in range(1, subs):
                shared(i, j, k).start()
    loads[2].wait()

    def take(rows, total):
        after[rows] = v_frames[rows].astype(F32) + total

    scatter.finish(take, 64)
    last = pltpu.make_async_copy(after, o_after, store.at[4])
    last.start()
    scatter.drain()
    for i, (gather, _, _) in enumerate(gathers):
        gather.drain()
        for j in range(3):
            for k in range(1, subs):
                shared(i, j, k).wait()
    for copy in stores:
        copy.wait()
    last.wait()


def attend(triple, out, frames, wq, wo, subs):
    _, n, width = triple.shape
    local, m = out.shape
    extra = 18 + 6 * (subs - 1)
    return pl.pallas_call(
        attend_kernel,
        name="attend",
        out_shape=[
            shape(4, n, local), shape(4, n, 128, kind=F32), shape(n, m, kind=F32),
            shape(4, *wq.shape), shape(4, *wo.shape),
        ],
        in_specs=[ANY] * 5,
        out_specs=[ANY] * 5,
        scratch_shapes=[
            pltpu.VMEM((4, n, width), BF), pltpu.VMEM((local, m), BF), pltpu.VMEM((n, m), frames.dtype),
            pltpu.VMEM((4, n, local), BF), pltpu.VMEM((4, n, 128), F32), pltpu.VMEM((n, m), F32),
            pltpu.VMEM((4, n, m), BF), pltpu.VMEM((6, n // 2, m), BF), pltpu.VMEM((2, n // 2, m), BF),
            pltpu.VMEM(wq.shape, BF), pltpu.VMEM(wo.shape, BF),
            dma(5), dma(5), dma(extra), dma(extra), dma(1),
        ],
        compiler_params=params(2),
    )(triple, out, frames, wq, wo)


def stack_pair(block, rows):
    lanes = head_lanes(rows)
    zero = jnp.zeros_like(block)
    return jnp.concatenate([jnp.where(lanes < HEAD, block, zero), jnp.where(lanes >= HEAD, block, zero)], 0)


def pair_softmax(query, keys):
    scale = HEAD ** (-0.5) * LOG2E
    scores = dot_t(query, keys)
    left = head_lanes(scores.shape[0]) < HEAD
    low = jnp.max(jnp.where(left, scores, -jnp.inf), -1, keepdims=True)
    high = jnp.max(jnp.where(left, -jnp.inf, scores), -1, keepdims=True)
    exponent = jnp.exp2((scores - jnp.where(left, low, high)) * scale)
    total = pair_sum(exponent, left)
    return exponent / total, left


def pair_sum(values, left):
    low = jnp.sum(jnp.where(left, values, 0.0), -1, keepdims=True)
    high = jnp.sum(jnp.where(left, 0.0, values), -1, keepdims=True)
    return jnp.where(left, low, high)


def cross_kernel(
    after_in, gains_in, wq_in, wo_in, memory_in, cot_in,
    o_query, o_flat, o_after, o_rows, o_grads,
    after, gains, wq, wo, memory, cot, rows, query, flat, result, feed, grads, load, store, send, recv,
):
    t, x, y, d = neighbours()
    loads = [
        pltpu.make_async_copy(a, b, load.at[i])
        for i, (a, b) in enumerate(
            ((cot_in, cot), (after_in, after), (gains_in, gains), (wq_in, wq), (memory_in, memory), (wo_in, wo))
        )
    ]
    for copy in loads:
        copy.start()
    greet([{"tensor": x}, {"tensor": y}])
    n, m = after.shape
    width = wq.shape[2]
    texts = memory.shape[1]
    loads[0].wait()

    def round_block(i, carry):
        here = rows_at(i, 64)
        grads[t, here] = cot[here].astype(BF)
        return carry

    lax.fori_loop(0, n // 64, round_block, 0)
    gather = Gather(grads.at[t], grads, send, recv, 0)
    gather.start()
    loads[1].wait()
    loads[2].wait()

    def norm_block(i, carry):
        here = rows_at(i, 64)
        hat, _ = normed_rows(after[here])
        rows[here] = (hat * gains[0:1] + gains[1:2]).astype(BF)
        return carry

    lax.fori_loop(0, n // 64, norm_block, 0)
    loads[3].wait()
    loads[4].wait()

    def quarter(q, carry):
        query[:, cols(q, width)] = dot(rows[...], wq[q]).astype(BF)

        def pair(p, carry):
            keys = stack_pair(memory[q, :, cols(p, 128)], texts)
            values = stack_pair(memory[q, :, pl.ds(pl.multiple_of(width + p * 128, 128), 128)], texts)
            here = pl.ds(pl.multiple_of(q * width + p * 128, 128), 128)
            probs, _ = pair_softmax(query[:, here], keys)
            flat[:, here] = dot(probs.astype(BF), values).astype(BF)
            return carry

        lax.fori_loop(0, width // 128, pair, 0)
        return carry

    lax.fori_loop(0, 4, quarter, 0)
    gather.relay_x()
    gather.relay_y()
    stores = [pltpu.make_async_copy(query, o_query, store.at[0]), pltpu.make_async_copy(flat, o_flat, store.at[1])]
    loads[5].wait()

    def out_step(j, carry):
        result[:, cols(j, 512)] = after[:, cols(j, 512)] + dot(flat[...], wo[:, cols(j, 512)])
        return carry

    lax.fori_loop(0, m // 512, out_step, 0)

    def feed_block(i, carry):
        here = rows_at(i, 64)
        hat, _ = normed_rows(result[here])
        feed[here] = (hat * gains[2:3] + gains[3:4]).astype(BF)
        return carry

    lax.fori_loop(0, n // 64, feed_block, 0)
    stores += [pltpu.make_async_copy(result, o_after, store.at[2]), pltpu.make_async_copy(feed, o_rows, store.at[3])]
    for copy in stores:
        copy.start()
    gather.have_x()
    gather.have_y()
    gather.have_d()
    last = pltpu.make_async_copy(grads, o_grads, store.at[4])
    last.start()
    gather.drain()
    for copy in stores:
        copy.wait()
    last.wait()


def cross(after, gains, wq, wo, memory, cot):
    n, m = after.shape
    return pl.pallas_call(
        cross_kernel,
        name="cross",
        out_shape=[shape(n, m), shape(n, m), shape(n, m, kind=F32), shape(n, m), shape(4, n, m)],
        in_specs=[ANY] * 6,
        out_specs=[ANY] * 5,
        scratch_shapes=[
            pltpu.VMEM((n, m), F32), pltpu.VMEM(gains.shape, F32), pltpu.VMEM(wq.shape, BF), pltpu.VMEM(wo.shape, BF),
            pltpu.VMEM(memory.shape, BF), pltpu.VMEM((n, m), F32), pltpu.VMEM((n, m), BF), pltpu.VMEM((n, m), BF),
            pltpu.VMEM((n, m), BF), pltpu.VMEM((n, m), F32), pltpu.VMEM((n, m), BF), pltpu.VMEM((4, n, m), BF),
            dma(6), dma(5), dma(6), dma(6),
        ],
        compiler_params=params(3),
    )(after, gains, wq, wo, memory, cot)


def gelu_both(pre):
    size = jnp.abs(pre) * 0.7071067811865476
    rate = 1.0 / (1.0 + 0.3275911 * size)
    bell = jnp.exp2(pre * pre * (-0.5 * LOG2E))
    series = rate * (
        0.254829592
        + rate * (-0.284496736 + rate * (1.421413741 + rate * (-1.453152027 + rate * 1.061405429)))
    )
    tail = 0.5 * series * bell
    gate = jnp.where(pre >= 0, 1.0 - tail, tail)
    return pre * gate, gate + pre * (0.3989422804014327 * bell)


class Halves:
    def __init__(self, whole, land, send, recv, base):
        self.whole, self.land, self.send, self.recv, self.base = whole, land, send, recv, base
        self.subs = lax.axis_size("sub")
        self.piece = whole.shape[1] // self.subs

    def copies(self, w):
        s = lax.axis_index("sub")
        made = []
        for k in range(1, self.subs):
            target = (s + k) % self.subs
            slot = w * (self.subs - 1) + k - 1
            made.append(
                pltpu.make_async_remote_copy(
                    self.whole.at[w, rows_at(target, self.piece)],
                    self.land.at[w, k - 1],
                    self.send.at[self.base + slot],
                    self.recv.at[self.base + slot],
                    device_id={"sub": target},
                    device_id_type=MESH,
                )
            )
        return made

    def start(self, w):
        for copy in self.copies(w):
            copy.start()

    def total(self, w, take, step):
        s = lax.axis_index("sub")
        for copy in self.copies(w):
            copy.wait_recv()

        def block(i, carry):
            here = rows_at(i, step)
            value = self.whole[w, pl.ds(pl.multiple_of(s * self.piece + i * step, step), step)].astype(F32)
            for k in range(1, self.subs):
                value = value + self.land[w, k - 1, here].astype(F32)
            take(here, value)
            return carry

        lax.fori_loop(0, self.piece // step, block, 0)

    def drain(self, w):
        for copy in self.copies(w):
            copy.wait_send()


def weight_grad(left, right, whole, w, halves, block):
    s = lax.axis_index("sub")
    subs = lax.axis_size("sub")
    total_rows = left.shape[0] * left.shape[1]
    count = whole.shape[1] // block
    begin = ((s + 1) % subs) * halves.piece // block

    def one(j, carry):
        b = (begin + j) % count
        turned = left[:, :, cols(b, block)].reshape(total_rows, block)

        def inner(i, carry):
            other = right[:, :, cols(i, 512)].reshape(total_rows, 512)
            whole[w, rows_at(b, block), cols(i, 512)] = dot_c(turned, other).astype(BF)
            return carry

        lax.fori_loop(0, whole.shape[2] // 512, inner, 0)
        return carry

    if subs == 2:
        lax.fori_loop(0, count // 2, one, 0)
        halves.start(w)
        lax.fori_loop(count // 2, count, one, 0)
    else:
        lax.fori_loop(0, count, one, 0)
        halves.start(w)


def feed_kernel(
    rows_in, grads_in, up_in, down_in, after_in, o_layer, o_norm, o_pieces,
    rows, grads, up, down, result, act, pre_grad, part_out, part_norm, land_out, land_norm, stage_out, stage_norm,
    whole, land_whole, load, store, send, recv,
):
    t, x, y, d = neighbours()
    s = lax.axis_index("sub")
    subs = lax.axis_size("sub")
    loads = [
        pltpu.make_async_copy(a, b, load.at[i])
        for i, (a, b) in enumerate(
            ((rows_in, rows.at[t]), (up_in, up), (grads_in, grads), (down_in, down), (after_in, result))
        )
    ]
    for copy in loads:
        copy.start()
    greet([{"tensor": x}, {"tensor": y}] + [{"sub": (s + k) % subs} for k in range(1, subs)])
    n, m = result.shape
    hidden = up.shape[1]
    loads[0].wait()
    gather = Gather(rows.at[t], rows, send, recv, 0)
    gather.start()
    back = Scatter(part_norm, land_norm, stage_norm, send, recv, 6)
    fore = Scatter(part_out, land_out, stage_out, send, recv, 12)
    halves = Halves(whole, land_whole, send, recv, 18)
    for copy in loads[1:4]:
        copy.wait()

    def work(place):
        def step(j, carry):
            here = cols(j, 256)
            value, slope = gelu_both(dot(rows[place], up[:, here]))
            act[place, :, here] = value.astype(BF)
            pre_grad[place, :, here] = (dot_t(grads[place], down[here]) * slope).astype(BF)
            return carry

        lax.fori_loop(0, hidden // 256, step, 0)

        def out_step(j, carry):
            part_norm[place, :, cols(j, 512)] = dot_t(pre_grad[place], up[rows_at(j, 512)]).astype(BF)
            part_out[place, :, cols(j, 512)] = dot(act[place], down[:, cols(j, 512)]).astype(BF)
            return carry

        lax.fori_loop(0, m // 512, out_step, 0)

    def turn(i, carry):
        far_y = i // 2
        far_x = i % 2
        place = (t // 2 + far_y - 2 * (t // 2) * far_y) * 2 + (t % 2 + far_x - 2 * (t % 2) * far_x)

        @pl.when(i == 1)
        def _():
            gather.relay_x()
            gather.relay_y()
            gather.have_x()

        @pl.when(i == 2)
        def _():
            gather.have_y()

        @pl.when(i == 3)
        def _():
            gather.have_d()

        work(place)

        @pl.when(i == 1)
        def _():
            back.along_x()

        @pl.when(i == 2)
        def _():
            back.along_y()

        @pl.when(i == 3)
        def _():
            back.diagonal()

        return carry

    lax.fori_loop(0, 4, turn, 0)
    fore.diagonal()
    fore.along_x()
    fore.along_y()
    weight_grad(act, grads, whole, 0, halves, 256)
    back.relay()
    weight_grad(rows, pre_grad, whole, 1, halves, 256)
    fore.relay()
    loads[4].wait()
    pieces = land_whole
    for w in range(2):

        def take(here, value, w=w):
            pieces[w, 0, here] = value.astype(BF)

        halves.total(w, take, 64)
    stores = [pltpu.make_async_copy(pieces.at[:, 0], o_pieces, store.at[0])]
    stores[0].start()

    def take_out(here, total):
        result[here] = result[here] + total

    norm_total = part_norm

    fore.finish(take_out, 64)
    stores.append(pltpu.make_async_copy(result, o_layer, store.at[1]))
    stores[1].start()

    def take_norm(here, total):
        norm_total[t, here] = total.astype(BF)

    back.finish(take_norm, 64)
    stores.append(pltpu.make_async_copy(norm_total.at[t], o_norm, store.at[2]))
    stores[2].start()
    gather.drain()
    back.drain()
    fore.drain()
    for w in range(2):
        halves.drain(w)
    for copy in stores:
        copy.wait()


def feed(rows, grads, up, down, after, subs):
    n, m = rows.shape
    hidden = up.shape[1]
    count = 18 + 2 * (subs - 1)
    return pl.pallas_call(
        feed_kernel,
        name="feed",
        out_shape=[shape(n, m, kind=F32), shape(n, m), shape(2, m // subs, hidden)],
        in_specs=[ANY] * 5,
        out_specs=[ANY] * 3,
        scratch_shapes=[
            pltpu.VMEM((4, n, m), BF), pltpu.VMEM((4, n, m), BF), pltpu.VMEM((m, hidden), BF), pltpu.VMEM((hidden, m), BF),
            pltpu.VMEM((n, m), F32), pltpu.VMEM((4, n, hidden), BF), pltpu.VMEM((4, n, hidden), BF),
            pltpu.VMEM((4, n, m), BF), pltpu.VMEM((4, n, m), BF),
            pltpu.VMEM((6, n // 2, m), BF), pltpu.VMEM((6, n // 2, m), BF),
            pltpu.VMEM((2, n // 2, m), BF), pltpu.VMEM((2, n // 2, m), BF),
            pltpu.VMEM((2, m, hidden), BF), pltpu.VMEM((2, subs - 1, m // subs, hidden), BF),
            dma(5), dma(3), dma(count), dma(count),
        ],
        compiler_params=params(4),
    )(rows, grads, up, down, after)


def norm_back_block(grad, source, gain):
    hat, inverse = normed_rows(source)
    scaled = grad * gain
    inner = scaled - jnp.mean(scaled, -1, keepdims=True) - hat * jnp.mean(scaled * hat, -1, keepdims=True)
    return inverse * inner, grad * hat


def fold(block):
    total = block[0:8]
    for i in range(1, block.shape[0] // 8):
        total = total + block[8 * i : 8 * i + 8]
    return total


def unstack(block):
    lanes = head_lanes(block.shape[0] // 2)
    return jnp.where(lanes < HEAD, block[: block.shape[0] // 2], block[block.shape[0] // 2 :])


def cross_back_kernel(
    cot_in, norm_in, cross_in, self_in, gains_in, query_in, flat_in, memory_in, wq_in, wo_in,
    o_out, o_branch, o_sums, o_memory, o_wq, o_wo,
    cot, norm, after_cross, after_self, gains, query, flat, memory, wq, wo,
    branch, rows, query_grad, memory_grad, sums, whole_q, whole_o, land_q, land_o, piece_q, piece_o,
    load, store, send, recv,
):
    s = lax.axis_index("sub")
    subs = lax.axis_size("sub")
    loads = [
        pltpu.make_async_copy(a, b, load.at[i])
        for i, (a, b) in enumerate(
            (
                (cot_in, cot), (norm_in, norm), (cross_in, after_cross), (gains_in, gains), (wo_in, wo),
                (query_in, query), (flat_in, flat), (memory_in, memory), (self_in, after_self), (wq_in, wq),
            )
        )
    ]
    for copy in loads:
        copy.start()
    greet([{"sub": (s + k) % subs} for k in range(1, subs)])
    n, m = cot.shape
    width = wq.shape[2]
    texts = memory.shape[1]
    for copy in loads[:4]:
        copy.wait()
    scale = HEAD ** (-0.5)

    def feed_block(i, carry):
        here = rows_at(i, 64)
        grad = norm[here].astype(F32)
        inner, terms = norm_back_block(grad, after_cross[here], gains[2:3])
        total = cot[here] + inner
        cot[here] = total
        branch[here] = total.astype(BF)
        return carry[0] + fold(terms), carry[1] + fold(grad)

    zero = jnp.zeros((8, m), F32)
    gain_sum, bias_sum = lax.fori_loop(0, n // 64, feed_block, (zero, zero))
    sums[0:8] = gain_sum
    sums[8:16] = bias_sum
    loads[8].wait()

    def norm_block(i, carry):
        here = rows_at(i, 64)
        hat, _ = normed_rows(after_self[here])
        rows[here] = (hat * gains[0:1] + gains[1:2]).astype(BF)
        return carry

    lax.fori_loop(0, n // 64, norm_block, 0)
    for copy in loads[4:8]:
        copy.wait()

    def quarter(q, carry):
        grad_heads = dot_t(branch[...], wo[rows_at(q, width)]).astype(BF)
        whole_q_cols = cols(q, width)
        query_grad_block = []
        for p in range(width // 128):
            lane = slice(p * 128, p * 128 + 128)
            keys = stack_pair(memory[q, :, lane], texts)
            values = stack_pair(memory[q, :, width + p * 128 : width + p * 128 + 128], texts)
            here = pl.ds(pl.multiple_of(q * width + p * 128, 128), 128)
            grad = grad_heads[:, lane]
            ask = query[:, here]
            probs, left = pair_softmax(ask, keys)
            grad_probs = dot_t(grad, values)
            centred = pair_sum(grad_probs * probs, left)
            grad_scores = (probs * (grad_probs - centred)).astype(BF)
            query_grad[:, here] = (dot(grad_scores, keys) * scale).astype(BF)
            memory_grad[q, :, lane] = unstack(dot_c(grad_scores, ask) * scale).astype(BF)
            memory_grad[q, :, width + p * 128 : width + p * 128 + 128] = unstack(
                dot_c(probs.astype(BF), grad)
            ).astype(BF)
        return carry

    lax.fori_loop(0, 4, quarter, 0)
    stores = [pltpu.make_async_copy(memory_grad, o_memory, store.at[0])]
    stores[0].start()
    halves_q = Halves(whole_q, land_q, send, recv, 0)
    halves_o = Halves(whole_o, land_o, send, recv, 4 * (subs - 1))

    def weights(q, carry):
        def grad_o(j, carry):
            whole_o[q, :, cols(j, 512)] = dot_c(flat[:, cols(q, width)], branch[:, cols(j, 512)]).astype(BF)
            return carry

        lax.fori_loop(0, m // 512, grad_o, 0)

        def grad_q(j, carry):
            whole_q[q, rows_at(j, 256)] = dot_c(rows[:, cols(j, 256)], query_grad[:, cols(q, width)]).astype(BF)
            return carry

        lax.fori_loop(0, m // 256, grad_q, 0)
        return carry

    lax.fori_loop(0, 4, weights, 0)
    for q in range(4):
        halves_q.start(q)
        halves_o.start(q)
    loads[9].wait()

    def norm_grad(j, carry):
        here = rows_at(j, 256)
        total = jnp.zeros((n, 256), F32)
        for q in range(4):
            total = total + dot_t(query_grad[:, q * width : (q + 1) * width], wq[q, here])
        after_cross[:, cols(j, 256)] = total
        return carry

    lax.fori_loop(0, m // 256, norm_grad, 0)

    def self_block(i, carry):
        here = rows_at(i, 64)
        grad = after_cross[here]
        inner, terms = norm_back_block(grad, after_self[here], gains[0:1])
        total = cot[here] + inner
        cot[here] = total
        branch[here] = total.astype(BF)
        return carry[0] + fold(terms), carry[1] + fold(grad)

    gain_sum, bias_sum = lax.fori_loop(0, n // 64, self_block, (zero, zero))
    sums[16:24] = gain_sum
    sums[24:32] = bias_sum
    stores += [
        pltpu.make_async_copy(cot, o_out, store.at[1]),
        pltpu.make_async_copy(branch, o_branch, store.at[2]),
        pltpu.make_async_copy(sums, o_sums, store.at[3]),
    ]
    for copy in stores[1:]:
        copy.start()
    for halves, piece in ((halves_q, piece_q), (halves_o, piece_o)):
        for q in range(4):

            def take(here, value, q=q, piece=piece):
                piece[q, here] = value.astype(BF)

            halves.total(q, take, 16)
    stores += [pltpu.make_async_copy(piece_q, o_wq, store.at[4]), pltpu.make_async_copy(piece_o, o_wo, store.at[5])]
    for copy in stores[4:]:
        copy.start()
    for q in range(4):
        halves_q.drain(q)
        halves_o.drain(q)
    for copy in stores:
        copy.wait()


def cross_back(cot, norm, after_cross, after_self, gains, query, flat, memory, wq, wo, subs):
    n, m = cot.shape
    width = wq.shape[2]
    count = 8 * (subs - 1)
    part_q, part_o = (4, m // subs, width), (4, width // subs, m)
    return pl.pallas_call(
        cross_back_kernel,
        name="cross_back",
        out_shape=[
            shape(n, m, kind=F32), shape(n, m), shape(32, m, kind=F32), shape(*memory.shape), shape(*part_q), shape(*part_o),
        ],
        in_specs=[ANY] * 10,
        out_specs=[ANY] * 6,
        scratch_shapes=[
            pltpu.VMEM((n, m), F32), pltpu.VMEM((n, m), BF), pltpu.VMEM((n, m), F32), pltpu.VMEM((n, m), F32),
            pltpu.VMEM(gains.shape, F32), pltpu.VMEM((n, m), BF), pltpu.VMEM((n, m), BF), pltpu.VMEM(memory.shape, BF),
            pltpu.VMEM(wq.shape, BF), pltpu.VMEM(wo.shape, BF),
            pltpu.VMEM((n, m), BF), pltpu.VMEM((n, m), BF), pltpu.VMEM((n, m), BF), pltpu.VMEM(memory.shape, BF),
            pltpu.VMEM((32, m), F32), pltpu.VMEM((4, m, width), BF), pltpu.VMEM((4, width, m), BF),
            pltpu.VMEM((4, subs - 1, m // subs, width), BF), pltpu.VMEM((4, subs - 1, width // subs, m), BF),
            pltpu.VMEM(part_q, BF), pltpu.VMEM(part_o, BF),
            dma(10), dma(6), dma(count), dma(count),
        ],
        compiler_params=params(5),
    )(cot, norm, after_cross, after_self, gains, query, flat, memory, wq, wo)


def attend_rows_back(triple, place, blocks, heads, grad_heads, deltas, sums, grads, grad_keys, grad_values):
    n = triple.shape[1]
    width = heads * HEAD
    scale = HEAD ** (-0.5)
    lanes = head_lanes(n)
    key_lanes = head_lanes(blocks * n)

    def pair(p, carry):
        here = pl.ds(pl.multiple_of(p * 128, 128), 128)
        key_cols = pl.ds(pl.multiple_of(width + p * 128, 128), 128)
        value_cols = pl.ds(pl.multiple_of(2 * width + p * 128, 128), 128)
        query = triple[place, :, here]
        grad = grad_heads[place, :, here]
        keys = triple[0:blocks, :, key_cols].reshape(blocks * n, 128)
        values = triple[0:blocks, :, value_cols].reshape(blocks * n, 128)
        stats = sums[place]
        means = deltas[place]
        found = []
        for h in range(2):
            mine = (lanes < HEAD) if h == 0 else (lanes >= HEAD)
            log_sum = jnp.sum(jnp.where(lanes == 2 * p + h, stats, 0.0), -1, keepdims=True)
            delta = jnp.sum(jnp.where(lanes == 2 * p + h, means, 0.0), -1, keepdims=True)
            scores = dot_t(jnp.where(mine, query, jnp.zeros_like(query)), keys)
            row = lax.broadcasted_iota(jnp.int32, scores.shape, 0)
            col = lax.broadcasted_iota(jnp.int32, scores.shape, 1)
            probs = jnp.where(
                col <= row + (blocks - 1) * n, jnp.exp2(scores * (scale * LOG2E) - log_sum), 0.0
            )
            grad_probs = dot_t(jnp.where(mine, grad, jnp.zeros_like(grad)), values)
            grad_scores = (probs * (grad_probs - delta)).astype(BF)
            found.append((dot(grad_scores, keys), dot_c(grad_scores, query), dot_c(probs.astype(BF), grad)))
        grads[place, :, here] = (jnp.where(lanes < HEAD, found[0][0], found[1][0]) * scale).astype(BF)
        grad_keys[0 : blocks * n, here] += jnp.where(key_lanes < HEAD, found[0][1], found[1][1]) * scale
        grad_values[0 : blocks * n, here] += jnp.where(key_lanes < HEAD, found[0][2], found[1][2])
        return carry

    lax.fori_loop(0, heads // 2, pair, 0)


def attend_back_kernel(
    branch_in, triple_in, flat_in, sums_in, out_in, qkv_in, rows_in, frames_in, gains_in, grad_in, memory_in, text_in, kv_in,
    cross_q_in, cross_o_in,
    o_frames, o_sums, o_text, o_qkv, o_out, o_kv, o_cq, o_co,
    branch, triple, flat, sums, out, qkv, rows, frames, gains, grad_out, memory, text, kv,
    cross_q, cross_o, land_q, land_o, land_m, stage_q, stage_o, stage_m,
    grad_heads, deltas, grads, grad_keys, grad_values, part, land, stage, whole_qkv, land_qkv, whole_out, land_out,
    whole_kv, land_kv, text_grad, sums_out, sum_m,
    load, store, send, recv,
):
    t, x, y, d = neighbours()
    s = lax.axis_index("sub")
    subs = lax.axis_size("sub")
    names = (
        (branch_in, branch.at[t]), (out_in, out), (flat_in, flat), (triple_in, triple), (sums_in, sums),
        (memory_in, memory), (cross_q_in, cross_q), (cross_o_in, cross_o), (qkv_in, qkv), (rows_in, rows),
        (text_in, text), (kv_in, kv), (frames_in, frames), (gains_in, gains), (grad_in, grad_out),
    )
    loads = [pltpu.make_async_copy(a, b, load.at[i]) for i, (a, b) in enumerate(names)]
    for copy in loads:
        copy.start()
    greet([{"tensor": x}, {"tensor": y}] + [{"sub": (s + k) % subs} for k in range(1, subs)])
    n, m = grad_out.shape
    width = triple.shape[2]
    local = out.shape[0]
    heads = local // HEAD
    gather = Gather(branch.at[t], branch, send, recv, 0)
    scatter = Scatter(part, land, stage, send, recv, 6)
    scatter_m = Scatter(memory, land_m, stage_m, send, recv, 12)
    scatter_q = Scatter(cross_q, land_q, stage_q, send, recv, 18)
    scatter_o = Scatter(cross_o, land_o, stage_o, send, recv, 24)
    halves_qkv = Halves(whole_qkv, land_qkv, send, recv, 30)
    halves_out = Halves(whole_out, land_out, send, recv, 30 + subs - 1)
    halves_kv = Halves(whole_kv, land_kv, send, recv, 30 + 2 * (subs - 1))
    loads[0].wait()
    gather.start()
    for copy in loads[5:8]:
        copy.wait()
    for each in (scatter_m, scatter_q, scatter_o):
        each.diagonal()
        each.along_x()
        each.along_y()
    for copy in loads[1:5]:
        copy.wait()
    grad_keys[...] = jnp.zeros_like(grad_keys)
    grad_values[...] = jnp.zeros_like(grad_values)
    lanes = head_lanes(n)

    def turn(i, carry):
        far_y = i // 2
        far_x = i % 2
        place = (t // 2 + far_y - 2 * (t // 2) * far_y) * 2 + (t % 2 + far_x - 2 * (t % 2) * far_x)

        @pl.when(i == 1)
        def _():
            gather.relay_x()
            gather.relay_y()
            gather.have_x()

        @pl.when(i == 2)
        def _():
            gather.have_y()

        @pl.when(i == 3)
        def _():
            gather.have_d()

        grad_heads[place] = dot_t(branch[place], out[...]).astype(BF)

        def delta(p, stats):
            here = pl.ds(pl.multiple_of(p * 128, 128), 128)
            product = grad_heads[place, :, here].astype(F32) * flat[place, :, here].astype(F32)
            low = jnp.sum(jnp.where(lanes < HEAD, product, 0.0), -1, keepdims=True)
            high = jnp.sum(jnp.where(lanes < HEAD, 0.0, product), -1, keepdims=True)
            return jnp.where(lanes == 2 * p, low, jnp.where(lanes == 2 * p + 1, high, stats))

        deltas[place] = lax.fori_loop(0, heads // 2, delta, jnp.zeros((n, 128), F32))
        for blocks in range(1, 5):

            @pl.when(place == blocks - 1)
            def _(blocks=blocks):
                attend_rows_back(
                    triple, blocks - 1, blocks, heads, grad_heads, deltas, sums, grads, grad_keys, grad_values
                )

        return carry

    lax.fori_loop(0, 4, turn, 0)
    for copy in loads[8:12]:
        copy.wait()

    def finish_grads(i, carry):
        grads[i, :, local : 2 * local] = grad_keys[rows_at(i, n)].astype(BF)
        grads[i, :, 2 * local :] = grad_values[rows_at(i, n)].astype(BF)
        return carry

    lax.fori_loop(0, 4, finish_grads, 0)

    def back(i, carry):
        far_y = 1 - i // 2
        far_x = 1 - i % 2
        place = (t // 2 + far_y - 2 * (t // 2) * far_y) * 2 + (t % 2 + far_x - 2 * (t % 2) * far_x)

        def step(j, carry):
            part[place, :, cols(j, 512)] = dot_t(grads[place], qkv[rows_at(j, 512)]).astype(BF)
            return carry

        lax.fori_loop(0, m // 512, step, 0)

        @pl.when(i == 0)
        def _():
            scatter.diagonal()

        @pl.when(i == 1)
        def _():
            scatter.along_y()

        @pl.when(i == 2)
        def _():
            scatter.along_x()

        return carry

    lax.fori_loop(0, 4, back, 0)
    for each in (scatter_m, scatter_q, scatter_o):
        each.relay()

    def take_m(here, total):
        sum_m[here] = total.astype(BF)

    scatter_m.finish(take_m, 16)
    text_grad[...] = dot_t(sum_m[...], kv[...])
    stores = [pltpu.make_async_copy(text_grad, o_text, store.at[0])]
    stores[0].start()

    def grad_kv(j, carry):
        whole_kv[0, rows_at(j, 384)] = dot_c(text[:, cols(j, 384)], sum_m[...]).astype(BF)
        return carry

    lax.fori_loop(0, m // 384, grad_kv, 0)
    halves_kv.start(0)

    def grad_wout(j, carry):
        whole_out[0, :, cols(j, 512)] = dot_c(
            flat[...].reshape(4 * n, local), branch[:, :, cols(j, 512)].reshape(4 * n, 512)
        ).astype(BF)
        return carry

    lax.fori_loop(0, m // 512, grad_wout, 0)
    halves_out.start(0)
    scatter.relay()

    def grad_wqkv(j, carry):
        turned = rows[:, :, cols(j, 256)].reshape(4 * n, 256)

        def inner(i, carry):
            whole_qkv[0, rows_at(j, 256), cols(i, 384)] = dot_c(
                turned, grads[:, :, cols(i, 384)].reshape(4 * n, 384)
            ).astype(BF)
            return carry

        lax.fori_loop(0, width // 384, inner, 0)
        return carry

    lax.fori_loop(0, m // 256, grad_wqkv, 0)
    halves_qkv.start(0)
    for each, landed, output, slot in ((scatter_q, land_q, o_cq, 1), (scatter_o, land_o, o_co, 2)):
        half = each.half

        def take(here, total, each=each):
            each.part[t, here] = total.astype(BF)

        each.finish(take, 16)
        stores.append(pltpu.make_async_copy(each.part.at[t], output, store.at[slot]))
        stores[-1].start()
    for each, output, slot in ((halves_kv, o_kv, 3), (halves_out, o_out, 4), (halves_qkv, o_qkv, 5)):

        def take(here, total, each=each):
            each.land[0, 0, here] = total.astype(BF)

        each.total(0, take, 16)
        stores.append(pltpu.make_async_copy(each.land.at[0, 0], output, store.at[slot]))
        stores[-1].start()
    for copy in loads[12:]:
        copy.wait()

    def take_norm(here, total):
        part[t, here] = total.astype(BF)

    scatter.finish(take_norm, 64)

    def frame_block(i, carry):
        here = rows_at(i, 64)
        grad = part[t, here].astype(F32)
        inner, terms = norm_back_block(grad, frames[here].astype(F32), gains[0:1])
        grad_out[here] = grad_out[here] + inner
        return carry[0] + fold(terms), carry[1] + fold(grad)

    zero = jnp.zeros((8, m), F32)
    gain_sum, bias_sum = lax.fori_loop(0, n // 64, frame_block, (zero, zero))
    sums_out[0:8] = gain_sum
    sums_out[8:16] = bias_sum
    stores += [pltpu.make_async_copy(grad_out, o_frames, store.at[6]), pltpu.make_async_copy(sums_out, o_sums, store.at[7])]
    for copy in stores[-2:]:
        copy.start()
    gather.drain()
    for each in (scatter, scatter_m, scatter_q, scatter_o):
        each.drain()
    for each in (halves_qkv, halves_out, halves_kv):
        each.drain(0)
    for copy in stores:
        copy.wait()


def attend_back(branch, triple, flat, sums, out, qkv, rows, frames, gains, grad, memory, text, kv, cross_q, cross_o, subs):
    n, m = grad.shape
    width = triple.shape[2]
    local = out.shape[0]
    texts, kvw = text.shape[0], kv.shape[1]
    count = 30 + 3 * (subs - 1)
    piece_q, piece_o = cross_q.shape[1:], cross_o.shape[1:]
    v = pltpu.VMEM
    return pl.pallas_call(
        attend_back_kernel,
        name="attend_back",
        out_shape=[
            shape(n, m, kind=F32), shape(16, m, kind=F32), shape(texts, m, kind=F32), shape(m // subs, width),
            shape(local // subs, m), shape(m // subs, kvw), shape(*piece_q), shape(*piece_o),
        ],
        in_specs=[ANY] * 15,
        out_specs=[ANY] * 8,
        scratch_shapes=[
            v((4, n, m), BF), v(triple.shape, BF), v(flat.shape, BF), v(sums.shape, F32), v(out.shape, BF), v(qkv.shape, BF),
            v(rows.shape, BF), v(frames.shape, frames.dtype), v(gains.shape, F32), v((n, m), F32), v(memory.shape, BF),
            v(text.shape, BF), v(kv.shape, BF),
            v(cross_q.shape, BF), v(cross_o.shape, BF),
            v((6, piece_q[0] // 2, piece_q[1]), BF), v((6, piece_o[0] // 2, piece_o[1]), BF), v((6, texts // 2, kvw), BF),
            v((2, piece_q[0] // 2, piece_q[1]), BF), v((2, piece_o[0] // 2, piece_o[1]), BF), v((2, texts // 2, kvw), BF),
            v((4, n, local), BF), v((4, n, 128), F32), v((4, n, width), BF), v((4 * n, local), F32), v((4 * n, local), F32),
            v((4, n, m), BF), v((6, n // 2, m), BF), v((2, n // 2, m), BF),
            v((1, m, width), BF), v((1, subs - 1, m // subs, width), BF),
            v((1, local, m), BF), v((1, subs - 1, local // subs, m), BF),
            v((1, m, kvw), BF), v((1, subs - 1, m // subs, kvw), BF),
            v((texts, m), F32), v((16, m), F32), v((texts, kvw), BF),
            dma(15), dma(8), dma(count), dma(count),
        ],
        compiler_params=params(6),
    )(branch, triple, flat, sums, out, qkv, rows, frames, gains, grad, memory, text, kv, cross_q, cross_o)


def total_kernel(
    feed_in, qkv_in, cq_in, kv_in, out_in, co_in, sums_a_in, sums_b_in, text_in,
    o_up, o_down, o_qkv, o_cq, o_kv, o_out, o_co, o_text, o_vectors,
    own, from_left, from_right, to_right, to_left, result, sums_a, sums_b, text, text_land, text_full, vectors, vectors_land, share,
    share_land, load, store, send_right, recv_right, send_left, recv_left, send, recv,
):
    t, x, y, d = neighbours()
    s, subs = lax.axis_index("sub"), lax.axis_size("sub")
    g, groups = lax.axis_index("group"), lax.axis_size("group")
    chunk = result.shape[1]
    m = own.shape[1]
    width, cq_width, kv_width = qkv_in.shape[1], cq_in.shape[1], kv_in.shape[1]
    piece, kv_rows, out_rows = feed_in.shape[1], kv_in.shape[0] // 2, out_in.shape[0]
    start_qkv = 2 * piece
    start_kv = start_qkv + qkv_in.shape[0]
    start_out = start_kv + kv_rows
    start_co = start_out + out_rows
    count = own.shape[0] // chunk
    loads = [
        pltpu.make_async_copy(a, b, load.at[i])
        for i, (a, b) in enumerate(
            (
                (feed_in.at[0], own.at[pl.ds(0, piece)]),
                (feed_in.at[1], own.at[pl.ds(piece, piece)]),
                (qkv_in, own.at[pl.ds(start_qkv, piece), pl.ds(0, width)]),
                (cq_in, own.at[pl.ds(start_qkv, piece), pl.ds(width, cq_width)]),
                (kv_in.at[pl.ds(0, kv_rows)], own.at[pl.ds(start_kv, kv_rows), pl.ds(0, kv_width)]),
                (kv_in.at[pl.ds(kv_rows, kv_rows)], own.at[pl.ds(start_kv, kv_rows), pl.ds(kv_width, kv_width)]),
                (out_in, own.at[pl.ds(start_out, out_rows)]),
                (co_in, own.at[pl.ds(start_co, out_rows)]),
                (sums_a_in, sums_a),
                (sums_b_in, sums_b),
                (text_in, text),
            )
        )
    ]
    for copy in loads:
        copy.start()
    greet(
        [{"tensor": x}, {"tensor": y}, {"tensor": d}]
        + [{"sub": (s + k) % subs} for k in range(1, subs)]
        + [{"group": (g + k) % groups} for k in range(1, groups)]
    )
    for copy in loads:
        copy.wait()
    share_width = m // subs
    for i in range(6):
        source, at = (sums_a, i) if i < 4 else (sums_b, i - 4)
        row = jnp.sum(source[8 * at : 8 * at + 8], 0, keepdims=True)
        for j in range(subs):
            vectors[j, i : i + 1] = row[:, j * share_width : (j + 1) * share_width]
    strip = text.shape[0] // 4

    def remote(source, target, k, device):
        return pltpu.make_async_remote_copy(
            source, target, send.at[k], recv.at[k], device_id=device, device_id_type=MESH
        )

    square = (x, y, d)
    first = [remote(vectors, vectors_land.at[k], k, {"tensor": square[k]}) for k in range(3)]
    first += [
        remote(text.at[rows_at(square[k], strip)], text_land.at[k], 3 + k, {"tensor": square[k]}) for k in range(3)
    ]
    second = [
        remote(share.at[0, (s + k) % subs], share_land.at[k - 1], 5 + k, {"sub": (s + k) % subs}) for k in range(1, subs)
    ]
    base = 5 + subs
    second += [
        remote(text_full.at[rows_at(t, strip)], text_full.at[rows_at(t, strip)], base + k, {"tensor": square[k]}) for k in range(3)
    ]
    base += 3
    third = [
        remote(share.at[1, 0], share_land.at[subs - 2 + k], base + k - 1, {"group": (g + k) % groups})
        for k in range(1, groups)
    ]
    for copy in first:
        copy.start()

    def right(c):
        return pltpu.make_async_remote_copy(
            to_right.at[c % 4], from_left.at[c], send_right.at[c % 4], recv_right.at[c],
            device_id={"group": (g + 1) % groups}, device_id_type=MESH,
        )

    def left(c):
        return pltpu.make_async_remote_copy(
            to_left.at[c % 4], from_right.at[c], send_left.at[c % 4], recv_left.at[c],
            device_id={"group": (g + groups - 1) % groups}, device_id_type=MESH,
        )

    def outputs(c, act):
        row = c * chunk
        slot = c % 4
        block = result.at[slot]

        def region(begin, end, copies):
            @pl.when(jnp.logical_and(row >= begin, row < end))
            def _():
                for i, (source, target) in enumerate(copies(pl.multiple_of(row - begin, chunk))):
                    act(pltpu.make_async_copy(source, target, store.at[2 * slot + i]))

        def whole(output):
            return lambda at: [(block, output.at[pl.ds(at, chunk)])]

        region(0, piece, whole(o_down))
        region(piece, start_qkv, whole(o_up))
        region(
            start_qkv, start_kv,
            lambda at: [
                (block.at[:, pl.ds(0, width)], o_qkv.at[pl.ds(at, chunk)]),
                (block.at[:, pl.ds(width, cq_width)], o_cq.at[pl.ds(at, chunk)]),
            ],
        )
        region(
            start_kv, start_out,
            lambda at: [
                (block.at[:, pl.ds(0, kv_width)], o_kv.at[pl.ds(at, chunk)]),
                (
                    block.at[:, pl.ds(kv_width, kv_width)],
                    o_kv.at[pl.ds(pl.multiple_of(kv_rows + at, chunk), chunk)],
                ),
            ],
        )
        region(start_out, start_co, whole(o_out))
        region(start_co, start_co + out_rows, whole(o_co))

    lag = 2
    far = jnp.maximum(g, groups - 1 - g)

    def step(k, carry):
        c = k - lag * g

        @pl.when(jnp.logical_and(c >= 0, c < count))
        def _():
            @pl.when(g > 0)
            def _():
                right(c).wait_recv()

            @pl.when(g < groups - 1)
            def _():
                @pl.when(c >= 4)
                def _():
                    right(c - 4).wait_send()

                mine = own[rows_at(c, chunk)]

                @pl.when(g > 0)
                def _():
                    to_right[c % 4] = (mine.astype(F32) + from_left[c].astype(F32)).astype(BF)

                @pl.when(g == 0)
                def _():
                    to_right[c % 4] = mine

                right(c).start()

        e = k - lag * (groups - 1 - g)

        @pl.when(jnp.logical_and(e >= 0, e < count))
        def _():
            @pl.when(g < groups - 1)
            def _():
                left(e).wait_recv()

            @pl.when(g > 0)
            def _():
                @pl.when(e >= 4)
                def _():
                    left(e - 4).wait_send()

                mine = own[rows_at(e, chunk)]

                @pl.when(g < groups - 1)
                def _():
                    to_left[e % 4] = (mine.astype(F32) + from_right[e].astype(F32)).astype(BF)

                @pl.when(g == groups - 1)
                def _():
                    to_left[e % 4] = mine

                left(e).start()

        f = k - lag * far

        @pl.when(jnp.logical_and(f >= 0, f < count))
        def _():
            @pl.when(f >= 4)
            def _():
                outputs(f - 4, lambda copy: copy.wait())

            mine = own[rows_at(f, chunk)].astype(F32)

            @pl.when(jnp.logical_and(g > 0, g < groups - 1))
            def _():
                result[f % 4] = mine + from_left[f].astype(F32) + from_right[f].astype(F32)

            @pl.when(g == 0)
            def _():
                result[f % 4] = mine + from_right[f].astype(F32)

            @pl.when(g == groups - 1)
            def _():
                result[f % 4] = mine + from_left[f].astype(F32)

            outputs(f, lambda copy: copy.start())

        return carry

    steps = count + lag * (groups - 1)
    lax.fori_loop(0, 3, step, 0)
    for copy in first:
        copy.wait_recv()
    for j in range(subs):
        share[0, j] = vectors[j] + vectors_land[0, j] + vectors_land[1, j] + vectors_land[2, j]
    text_full[rows_at(t, strip)] = text[rows_at(t, strip)] + text_land[0] + text_land[1] + text_land[2]
    for copy in first:
        copy.wait_send()
    for copy in second:
        copy.start()
    lax.fori_loop(3, 6, step, 0)
    for copy in second:
        copy.wait_recv()
    total = share[0, s]
    for k in range(1, subs):
        total = total + share_land[k - 1]
    share[1, 0] = total
    text_store = pltpu.make_async_copy(text_full, o_text, store.at[8])
    text_store.start()
    for copy in third:
        copy.start()
    lax.fori_loop(6, steps, step, 0)
    for copy in third:
        copy.wait_recv()
    total = share[1, 0]
    for k in range(1, groups):
        total = total + share_land[subs - 2 + k]
    share[2, 0] = total
    vector_store = pltpu.make_async_copy(share.at[2, 0], o_vectors, store.at[9])
    vector_store.start()
    for copy in second + third:
        copy.wait_send()

    @pl.when(g < groups - 1)
    def _():
        for i in range(4):
            right(count - 4 + i).wait_send()

    @pl.when(g > 0)
    def _():
        for i in range(4):
            left(count - 4 + i).wait_send()

    for i in range(4):
        outputs(count - 4 + i, lambda copy: copy.wait())
    text_store.wait()
    vector_store.wait()


def total(pieces, qkv, cq, kv, out, co, sums_a, sums_b, text, subs, groups):
    _, piece, m = pieces.shape
    rows = 2 * piece + qkv.shape[0] + kv.shape[0] // 2 + out.shape[0] + co.shape[0]
    chunk = 96 if out.shape[0] % 96 == 0 else 48
    count = rows // chunk
    v = pltpu.VMEM
    sems = 8 + subs + groups
    return pl.pallas_call(
        total_kernel,
        name="total",
        out_shape=[shape(*dims, kind=F32) for dims in (
            (piece, m), (piece, m), qkv.shape, cq.shape, kv.shape, out.shape, co.shape, text.shape, (8, m // subs),
        )],
        in_specs=[ANY] * 9,
        out_specs=[ANY] * 9,
        scratch_shapes=[
            v((rows, m), BF), v((count, chunk, m), BF), v((count, chunk, m), BF), v((4, chunk, m), BF), v((4, chunk, m), BF),
            v((4, chunk, m), F32), v(sums_a.shape, F32), v(sums_b.shape, F32), v(text.shape, F32),
            v((3, text.shape[0] // 4, m), F32), v(text.shape, F32), v((subs, 8, m // subs), F32), v((3, subs, 8, m // subs), F32),
            v((3, subs, 8, m // subs), F32), v((subs - 1 + groups - 1, 8, m // subs), F32),
            dma(11), dma(10), dma(4), dma(count), dma(4), dma(count), dma(sems), dma(sems),
        ],
        compiler_params=params(7),
    )(pieces, qkv, cq, kv, out, co, sums_a, sums_b, text)


def local(
    frames, text_states, selfgain, selfbias, selfqkv, selfout, crossgain, crossbias, crossquery, crosskv, crossout,
    feedgain, feedbias, feedup, feeddown, cotangent,
):
    subs, groups = lax.axis_size("sub"), lax.axis_size("group")
    m = frames.shape[2]
    width = selfout.shape[0]
    qkv = selfqkv.reshape(m, 3 * width)
    kv = crosskv.reshape(m, 2 * width)
    self_gains = jnp.stack([selfgain, selfbias])
    gains = jnp.stack([crossgain, crossbias, feedgain, feedbias])
    rows, triple, memory = enter(frames[0], self_gains[0:1], self_gains[1:2], qkv, text_states[0], kv)
    flat, sums, after_self, wq, wo = attend(triple, selfout, frames[0], crossquery, crossout, subs)
    wo = wo.reshape(4 * width, m)
    query, cross_flat, after_cross, feed_rows, grads = cross(after_self, gains, wq, wo, memory, cotangent[0])
    layer_output, norm_grad, pieces = feed(feed_rows, grads, feedup, feeddown, after_cross, subs)
    grad_out, branch, sums_a, memory_grad, piece_q, piece_o = cross_back(
        cotangent[0], norm_grad, after_cross, after_self, gains, query, cross_flat, memory, wq, wo, subs
    )
    frame_grad, sums_b, text_part, grad_qkv, grad_out_weight, grad_kv, grad_cq, grad_co = attend_back(
        branch, triple, flat, sums, selfout, qkv, rows, frames[0], self_gains, grad_out, memory_grad, text_states[0], kv,
        piece_q, piece_o, subs,
    )
    up, down, full_qkv, full_cq, full_kv, full_out, full_co, text_grad, vectors = total(
        pieces, grad_qkv, grad_cq, grad_kv, grad_out_weight, grad_co, sums_a, sums_b, text_part, subs, groups
    )
    return (
        layer_output[None],
        frame_grad[None],
        text_grad[None],
        vectors[4],
        vectors[5],
        full_qkv.reshape(-1, 3, width),
        full_out,
        vectors[2],
        vectors[3],
        full_cq,
        full_kv.reshape(-1, 2, width),
        full_co,
        vectors[0],
        vectors[1],
        up,
        down,
    )


def solution(mesh):
    clips = P(("sub", "group"), "tensor", None)
    whole = P(("sub", "group"), None, None)
    narrow, wide = P("tensor", None), P(None, "tensor")
    third = P(None, None, "tensor")
    vector = P("sub")
    return jax.shard_map(
        local,
        mesh=mesh,
        in_specs=(
            clips, whole, P(), P(), third, narrow, P(), P(), wide, third, narrow, P(), P(), wide, narrow, clips,
        ),
        out_specs=(
            clips, clips, whole, vector, vector, P("sub", None, "tensor"), P(("tensor", "sub"), None), vector, vector,
            P("sub", "tensor"), P("sub", None, "tensor"), P(("tensor", "sub"), None), vector, vector,
            P("sub", "tensor"), P(("tensor", "sub"), None),
        ),
        check_vma=False,
    )
```

time: 1190 us -> 641 us (0.54); the launches traced: 1180 us -> 640 us
  waiting for transfers between devices: 780 us -> 0 us
  Pallas kernels: 0 us -> 595 us
  matrix products: 196 us -> 0 us
  other arithmetic: 96 us -> 1.25 us
  blocking collectives: 39 us -> 0 us
  between operations: 16.3 us -> 0.74 us
    pallas_call x0 -> x7, Pallas kernels: none -> 595 us  [the longest x1 232 us: total(): pl.pallas_call(total_kernel, name='total', out_shape=[shape(*dims, kind=F...]
    psum x2 -> x0, waiting for transfers between devices: 326 us -> none  [the longest x1 280 us: local(): lax.psum(shards[2].astype(jnp.bfloat16), 'group').astype(jnp.float32)]
    reduce_scatter x12 -> x0, waiting for transfers between devices: 254 us -> none  [the longest x3 133 us: project_rows(): lax.psum_scatter(partial_term(jnp.int32(0), left_side.shape[0] // lax.axi...]
    all_gather x6 -> x0, waiting for transfers between devices: 199 us -> none  [the longest x3 121 us: gather_rows(): return lax.all_gather(values, 'tensor', axis=0, tiled=True)]
    dot_general x45 -> x0, matrix products: 196 us -> none  [the longest x7 55.6 us: outer_cols(): lax.dot_general(left_side, right_side, (((1,), (1,)), ((), ())), preferre...]
    convert_element_type x25 -> x0, other arithmetic: 64 us -> none  [the longest x4 22.6 us: attend_backward(): grad_scores = (probs * (grad_probs - centred)).astype(jnp.bfloat16)]
    psum x2 -> x0, blocking collectives: 35.5 us -> none  [the longest x1 20.2 us: local(): lax.psum(shards[0].astype(jnp.bfloat16), 'group').astype(jnp.float32)]
    reduce_sum x16 -> x0, other arithmetic: 22.3 us -> none  [the longest x6 8.4 us: norm_back(): return (grad_in, jnp.sum(grad_out * normed, 0), jnp.sum(grad_out, 0))]
  transfers between devices with their start and end apart: 21 -> 0, of which waited for: 14 -> 0; matrix products, arithmetic and copies ran while one was open for 16% -> 0% of each run, Pallas kernels for 0% -> 0%
where the time goes in v1:
time: 641 us; the launch traced here: 640 us
  Pallas kernels  595 us (93%)
  local copies, waits for them, and re-layouts  42.9 us (7%)
    pallas_call x1, Pallas kernels, total(): pl.pallas_call(total_kernel, name='total', out_shape=[shape(*dims, kind=F...  232 us
    pallas_call x1, Pallas kernels, attend_back(): pl.pallas_call(attend_back_kernel, name='attend_back', out_shape=[shape(n...  109 us
    pallas_call x1, Pallas kernels, feed(): pl.pallas_call(feed_kernel, name='feed', out_shape=[shape(n, m, kind=F32)...  87.2 us
    pallas_call x1, Pallas kernels, attend(): pl.pallas_call(attend_kernel, name='attend', out_shape=[shape(4, n, local...  68.3 us
    pallas_call x1, Pallas kernels, enter(): pl.pallas_call(enter_kernel, name='enter', out_shape=[shape(4, n, m), sha...  36.8 us
    pallas_call x1, Pallas kernels, cross_back(): pl.pallas_call(cross_back_kernel, name='cross_back', out_shape=[shape(n,...  32.6 us
    pallas_call x1, Pallas kernels, cross(): pl.pallas_call(cross_kernel, name='cross', out_shape=[shape(n, m), shape(...  29.2 us
    unnamed x29, local copies, waits for them, and re-layouts  26.3 us

profile of v1, /device:TPU:0, one launch (start us, length us, event | category | flops | bytes accessed | tf_op | source)
XLA Modules:
  0.0 640.2 jit_solution(2650819424948701595)
XLA Ops:
  0.6 0.7 stack.24.gain
  1.4 0.7 stack.25.bias
  2.1 0.7 stack.26
  2.8 0.7 stack.27
  3.5 0.7 stack.28
  4.2 0.7 stack.29
  4.9 0.6 pad_maximum_fusion.gains_in
  5.5 0.6 pad_maximum_fusion.1.gains_in
  6.1 3.5 copy.39
  9.7 4.3 copy.34
  13.9 3.7 copy.35.qkv.qkv_in
  17.6 36.8 %enter.1 = (bf16[4,256,1536]{2,1,0:T(8,128)(2,1)}, bf16[4,256,1152]{2,1,0:T(8,128)(2,1)}, bf16[4,64,768]{2,1,0:T(8,128)(2,1)}) custom-call(bf16[256,1536]{1,0:T(8,128)(2,1)} %bitcast.17, f32[1,1536]{1,0:T(1,128)} %copy-done.5, f32[1,1536]{1,0:T(1,128)} %copy-done.6, bf16[1536,1152]{1,0:T(8,128)(2,1)} %copy.35.qkv.qkv_in, bf16[64,1536]{1,0:T(8,128)(2,1)} %bitcast.27, ...), custom_call_target="tpu_custom_call" | custom-call | tf_op jit(solution)/shard_map/enter/pallas_call | solution.py:281
  54.4 68.3 %attend.1 = (bf16[4,256,384]{2,1,0:T(8,128)(2,1)}, f32[4,256,128]{2,1,0:T(8,128)}, f32[256,1536]{1,0:T(8,128)}, bf16[4,1536,384]{2,1,0:T(8,128)(2,1)}, bf16[4,384,1536]{2,1,0:T(8,128)(2,1)}) custom-call(bf16[4,256,1152]{2,1,0:T(8,128)(2,1)} %get-tuple-element.55.triple_in, bf16[384,1536]{1,0:T(8,128)(2,1)} %out_in.3, bf16[256,1536]{1,0:T(8,128)(2,1)} %bitcast.18, ...), custom_call_target="tpu_custom_call" | custom-call | tf_op jit(solution)/shard_map/attend/pallas_call | solution.py:458
  122.7 29.2 %cross.1 = (bf16[256,1536]{1,0:T(8,128)(2,1)}, bf16[256,1536]{1,0:T(8,128)(2,1)}, f32[256,1536]{1,0:T(8,128)}, bf16[256,1536]{1,0:T(8,128)(2,1)}, bf16[4,256,1536]{2,1,0:T(8,128)(2,1)}) custom-call(f32[256,1536]{1,0:T(8,128)} %get-tuple-element.56.after_in.self_in, f32[4,1536]{1,0:T(4,128)} %pad_maximum_fusion.gains_in, ...), custom_call_target="tpu_custom_call" | custom-call | tf_op jit(solution)/shard_map/cross/pallas_call | solution.py:591
  152.0 87.2 %feed.1 = (f32[256,1536]{1,0:T(8,128)}, bf16[256,1536]{1,0:T(8,128)(2,1)}, bf16[2,768,1536]{2,1,0:T(8,128)(2,1)}) custom-call(bf16[256,1536]{1,0:T(8,128)(2,1)} %get-tuple-element.60.rows_in, bf16[4,256,1536]{2,1,0:T(8,128)(2,1)} %get-tuple-element.61.grads_in, bf16[1536,1536]{1,0:T(8,128)(2,1)} %up_in.1, bf16[1536,1536]{1,0:T(8,128)(2,1)} %down_in.1, ...), custom_call_target="tpu_custom_call" | custom-call | tf_op jit(solution)/shard_map/feed/pallas_call | solution.py:823
  239.3 32.6 %cross_back.1 = (f32[256,1536]{1,0:T(8,128)}, bf16[256,1536]{1,0:T(8,128)(2,1)}, f32[32,1536]{1,0:T(8,128)}, bf16[4,64,768]{2,1,0:T(8,128)(2,1)}, bf16[4,768,384...) custom-call(f32[256,1536]{1,0:T(8,128)} %bitcast.21, bf16[256,1536]{1,0:T(8,128)(2,1)} %get-tuple-element.64.norm_in, ...), custom_call_target="tpu_custom_call" | custom-call | tf_op jit(solution)/shard_map/cross_back/pallas_call | solution.py:1013
  271.9 108.9 %attend_back.1 = (f32[256,1536]{1,0:T(8,128)}, f32[16,1536]{1,0:T(8,128)}, f32[64,1536]{1,0:T(8,128)}, bf16[768,1152]{1,0:T(8,128)(2,1)}, bf16[192,1536]{1,0:T(8...) custom-call(bf16[256,1536]{1,0:T(8,128)(2,1)} %get-tuple-element.67.branch_in, ...), custom_call_target="tpu_custom_call" | custom-call | tf_op jit(solution)/shard_map/attend_back/pallas_call | solution.py:1296
  380.8 232.2 %total.1 = (f32[768,1536]{1,0:T(8,128)}, f32[768,1536]{1,0:T(8,128)}, f32[768,1152]{1,0:T(8,128)}, f32[768,384]{1,0:T(8,128)}, f32[768,768]{1,0:T(8,128)}, /*ind...) custom-call(bf16[2,768,1536]{2,1,0:T(8,128)(2,1)} %get-tuple-element.76.feed_in, ...), custom_call_target="tpu_custom_call" | custom-call | tf_op jit(solution)/shard_map/total/pallas_call | solution.py:1589
  613.0 1.6 slice_reduce_fusion
  614.6 3.9 reshape.51
  618.5 3.3 copy.37
  621.8 2.9 copy.38
  624.7 2.8 copy.48
  627.5 1.1 copy.49
  628.7 0.1 copy-done.4
  628.7 0.7 copy.50
  629.5 0.0 copy-done.3
  629.5 1.0 copy.51
  630.5 1.0 copy.52
  631.5 1.0 copy.53
  632.5 5.5 copy.54
  638.1 2.2 copy.55
  (17 shorter events, 0.0 us)
Async XLA Ops:
  1.3 8.3 %copy-start.5 = (f32[1,1536]{1,0:T(1,128)}, f32[1,1536]{1,0:T(1,128)S(1)}, u32[]{:S(2)}) copy-start(f32[1,1536]{1,0:T(1,128)S(1)} %stack.24.gain) | copy-start | bytes 18436
  2.1 7.6 %copy-start.6 = (f32[1,1536]{1,0:T(1,128)}, f32[1,1536]{1,0:T(1,128)S(1)}, u32[]{:S(2)}) copy-start(f32[1,1536]{1,0:T(1,128)S(1)} %stack.25.bias) | copy-start | bytes 18436
  624.7 2.8 copy-start
  627.5 1.2 copy-start.4
  627.5 2.0 copy-start.3
  628.7 1.8 copy-start.2
  629.5 2.0 copy-start.1
  631.5 6.5 %slice-start = ((s8[4718592]{0:T(1024)(128)(4,1)}), s8[4194304]{0:T(1024)(128)(4,1)S(1)}, s32[]{:S(2)}) async-start(s8[4718592]{0:T(1024)(128)(4,1)} %bitcast.22), calls=%async_computation | async-start | bytes 8388608
  632.5 5.5 slice-start.1

commit v2 on v1

--- a/solution.py
+++ b/solution.py
@@ -192,6 +192,167 @@
 
 def shape(*dims, kind=BF):
     return jax.ShapeDtypeStruct(dims, kind)
+
+
+LAG = 2
+RING = 4
+
+
+def either(condition, other):
+    return jnp.logical_and(condition, other)
+
+
+class Pump:
+    def __init__(self, own, land, ring, result, send, recv, store, first, last, count, outputs):
+        self.own, self.land, self.ring, self.result = own, land, ring, result
+        self.send, self.recv, self.store = send, recv, store
+        self.first, self.last, self.count, self.outputs = first, last, count, outputs
+        self.window = land.shape[1]
+        self.g, self.n = lax.axis_index("group"), lax.axis_size("group")
+
+    def copy(self, way, c):
+        target = (self.g + 1) % self.n if way == 0 else (self.g + self.n - 1) % self.n
+        return pltpu.make_async_remote_copy(
+            self.ring.at[way, c % RING],
+            self.land.at[way, c % self.window],
+            self.send.at[way, c % RING],
+            self.recv.at[way, c % self.window],
+            device_id={"group": target},
+            device_id_type=MESH,
+        )
+
+    def flow(self, way, k):
+        place = self.g if way == 0 else self.n - 1 - self.g
+        c = k - LAG * place
+
+        @pl.when(either(c >= 0, c < self.count))
+        def _():
+            @pl.when(either(place > 0, k - LAG >= self.first))
+            def _():
+                self.copy(way, c).wait_recv()
+
+            @pl.when(place < self.n - 1)
+            def _():
+                @pl.when(either(c >= RING, k - RING >= self.first))
+                def _():
+                    self.copy(way, c - RING).wait_send()
+
+                @pl.when(place > 0)
+                def _():
+                    before = self.land[way, c % self.window].astype(F32)
+                    self.ring[way, c % RING] = (self.own[c].astype(F32) + before).astype(BF)
+
+                @pl.when(place == 0)
+                def _():
+                    self.ring[way, c % RING] = self.own[c]
+
+                self.copy(way, c).start()
+
+    def finished(self, k):
+        far = jnp.maximum(self.g, self.n - 1 - self.g)
+        return k - LAG * far
+
+    def step(self, k):
+        self.flow(0, k)
+        self.flow(1, k)
+        f = self.finished(k)
+
+        @pl.when(either(f >= 0, f < self.count))
+        def _():
+            @pl.when(either(f >= RING, k - RING >= self.first))
+            def _():
+                self.outputs(f - RING, self.result.at[f % RING], self.store, lambda copy: copy.wait())
+
+            mine = self.own[f].astype(F32)
+            slot, held = f % RING, f % self.window
+
+            @pl.when(either(self.g > 0, self.g < self.n - 1))
+            def _():
+                both = self.land[0, held].astype(F32) + self.land[1, held].astype(F32)
+                self.result[slot] = (mine + both).astype(BF)
+
+            @pl.when(self.g == 0)
+            def _():
+                self.result[slot] = (mine + self.land[1, held].astype(F32)).astype(BF)
+
+            @pl.when(self.g == self.n - 1)
+            def _():
+                self.result[slot] = (mine + self.land[0, held].astype(F32)).astype(BF)
+
+            self.outputs(f, self.result.at[slot], self.store, lambda copy: copy.start())
+
+    def drain(self):
+        for way in range(2):
+            place = self.g if way == 0 else self.n - 1 - self.g
+            top = jnp.minimum(self.last - LAG * place, self.count)
+            for j in range(1, RING + 1):
+                c = top - j
+
+                @pl.when(either(place < self.n - 1, either(c >= 0, c + LAG * place >= self.first)))
+                def _(way=way, c=c):
+                    self.copy(way, c).wait_send()
+
+            for k in range(max(self.first, self.last - LAG), self.last):
+                c = k - LAG * (place - 1)
+
+                @pl.when(either(place > 0, either(c >= 0, c < self.count)))
+                def _(way=way, c=c):
+                    self.copy(way, c).wait_recv()
+
+        far = jnp.maximum(self.g, self.n - 1 - self.g)
+        top = jnp.minimum(self.last - LAG * far, self.count)
+        for j in range(1, RING + 1):
+            f = top - j
+
+            @pl.when(either(f >= 0, f + LAG * far >= self.first))
+            def _(f=f):
+                self.outputs(f, self.result.at[f % RING], self.store, lambda copy: copy.wait())
+
+
+class Layout:
+    def __init__(self, m, local, subs, groups):
+        piece = m // subs
+        self.m, self.piece, self.local = m, piece, local
+        self.out_rows = local // subs
+        self.chunk = 48
+        self.feed = 2 * piece
+        self.qkv = self.feed
+        self.kv = self.qkv + 3 * piece // 4
+        self.out = self.kv + piece // 2
+        self.cq = self.out + self.out_rows
+        self.co = self.cq + piece // 4
+        self.rows = self.co + self.out_rows
+        self.count = self.rows // self.chunk
+        self.feed_count = self.feed // self.chunk
+        self.window = LAG * (groups + 1)
+        self.middle = min(10, self.feed_count // 3)
+        self.later = min(32, self.feed_count)
+        self.end = self.count + LAG * (groups - 1)
+
+
+def feed_outputs(layout, o_feed):
+    def outputs(c, block, store, act):
+        act(pltpu.make_async_copy(block, o_feed.at[c], store.at[c % RING, 0]))
+
+    return outputs
+
+
+def pump_scratch(layout, count):
+    chunk, m = layout.chunk, layout.m
+    return [
+        pltpu.VMEM((count, chunk, m), BF),
+        pltpu.VMEM((2, layout.window, chunk, m), BF),
+        pltpu.VMEM((2, RING, chunk, m), BF),
+        pltpu.VMEM((RING, chunk, m), BF),
+        pltpu.SemaphoreType.DMA((2, RING)),
+        pltpu.SemaphoreType.DMA((2, layout.window)),
+        pltpu.SemaphoreType.DMA((RING, 4)),
+    ]
+
+
+def group_ring():
+    g, n = lax.axis_index("group"), lax.axis_size("group")
+    return [{"group": (g + 1) % n}, {"group": (g + n - 1) % n}]
 
 
 def enter_kernel(
@@ -694,8 +855,8 @@
 
 
 def feed_kernel(
-    rows_in, grads_in, up_in, down_in, after_in, o_layer, o_norm, o_pieces,
-    rows, grads, up, down, result, act, pre_grad, part_out, part_norm, land_out, land_norm, stage_out, stage_norm,
+    rows_in, grads_in, up_in, down_in, o_part, o_norm, o_pieces,
+    rows, grads, up, down, act, pre_grad, part_out, part_norm, land_norm, stage_norm,
     whole, land_whole, load, store, send, recv,
 ):
     t, x, y, d = neighbours()
@@ -704,20 +865,19 @@
     loads = [
         pltpu.make_async_copy(a, b, load.at[i])
         for i, (a, b) in enumerate(
-            ((rows_in, rows.at[t]), (up_in, up), (grads_in, grads), (down_in, down), (after_in, result))
+            ((rows_in, rows.at[t]), (up_in, up), (grads_in, grads), (down_in, down))
         )
     ]
     for copy in loads:
         copy.start()
     greet([{"tensor": x}, {"tensor": y}] + [{"sub": (s + k) % subs} for k in range(1, subs)])
-    n, m = result.shape
+    _, n, m = rows.shape
     hidden = up.shape[1]
     loads[0].wait()
     gather = Gather(rows.at[t], rows, send, recv, 0)
     gather.start()
     back = Scatter(part_norm, land_norm, stage_norm, send, recv, 6)
-    fore = Scatter(part_out, land_out, stage_out, send, recv, 12)
-    halves = Halves(whole, land_whole, send, recv, 18)
+    halves = Halves(whole, land_whole, send, recv, 12)
     for copy in loads[1:4]:
         copy.wait()
 
@@ -774,14 +934,11 @@
         return carry
 
     lax.fori_loop(0, 4, turn, 0)
-    fore.diagonal()
-    fore.along_x()
-    fore.along_y()
+    stores = [pltpu.make_async_copy(part_out, o_part, store.at[1])]
+    stores[0].start()
     weight_grad(act, grads, whole, 0, halves, 256)
     back.relay()
     weight_grad(rows, pre_grad, whole, 1, halves, 256)
-    fore.relay()
-    loads[4].wait()
     pieces = land_whole
     for w in range(2):
 
@@ -789,17 +946,10 @@
             pieces[w, 0, here] = value.astype(BF)
 
         halves.total(w, take, 64)
-    stores = [pltpu.make_async_copy(pieces.at[:, 0], o_pieces, store.at[0])]
-    stores[0].start()
-
-    def take_out(here, total):
-        result[here] = result[here] + total
-
+    stores.append(pltpu.make_async_copy(pieces.at[:, 0], o_pieces, store.at[0]))
+    stores[1].start()
     norm_total = part_norm
 
-    fore.finish(take_out, 64)
-    stores.append(pltpu.make_async_copy(result, o_layer, store.at[1]))
-    stores[1].start()
 
     def take_norm(here, total):
         norm_total[t, here] = total.astype(BF)
@@ -809,34 +959,32 @@
     stores[2].start()
     gather.drain()
     back.drain()
-    fore.drain()
     for w in range(2):
         halves.drain(w)
     for copy in stores:
         copy.wait()
 
 
-def feed(rows, grads, up, down, after, subs):
+def feed(rows, grads, up, down, subs):
     n, m = rows.shape
     hidden = up.shape[1]
-    count = 18 + 2 * (subs - 1)
+    count = 12 + 2 * (subs - 1)
     return pl.pallas_call(
         feed_kernel,
         name="feed",
-        out_shape=[shape(n, m, kind=F32), shape(n, m), shape(2, m // subs, hidden)],
-        in_specs=[ANY] * 5,
+        out_shape=[shape(4, n, m), shape(n, m), shape(2, m // subs, hidden)],
+        in_specs=[ANY] * 4,
         out_specs=[ANY] * 3,
         scratch_shapes=[
             pltpu.VMEM((4, n, m), BF), pltpu.VMEM((4, n, m), BF), pltpu.VMEM((m, hidden), BF), pltpu.VMEM((hidden, m), BF),
-            pltpu.VMEM((n, m), F32), pltpu.VMEM((4, n, hidden), BF), pltpu.VMEM((4, n, hidden), BF),
+            pltpu.VMEM((4, n, hidden), BF), pltpu.VMEM((4, n, hidden), BF),
             pltpu.VMEM((4, n, m), BF), pltpu.VMEM((4, n, m), BF),
-            pltpu.VMEM((6, n // 2, m), BF), pltpu.VMEM((6, n // 2, m), BF),
-            pltpu.VMEM((2, n // 2, m), BF), pltpu.VMEM((2, n // 2, m), BF),
+            pltpu.VMEM((6, n // 2, m), BF), pltpu.VMEM((2, n // 2, m), BF),
             pltpu.VMEM((2, m, hidden), BF), pltpu.VMEM((2, subs - 1, m // subs, hidden), BF),
-            dma(5), dma(3), dma(count), dma(count),
+            dma(4), dma(3), dma(count), dma(count),
         ],
         compiler_params=params(4),
-    )(rows, grads, up, down, after)
+    )(rows, grads, up, down)
 
 
 def norm_back_block(grad, source, gain):
@@ -859,12 +1007,15 @@
 
 
 def cross_back_kernel(
-    cot_in, norm_in, cross_in, self_in, gains_in, query_in, flat_in, memory_in, wq_in, wo_in,
-    o_out, o_branch, o_sums, o_memory, o_wq, o_wo,
+    layout,
+    cot_in, norm_in, cross_in, self_in, gains_in, query_in, flat_in, memory_in, wq_in, wo_in, part_in, own_in,
+    o_out, o_branch, o_sums, o_memory, o_wq, o_wo, o_layer, o_feed, o_land,
     cot, norm, after_cross, after_self, gains, query, flat, memory, wq, wo,
     branch, rows, query_grad, memory_grad, sums, whole_q, whole_o, land_q, land_o, piece_q, piece_o,
+    norm_self, part, land_part, stage_part, own, land, ring, result, ring_send, ring_recv, ring_store,
     load, store, send, recv,
 ):
+    t, x, y, d = neighbours()
     s = lax.axis_index("sub")
     subs = lax.axis_size("sub")
     loads = [
@@ -873,17 +1024,27 @@
             (
                 (cot_in, cot), (norm_in, norm), (cross_in, after_cross), (gains_in, gains), (wo_in, wo),
                 (query_in, query), (flat_in, flat), (memory_in, memory), (self_in, after_self), (wq_in, wq),
+                (part_in, part), (own_in, own),
             )
         )
     ]
     for copy in loads:
         copy.start()
-    greet([{"sub": (s + k) % subs} for k in range(1, subs)])
+    greet([{"tensor": x}, {"tensor": y}] + [{"sub": (s + k) % subs} for k in range(1, subs)] + group_ring())
+    scatter = Scatter(part, land_part, stage_part, send, recv, 8 * (subs - 1))
+    pump = Pump(
+        own, land, ring, result, ring_send, ring_recv, ring_store, 0, layout.middle, layout.count,
+        feed_outputs(layout, o_feed),
+    )
     n, m = cot.shape
     width = wq.shape[2]
     texts = memory.shape[1]
-    for copy in loads[:4]:
+    for copy in (*loads[:4], *loads[10:]):
         copy.wait()
+    scatter.diagonal()
+    scatter.along_x()
+    scatter.along_y()
+    pump.step(jnp.int32(0))
     scale = HEAD ** (-0.5)
 
     def feed_block(i, carry):
@@ -910,8 +1071,17 @@
     lax.fori_loop(0, n // 64, norm_block, 0)
     for copy in loads[4:8]:
         copy.wait()
+    middle = layout.middle
+
+    def tick(k):
+        @pl.when(k < middle)
+        def _():
+            pump.step(k)
+
+    tick(jnp.int32(1))
 
     def quarter(q, carry):
+        tick(q + 2)
         grad_heads = dot_t(branch[...], wo[rows_at(q, width)]).astype(BF)
         whole_q_cols = cols(q, width)
         query_grad_block = []
@@ -939,7 +1109,11 @@
     halves_q = Halves(whole_q, land_q, send, recv, 0)
     halves_o = Halves(whole_o, land_o, send, recv, 4 * (subs - 1))
 
+    scatter.relay()
+
     def weights(q, carry):
+        tick(q + 6)
+
         def grad_o(j, carry):
             whole_o[q, :, cols(j, 512)] = dot_c(flat[:, cols(q, width)], branch[:, cols(j, 512)]).astype(BF)
             return carry
@@ -964,14 +1138,14 @@
         total = jnp.zeros((n, 256), F32)
         for q in range(4):
             total = total + dot_t(query_grad[:, q * width : (q + 1) * width], wq[q, here])
-        after_cross[:, cols(j, 256)] = total
+        norm_self[:, cols(j, 256)] = total
         return carry
 
     lax.fori_loop(0, m // 256, norm_grad, 0)
 
     def self_block(i, carry):
         here = rows_at(i, 64)
-        grad = after_cross[here]
+        grad = norm_self[here]
         inner, terms = norm_back_block(grad, after_self[here], gains[0:1])
         total = cot[here] + inner
         cot[here] = total
@@ -988,6 +1162,13 @@
     ]
     for copy in stores[1:]:
         copy.start()
+
+    def take_layer(here, total):
+        after_cross[here] = after_cross[here] + total
+
+    scatter.finish(take_layer, 64)
+    stores.append(pltpu.make_async_copy(after_cross, o_layer, store.at[6]))
+    stores[-1].start()
     for halves, piece in ((halves_q, piece_q), (halves_o, piece_o)):
         for q in range(4):
 
@@ -996,8 +1177,12 @@
 
             halves.total(q, take, 16)
     stores += [pltpu.make_async_copy(piece_q, o_wq, store.at[4]), pltpu.make_async_copy(piece_o, o_wo, store.at[5])]
-    for copy in stores[4:]:
+    for copy in stores[5:]:
         copy.start()
+    pump.drain()
+    stores.append(pltpu.make_async_copy(land, o_land, store.at[7]))
+    stores[-1].start()
+    scatter.drain()
     for q in range(4):
         halves_q.drain(q)
         halves_o.drain(q)
@@ -1005,19 +1190,22 @@
         copy.wait()
 
 
-def cross_back(cot, norm, after_cross, after_self, gains, query, flat, memory, wq, wo, subs):
+def cross_back(layout, cot, norm, after_cross, after_self, gains, query, flat, memory, wq, wo, part, own, subs):
     n, m = cot.shape
     width = wq.shape[2]
-    count = 8 * (subs - 1)
+    count = 8 * (subs - 1) + 6
+    chunks = layout.feed_count
+    held = (2, layout.window, layout.chunk, m)
     part_q, part_o = (4, m // subs, width), (4, width // subs, m)
     return pl.pallas_call(
-        cross_back_kernel,
+        partial(cross_back_kernel, layout),
         name="cross_back",
         out_shape=[
             shape(n, m, kind=F32), shape(n, m), shape(32, m, kind=F32), shape(*memory.shape), shape(*part_q), shape(*part_o),
+            shape(n, m, kind=F32), shape(layout.feed_count, layout.chunk, m), shape(*held),
         ],
-        in_specs=[ANY] * 10,
-        out_specs=[ANY] * 6,
+        in_specs=[ANY] * 12,
+        out_specs=[ANY] * 9,
         scratch_shapes=[
             pltpu.VMEM((n, m), F32), pltpu.VMEM((n, m), BF), pltpu.VMEM((n, m), F32), pltpu.VMEM((n, m), F32),
             pltpu.VMEM(gains.shape, F32), pltpu.VMEM((n, m), BF), pltpu.VMEM((n, m), BF), pltpu.VMEM(memory.shape, BF),
@@ -1026,59 +1214,58 @@
             pltpu.VMEM((32, m), F32), pltpu.VMEM((4, m, width), BF), pltpu.VMEM((4, width, m), BF),
             pltpu.VMEM((4, subs - 1, m // subs, width), BF), pltpu.VMEM((4, subs - 1, width // subs, m), BF),
             pltpu.VMEM(part_q, BF), pltpu.VMEM(part_o, BF),
-            dma(10), dma(6), dma(count), dma(count),
+            pltpu.VMEM((n, m), F32), pltpu.VMEM((4, n, m), BF), pltpu.VMEM((6, n // 2, m), BF), pltpu.VMEM((2, n // 2, m), BF),
+            *pump_scratch(layout, chunks),
+            dma(12), dma(8), dma(count), dma(count),
         ],
         compiler_params=params(5),
-    )(cot, norm, after_cross, after_self, gains, query, flat, memory, wq, wo)
-
-
-def attend_rows_back(triple, place, blocks, heads, grad_heads, deltas, sums, grads, grad_keys, grad_values):
+    )(cot, norm, after_cross, after_self, gains, query, flat, memory, wq, wo, part, own)
+
+
+def attend_pair_back(p, triple, place, blocks, heads, grad_heads, deltas, sums, grads, grad_keys, grad_values):
     n = triple.shape[1]
     width = heads * HEAD
     scale = HEAD ** (-0.5)
     lanes = head_lanes(n)
     key_lanes = head_lanes(blocks * n)
 
-    def pair(p, carry):
-        here = pl.ds(pl.multiple_of(p * 128, 128), 128)
-        key_cols = pl.ds(pl.multiple_of(width + p * 128, 128), 128)
-        value_cols = pl.ds(pl.multiple_of(2 * width + p * 128, 128), 128)
-        query = triple[place, :, here]
-        grad = grad_heads[place, :, here]
-        keys = triple[0:blocks, :, key_cols].reshape(blocks * n, 128)
-        values = triple[0:blocks, :, value_cols].reshape(blocks * n, 128)
-        stats = sums[place]
-        means = deltas[place]
-        found = []
-        for h in range(2):
-            mine = (lanes < HEAD) if h == 0 else (lanes >= HEAD)
-            log_sum = jnp.sum(jnp.where(lanes == 2 * p + h, stats, 0.0), -1, keepdims=True)
-            delta = jnp.sum(jnp.where(lanes == 2 * p + h, means, 0.0), -1, keepdims=True)
-            scores = dot_t(jnp.where(mine, query, jnp.zeros_like(query)), keys)
-            row = lax.broadcasted_iota(jnp.int32, scores.shape, 0)
-            col = lax.broadcasted_iota(jnp.int32, scores.shape, 1)
-            probs = jnp.where(
-                col <= row + (blocks - 1) * n, jnp.exp2(scores * (scale * LOG2E) - log_sum), 0.0
-            )
-            grad_probs = dot_t(jnp.where(mine, grad, jnp.zeros_like(grad)), values)
-            grad_scores = (probs * (grad_probs - delta)).astype(BF)
-            found.append((dot(grad_scores, keys), dot_c(grad_scores, query), dot_c(probs.astype(BF), grad)))
-        grads[place, :, here] = (jnp.where(lanes < HEAD, found[0][0], found[1][0]) * scale).astype(BF)
-        grad_keys[0 : blocks * n, here] += jnp.where(key_lanes < HEAD, found[0][1], found[1][1]) * scale
-        grad_values[0 : blocks * n, here] += jnp.where(key_lanes < HEAD, found[0][2], found[1][2])
-        return carry
-
-    lax.fori_loop(0, heads // 2, pair, 0)
+    here = pl.ds(pl.multiple_of(p * 128, 128), 128)
+    key_cols = pl.ds(pl.multiple_of(width + p * 128, 128), 128)
+    value_cols = pl.ds(pl.multiple_of(2 * width + p * 128, 128), 128)
+    query = triple[place, :, here]
+    grad = grad_heads[place, :, here]
+    keys = triple[0:blocks, :, key_cols].reshape(blocks * n, 128)
+    values = triple[0:blocks, :, value_cols].reshape(blocks * n, 128)
+    stats = sums[place]
+    means = deltas[place]
+    found = []
+    for h in range(2):
+        mine = (lanes < HEAD) if h == 0 else (lanes >= HEAD)
+        log_sum = jnp.sum(jnp.where(lanes == 2 * p + h, stats, 0.0), -1, keepdims=True)
+        delta = jnp.sum(jnp.where(lanes == 2 * p + h, means, 0.0), -1, keepdims=True)
+        scores = dot_t(jnp.where(mine, query, jnp.zeros_like(query)), keys)
+        row = lax.broadcasted_iota(jnp.int32, scores.shape, 0)
+        col = lax.broadcasted_iota(jnp.int32, scores.shape, 1)
+        probs = jnp.where(
+            col <= row + (blocks - 1) * n, jnp.exp2(scores * (scale * LOG2E) - log_sum), 0.0
+        )
+        grad_probs = dot_t(jnp.where(mine, grad, jnp.zeros_like(grad)), values)
+        grad_scores = (probs * (grad_probs - delta)).astype(BF)
+        found.append((dot(grad_scores, keys), dot_c(grad_scores, query), dot_c(probs.astype(BF), grad)))
+    grads[place, :, here] = (jnp.where(lanes < HEAD, found[0][0], found[1][0]) * scale).astype(BF)
+    grad_keys[0 : blocks * n, here] += jnp.where(key_lanes < HEAD, found[0][1], found[1][1]) * scale
+    grad_values[0 : blocks * n, here] += jnp.where(key_lanes < HEAD, found[0][2], found[1][2])
 
 
 def attend_back_kernel(
+    layout,
     branch_in, triple_in, flat_in, sums_in, out_in, qkv_in, rows_in, frames_in, gains_in, grad_in, memory_in, text_in, kv_in,
-    cross_q_in, cross_o_in,
-    o_frames, o_sums, o_text, o_qkv, o_out, o_kv, o_cq, o_co,
+    own_in, land_in, feed_in,
+    o_frames, o_sums, o_text, o_qkv, o_out, o_kv, o_feed, o_land,
     branch, triple, flat, sums, out, qkv, rows, frames, gains, grad_out, memory, text, kv,
-    cross_q, cross_o, land_q, land_o, land_m, stage_q, stage_o, stage_m,
+    land_m, stage_m,
     grad_heads, deltas, grads, grad_keys, grad_values, part, land, stage, whole_qkv, land_qkv, whole_out, land_out,
-    whole_kv, land_kv, text_grad, sums_out, sum_m,
+    whole_kv, land_kv, text_grad, sums_out, sum_m, own, held, ring, result, ring_send, ring_recv, ring_store,
     load, store, send, recv,
 ):
     t, x, y, d = neighbours()
@@ -1086,13 +1273,26 @@
     subs = lax.axis_size("sub")
     names = (
         (branch_in, branch.at[t]), (out_in, out), (flat_in, flat), (triple_in, triple), (sums_in, sums),
-        (memory_in, memory), (cross_q_in, cross_q), (cross_o_in, cross_o), (qkv_in, qkv), (rows_in, rows),
+        (memory_in, memory), (own_in, own), (land_in, held), (qkv_in, qkv), (rows_in, rows),
         (text_in, text), (kv_in, kv), (frames_in, frames), (gains_in, gains), (grad_in, grad_out),
     )
     loads = [pltpu.make_async_copy(a, b, load.at[i]) for i, (a, b) in enumerate(names)]
-    for copy in loads:
+    loads[7].start()
+    for copy in loads[:7] + loads[8:]:
         copy.start()
-    greet([{"tensor": x}, {"tensor": y}] + [{"sub": (s + k) % subs} for k in range(1, subs)])
+    loads[7].wait()
+    greet([{"tensor": x}, {"tensor": y}] + [{"sub": (s + k) % subs} for k in range(1, subs)] + group_ring())
+    first, last = layout.middle, layout.later
+    pump = Pump(
+        own, held, ring, result, ring_send, ring_recv, ring_store, first, last, layout.count,
+        feed_outputs(layout, o_feed),
+    )
+
+    def tick(k):
+        @pl.when(k + first < last)
+        def _():
+            pump.step(k + first)
+
     n, m = grad_out.shape
     width = triple.shape[2]
     local = out.shape[0]
@@ -1100,19 +1300,16 @@
     gather = Gather(branch.at[t], branch, send, recv, 0)
     scatter = Scatter(part, land, stage, send, recv, 6)
     scatter_m = Scatter(memory, land_m, stage_m, send, recv, 12)
-    scatter_q = Scatter(cross_q, land_q, stage_q, send, recv, 18)
-    scatter_o = Scatter(cross_o, land_o, stage_o, send, recv, 24)
-    halves_qkv = Halves(whole_qkv, land_qkv, send, recv, 30)
-    halves_out = Halves(whole_out, land_out, send, recv, 30 + subs - 1)
-    halves_kv = Halves(whole_kv, land_kv, send, recv, 30 + 2 * (subs - 1))
+    halves_qkv = Halves(whole_qkv, land_qkv, send, recv, 18)
+    halves_out = Halves(whole_out, land_out, send, recv, 18 + subs - 1)
+    halves_kv = Halves(whole_kv, land_kv, send, recv, 18 + 2 * (subs - 1))
     loads[0].wait()
     gather.start()
-    for copy in loads[5:8]:
+    for copy in loads[5:7]:
         copy.wait()
-    for each in (scatter_m, scatter_q, scatter_o):
-        each.diagonal()
-        each.along_x()
-        each.along_y()
+    scatter_m.diagonal()
+    scatter_m.along_x()
+    scatter_m.along_y()
     for copy in loads[1:5]:
         copy.wait()
     grad_keys[...] = jnp.zeros_like(grad_keys)
@@ -1148,14 +1345,20 @@
             return jnp.where(lanes == 2 * p, low, jnp.where(lanes == 2 * p + 1, high, stats))
 
         deltas[place] = lax.fori_loop(0, heads // 2, delta, jnp.zeros((n, 128), F32))
-        for blocks in range(1, 5):
-
-            @pl.when(place == blocks - 1)
-            def _(blocks=blocks):
-                attend_rows_back(
-                    triple, blocks - 1, blocks, heads, grad_heads, deltas, sums, grads, grad_keys, grad_values
-                )
-
+
+        def pair(p, carry):
+            tick(i * (heads // 2) + p)
+            for blocks in range(1, 5):
+
+                @pl.when(place == blocks - 1)
+                def _(blocks=blocks):
+                    attend_pair_back(
+                        p, triple, blocks - 1, blocks, heads, grad_heads, deltas, sums, grads, grad_keys, grad_values
+                    )
+
+            return carry
+
+        lax.fori_loop(0, heads // 2, pair, 0)
         return carry
 
     lax.fori_loop(0, 4, turn, 0)
@@ -1179,6 +1382,7 @@
             return carry
 
         lax.fori_loop(0, m // 512, step, 0)
+        tick(12 + i)
 
         @pl.when(i == 0)
         def _():
@@ -1195,8 +1399,7 @@
         return carry
 
     lax.fori_loop(0, 4, back, 0)
-    for each in (scatter_m, scatter_q, scatter_o):
-        each.relay()
+    scatter_m.relay()
 
     def take_m(here, total):
         sum_m[here] = total.astype(BF)
@@ -1224,6 +1427,7 @@
     scatter.relay()
 
     def grad_wqkv(j, carry):
+        tick(16 + j)
         turned = rows[:, :, cols(j, 256)].reshape(4 * n, 256)
 
         def inner(i, carry):
@@ -1237,16 +1441,7 @@
 
     lax.fori_loop(0, m // 256, grad_wqkv, 0)
     halves_qkv.start(0)
-    for each, landed, output, slot in ((scatter_q, land_q, o_cq, 1), (scatter_o, land_o, o_co, 2)):
-        half = each.half
-
-        def take(here, total, each=each):
-            each.part[t, here] = total.astype(BF)
-
-        each.finish(take, 16)
-        stores.append(pltpu.make_async_copy(each.part.at[t], output, store.at[slot]))
-        stores[-1].start()
-    for each, output, slot in ((halves_kv, o_kv, 3), (halves_out, o_out, 4), (halves_qkv, o_qkv, 5)):
+    for each, output, slot in ((halves_kv, o_kv, 1), (halves_out, o_out, 2), (halves_qkv, o_qkv, 3)):
 
         def take(here, total, each=each):
             each.land[0, 0, here] = total.astype(BF)
@@ -1273,11 +1468,14 @@
     gain_sum, bias_sum = lax.fori_loop(0, n // 64, frame_block, (zero, zero))
     sums_out[0:8] = gain_sum
     sums_out[8:16] = bias_sum
-    stores += [pltpu.make_async_copy(grad_out, o_frames, store.at[6]), pltpu.make_async_copy(sums_out, o_sums, store.at[7])]
+    stores += [pltpu.make_async_copy(grad_out, o_frames, store.at[4]), pltpu.make_async_copy(sums_out, o_sums, store.at[5])]
     for copy in stores[-2:]:
         copy.start()
+    pump.drain()
+    stores.append(pltpu.make_async_copy(held, o_land, store.at[6]))
+    stores[-1].start()
     gather.drain()
-    for each in (scatter, scatter_m, scatter_q, scatter_o):
+    for each in (scatter, scatter_m):
         each.drain()
     for each in (halves_qkv, halves_out, halves_kv):
         each.drain(0)
@@ -1285,86 +1483,93 @@
         copy.wait()
 
 
-def attend_back(branch, triple, flat, sums, out, qkv, rows, frames, gains, grad, memory, text, kv, cross_q, cross_o, subs):
+def attend_back(
+    layout, branch, triple, flat, sums, out, qkv, rows, frames, gains, grad, memory, text, kv, own, land, feed_sums, subs
+):
     n, m = grad.shape
     width = triple.shape[2]
     local = out.shape[0]
     texts, kvw = text.shape[0], kv.shape[1]
-    count = 30 + 3 * (subs - 1)
-    piece_q, piece_o = cross_q.shape[1:], cross_o.shape[1:]
+    count = 18 + 3 * (subs - 1)
     v = pltpu.VMEM
     return pl.pallas_call(
-        attend_back_kernel,
+        partial(attend_back_kernel, layout),
         name="attend_back",
         out_shape=[
             shape(n, m, kind=F32), shape(16, m, kind=F32), shape(texts, m, kind=F32), shape(m // subs, width),
-            shape(local // subs, m), shape(m // subs, kvw), shape(*piece_q), shape(*piece_o),
+            shape(local // subs, m), shape(m // subs, kvw), shape(*feed_sums.shape), shape(*land.shape),
         ],
-        in_specs=[ANY] * 15,
+        in_specs=[ANY] * 16,
         out_specs=[ANY] * 8,
+        input_output_aliases={15: 6},
         scratch_shapes=[
             v((4, n, m), BF), v(triple.shape, BF), v(flat.shape, BF), v(sums.shape, F32), v(out.shape, BF), v(qkv.shape, BF),
             v(rows.shape, BF), v(frames.shape, frames.dtype), v(gains.shape, F32), v((n, m), F32), v(memory.shape, BF),
             v(text.shape, BF), v(kv.shape, BF),
-            v(cross_q.shape, BF), v(cross_o.shape, BF),
-            v((6, piece_q[0] // 2, piece_q[1]), BF), v((6, piece_o[0] // 2, piece_o[1]), BF), v((6, texts // 2, kvw), BF),
-            v((2, piece_q[0] // 2, piece_q[1]), BF), v((2, piece_o[0] // 2, piece_o[1]), BF), v((2, texts // 2, kvw), BF),
+            v((6, texts // 2, kvw), BF), v((2, texts // 2, kvw), BF),
             v((4, n, local), BF), v((4, n, 128), F32), v((4, n, width), BF), v((4 * n, local), F32), v((4 * n, local), F32),
             v((4, n, m), BF), v((6, n // 2, m), BF), v((2, n // 2, m), BF),
             v((1, m, width), BF), v((1, subs - 1, m // subs, width), BF),
             v((1, local, m), BF), v((1, subs - 1, local // subs, m), BF),
             v((1, m, kvw), BF), v((1, subs - 1, m // subs, kvw), BF),
             v((texts, m), F32), v((16, m), F32), v((texts, kvw), BF),
-            dma(15), dma(8), dma(count), dma(count),
+            *pump_scratch(layout, layout.feed_count),
+            dma(15), dma(7), dma(count), dma(count),
         ],
         compiler_params=params(6),
-    )(branch, triple, flat, sums, out, qkv, rows, frames, gains, grad, memory, text, kv, cross_q, cross_o)
+    )(branch, triple, flat, sums, out, qkv, rows, frames, gains, grad, memory, text, kv, own, land, feed_sums)
 
 
 def total_kernel(
-    feed_in, qkv_in, cq_in, kv_in, out_in, co_in, sums_a_in, sums_b_in, text_in,
-    o_up, o_down, o_qkv, o_cq, o_kv, o_out, o_co, o_text, o_vectors,
-    own, from_left, from_right, to_right, to_left, result, sums_a, sums_b, text, text_land, text_full, vectors, vectors_land, share,
-    share_land, load, store, send_right, recv_right, send_left, recv_left, send, recv,
+    layout,
+    feed_in, qkv_in, kv_in, out_in, cross_q_in, cross_o_in, sums_a_in, sums_b_in, text_in, land_in, summed_in,
+    o_qkv, o_cq, o_kv, o_out, o_co, o_text, o_vectors, o_feed,
+    own, held, ring, result, ring_send, ring_recv, ring_store,
+    cross_q, cross_o, land_q, land_o, stage_q, stage_o,
+    sums_a, sums_b, text, text_land, text_full, vectors, vectors_land, share, share_land, load, store, send, recv,
 ):
     t, x, y, d = neighbours()
     s, subs = lax.axis_index("sub"), lax.axis_size("sub")
     g, groups = lax.axis_index("group"), lax.axis_size("group")
-    chunk = result.shape[1]
-    m = own.shape[1]
-    width, cq_width, kv_width = qkv_in.shape[1], cq_in.shape[1], kv_in.shape[1]
-    piece, kv_rows, out_rows = feed_in.shape[1], kv_in.shape[0] // 2, out_in.shape[0]
-    start_qkv = 2 * piece
-    start_kv = start_qkv + qkv_in.shape[0]
-    start_out = start_kv + kv_rows
-    start_co = start_out + out_rows
-    count = own.shape[0] // chunk
-    loads = [
-        pltpu.make_async_copy(a, b, load.at[i])
-        for i, (a, b) in enumerate(
+    chunk, m, local = layout.chunk, layout.m, layout.local
+    width, quarter = 3 * local, layout.piece // 4 // chunk
+    at_qkv, at_kv, at_out, at_cq, at_co = (
+        r // chunk for r in (layout.qkv, layout.kv, layout.out, layout.cq, layout.co)
+    )
+    outs = layout.out_rows // chunk
+    pairs = [
+        (land_in, held),
+        (feed_in, own.at[pl.ds(0, at_qkv)]),
+        (qkv_in.at[pl.ds(0, 3 * quarter)], own.at[pl.ds(at_qkv, 3 * quarter), :, pl.ds(0, width)]),
+    ]
+    for i in range(3):
+        pairs.append(
             (
-                (feed_in.at[0], own.at[pl.ds(0, piece)]),
-                (feed_in.at[1], own.at[pl.ds(piece, piece)]),
-                (qkv_in, own.at[pl.ds(start_qkv, piece), pl.ds(0, width)]),
-                (cq_in, own.at[pl.ds(start_qkv, piece), pl.ds(width, cq_width)]),
-                (kv_in.at[pl.ds(0, kv_rows)], own.at[pl.ds(start_kv, kv_rows), pl.ds(0, kv_width)]),
-                (kv_in.at[pl.ds(kv_rows, kv_rows)], own.at[pl.ds(start_kv, kv_rows), pl.ds(kv_width, kv_width)]),
-                (out_in, own.at[pl.ds(start_out, out_rows)]),
-                (co_in, own.at[pl.ds(start_co, out_rows)]),
-                (sums_a_in, sums_a),
-                (sums_b_in, sums_b),
-                (text_in, text),
+                qkv_in.at[pl.ds(3 * quarter, quarter), :, pl.ds(i * local, local)],
+                own.at[pl.ds(at_qkv + i * quarter, quarter), :, pl.ds(width, local)],
             )
         )
+    for i in range(2):
+        pairs.append(
+            (
+                kv_in.at[pl.ds(2 * i * quarter, 2 * quarter)],
+                own.at[pl.ds(at_kv, 2 * quarter), :, pl.ds(2 * i * local, 2 * local)],
+            )
+        )
+    pairs += [
+        (out_in, own.at[pl.ds(at_out, outs)]),
+        (sums_a_in, sums_a), (sums_b_in, sums_b), (text_in, text), (cross_q_in, cross_q), (cross_o_in, cross_o),
     ]
+    loads = [pltpu.make_async_copy(a, b, load.at[i]) for i, (a, b) in enumerate(pairs)]
     for copy in loads:
         copy.start()
+    loads[0].wait()
     greet(
         [{"tensor": x}, {"tensor": y}, {"tensor": d}]
         + [{"sub": (s + k) % subs} for k in range(1, subs)]
         + [{"group": (g + k) % groups} for k in range(1, groups)]
     )
-    for copy in loads:
+    for copy in loads[1:]:
         copy.wait()
     share_width = m // subs
     for i in range(6):
@@ -1396,141 +1601,64 @@
         remote(share.at[1, 0], share_land.at[subs - 2 + k], base + k - 1, {"group": (g + k) % groups})
         for k in range(1, groups)
     ]
+    base += groups - 1
+    scatter_q = Scatter(cross_q, land_q, stage_q, send, recv, base)
+    scatter_o = Scatter(cross_o, land_o, stage_o, send, recv, base + 6)
     for copy in first:
         copy.start()
-
-    def right(c):
-        return pltpu.make_async_remote_copy(
-            to_right.at[c % 4], from_left.at[c], send_right.at[c % 4], recv_right.at[c],
-            device_id={"group": (g + 1) % groups}, device_id_type=MESH,
-        )
-
-    def left(c):
-        return pltpu.make_async_remote_copy(
-            to_left.at[c % 4], from_right.at[c], send_left.at[c % 4], recv_left.at[c],
-            device_id={"group": (g + groups - 1) % groups}, device_id_type=MESH,
-        )
-
-    def outputs(c, act):
-        row = c * chunk
-        slot = c % 4
-        block = result.at[slot]
+    for each in (scatter_q, scatter_o):
+        each.diagonal()
+    for each in (scatter_q, scatter_o):
+        each.along_x()
+        each.along_y()
+
+    def outputs(c, block, slots, act):
+        slot = c % RING
 
         def region(begin, end, copies):
-            @pl.when(jnp.logical_and(row >= begin, row < end))
+            @pl.when(jnp.logical_and(c >= begin, c < end))
             def _():
-                for i, (source, target) in enumerate(copies(pl.multiple_of(row - begin, chunk))):
-                    act(pltpu.make_async_copy(source, target, store.at[2 * slot + i]))
+                for i, (source, target) in enumerate(copies(c - begin)):
+                    act(pltpu.make_async_copy(source, target, slots.at[slot, i]))
 
         def whole(output):
-            return lambda at: [(block, output.at[pl.ds(at, chunk)])]
-
-        region(0, piece, whole(o_down))
-        region(piece, start_qkv, whole(o_up))
+            return lambda r: [(block, output.at[r])]
+
+        region(layout.later - LAG * (groups - 1), at_qkv, lambda r: [(block, o_feed.at[c])])
         region(
-            start_qkv, start_kv,
-            lambda at: [
-                (block.at[:, pl.ds(0, width)], o_qkv.at[pl.ds(at, chunk)]),
-                (block.at[:, pl.ds(width, cq_width)], o_cq.at[pl.ds(at, chunk)]),
+            at_qkv, at_kv,
+            lambda r: [
+                (block.at[:, pl.ds(0, width)], o_qkv.at[r]),
+                (
+                    block.at[:, pl.ds(width, local)],
+                    o_qkv.at[3 * quarter + r % quarter, :, pl.ds(pl.multiple_of(r // quarter * local, local), local)],
+                ),
             ],
         )
         region(
-            start_kv, start_out,
-            lambda at: [
-                (block.at[:, pl.ds(0, kv_width)], o_kv.at[pl.ds(at, chunk)]),
-                (
-                    block.at[:, pl.ds(kv_width, kv_width)],
-                    o_kv.at[pl.ds(pl.multiple_of(kv_rows + at, chunk), chunk)],
-                ),
+            at_kv, at_out,
+            lambda r: [
+                (block.at[:, pl.ds(2 * i * local, 2 * local)], o_kv.at[2 * i * quarter + r]) for i in range(2)
             ],
         )
-        region(start_out, start_co, whole(o_out))
-        region(start_co, start_co + out_rows, whole(o_co))
-
-    lag = 2
-    far = jnp.maximum(g, groups - 1 - g)
-
-    def step(k, carry):
-        c = k - lag * g
-
-        @pl.when(jnp.logical_and(c >= 0, c < count))
-        def _():
-            @pl.when(g > 0)
-            def _():
-                right(c).wait_recv()
-
-            @pl.when(g < groups - 1)
-            def _():
-                @pl.when(c >= 4)
-                def _():
-                    right(c - 4).wait_send()
-
-                mine = own[rows_at(c, chunk)]
-
-                @pl.when(g > 0)
-                def _():
-                    to_right[c % 4] = (mine.astype(F32) + from_left[c].astype(F32)).astype(BF)
-
-                @pl.when(g == 0)
-                def _():
-                    to_right[c % 4] = mine
-
-                right(c).start()
-
-        e = k - lag * (groups - 1 - g)
-
-        @pl.when(jnp.logical_and(e >= 0, e < count))
-        def _():
-            @pl.when(g < groups - 1)
-            def _():
-                left(e).wait_recv()
-
-            @pl.when(g > 0)
-            def _():
-                @pl.when(e >= 4)
-                def _():
-                    left(e - 4).wait_send()
-
-                mine = own[rows_at(e, chunk)]
-
-                @pl.when(g < groups - 1)
-                def _():
-                    to_left[e % 4] = (mine.astype(F32) + from_right[e].astype(F32)).astype(BF)
-
-                @pl.when(g == groups - 1)
-                def _():
-                    to_left[e % 4] = mine
-
-                left(e).start()
-
-        f = k - lag * far
-
-        @pl.when(jnp.logical_and(f >= 0, f < count))
-        def _():
-            @pl.when(f >= 4)
-            def _():
-                outputs(f - 4, lambda copy: copy.wait())
-
-            mine = own[rows_at(f, chunk)].astype(F32)
-
-            @pl.when(jnp.logical_and(g > 0, g < groups - 1))
-            def _():
-                result[f % 4] = mine + from_left[f].astype(F32) + from_right[f].astype(F32)
-
-            @pl.when(g == 0)
-            def _():
-                result[f % 4] = mine + from_right[f].astype(F32)
-
-            @pl.when(g == groups - 1)
-            def _():
-                result[f % 4] = mine + from_left[f].astype(F32)
-
-            outputs(f, lambda copy: copy.start())
-
-        return carry
-
-    steps = count + lag * (groups - 1)
-    lax.fori_loop(0, 3, step, 0)
+        region(at_out, at_cq, whole(o_out))
+        region(
+            at_cq, at_co,
+            lambda r: [(block.at[:, pl.ds(i * local, local)], o_cq.at[i * quarter + r]) for i in range(4)],
+        )
+        region(at_co, at_co + outs, whole(o_co))
+
+    begin, end = layout.later, layout.end
+    pump = Pump(own, held, ring, result, ring_send, ring_recv, ring_store, begin, end, layout.count, outputs)
+
+    def run(a, b):
+        def step(k, carry):
+            pump.step(k)
+            return carry
+
+        lax.fori_loop(a, b, step, 0)
+
+    run(begin, begin + 3)
     for copy in first:
         copy.wait_recv()
     for j in range(subs):
@@ -1540,69 +1668,84 @@
         copy.wait_send()
     for copy in second:
         copy.start()
-    lax.fori_loop(3, 6, step, 0)
+    run(begin + 3, begin + 6)
     for copy in second:
         copy.wait_recv()
     total = share[0, s]
     for k in range(1, subs):
         total = total + share_land[k - 1]
     share[1, 0] = total
-    text_store = pltpu.make_async_copy(text_full, o_text, store.at[8])
+    text_store = pltpu.make_async_copy(text_full, o_text, store.at[0])
     text_store.start()
     for copy in third:
         copy.start()
-    lax.fori_loop(6, steps, step, 0)
+    relay = max(begin + 6, begin + (at_cq - begin) // 2)
+    run(begin + 6, relay)
+    for each in (scatter_q, scatter_o):
+        each.relay()
+    finish = min(at_cq, relay + 8)
+    run(relay, finish)
+
+    def take_q(rows, value):
+        row = rows.start
+        part = row // (quarter * chunk)
+        c = row // chunk - part * quarter
+        own[at_cq + c, :, pl.ds(pl.multiple_of(part * local, local), local)] = value.astype(BF)
+
+    scatter_q.finish(take_q, chunk)
+    step = min(chunk, scatter_o.half)
+
+    def take_o(rows, value):
+        own[at_co + rows.start // chunk, rows_at(rows.start % chunk // step, step)] = value.astype(BF)
+
+    scatter_o.finish(take_o, step)
+    run(finish, end)
     for copy in third:
         copy.wait_recv()
     total = share[1, 0]
     for k in range(1, groups):
         total = total + share_land[subs - 2 + k]
     share[2, 0] = total
-    vector_store = pltpu.make_async_copy(share.at[2, 0], o_vectors, store.at[9])
+    vector_store = pltpu.make_async_copy(share.at[2, 0], o_vectors, store.at[1])
     vector_store.start()
     for copy in second + third:
         copy.wait_send()
-
-    @pl.when(g < groups - 1)
-    def _():
-        for i in range(4):
-            right(count - 4 + i).wait_send()
-
-    @pl.when(g > 0)
-    def _():
-        for i in range(4):
-            left(count - 4 + i).wait_send()
-
-    for i in range(4):
-        outputs(count - 4 + i, lambda copy: copy.wait())
+    for each in (scatter_q, scatter_o):
+        each.drain()
+    pump.drain()
     text_store.wait()
     vector_store.wait()
 
 
-def total(pieces, qkv, cq, kv, out, co, sums_a, sums_b, text, subs, groups):
-    _, piece, m = pieces.shape
-    rows = 2 * piece + qkv.shape[0] + kv.shape[0] // 2 + out.shape[0] + co.shape[0]
-    chunk = 96 if out.shape[0] % 96 == 0 else 48
-    count = rows // chunk
+def total(layout, pieces, qkv, kv, out, cross_q, cross_o, sums_a, sums_b, text, land, summed, subs, groups):
+    m, chunk = layout.m, layout.chunk
     v = pltpu.VMEM
-    sems = 8 + subs + groups
+    sems = 7 + subs + groups + 12
+    tall = lambda a: a.reshape(-1, chunk, a.shape[1])
+    qkv, kv, out = tall(qkv), tall(kv), tall(out)
+    piece_q, piece_o = cross_q.shape[1:], cross_o.shape[1:]
     return pl.pallas_call(
-        total_kernel,
+        partial(total_kernel, layout),
         name="total",
-        out_shape=[shape(*dims, kind=F32) for dims in (
-            (piece, m), (piece, m), qkv.shape, cq.shape, kv.shape, out.shape, co.shape, text.shape, (8, m // subs),
-        )],
-        in_specs=[ANY] * 9,
-        out_specs=[ANY] * 9,
+        out_shape=[
+            shape(*qkv.shape), shape(layout.piece // chunk, chunk, layout.local), shape(*kv.shape), shape(*out.shape),
+            shape(*out.shape), shape(*text.shape, kind=F32), shape(8, m // subs, kind=F32), shape(*summed.shape),
+        ],
+        in_specs=[ANY] * 11,
+        out_specs=[ANY] * 8,
+        input_output_aliases={10: 7},
         scratch_shapes=[
-            v((rows, m), BF), v((count, chunk, m), BF), v((count, chunk, m), BF), v((4, chunk, m), BF), v((4, chunk, m), BF),
-            v((4, chunk, m), F32), v(sums_a.shape, F32), v(sums_b.shape, F32), v(text.shape, F32),
+            *pump_scratch(layout, layout.count),
+            v(cross_q.shape, BF), v(cross_o.shape, BF),
+            v((6, piece_q[0] // 2, piece_q[1]), BF), v((6, piece_o[0] // 2, piece_o[1]), BF),
+            v((2, piece_q[0] // 2, piece_q[1]), BF), v((2, piece_o[0] // 2, piece_o[1]), BF),
+            v(sums_a.shape, F32), v(sums_b.shape, F32), v(text.shape, F32),
             v((3, text.shape[0] // 4, m), F32), v(text.shape, F32), v((subs, 8, m // subs), F32), v((3, subs, 8, m // subs), F32),
             v((3, subs, 8, m // subs), F32), v((subs - 1 + groups - 1, 8, m // subs), F32),
-            dma(11), dma(10), dma(4), dma(count), dma(4), dma(count), dma(sems), dma(sems),
+            dma(14), dma(2), dma(sems), dma(sems),
         ],
         compiler_params=params(7),
-    )(pieces, qkv, cq, kv, out, co, sums_a, sums_b, text)
+    )(pieces, qkv, kv, out, cross_q, cross_o, sums_a, sums_b, text, land, summed)
 
 
 def local(
@@ -1620,34 +1763,38 @@
     flat, sums, after_self, wq, wo = attend(triple, selfout, frames[0], crossquery, crossout, subs)
     wo = wo.reshape(4 * width, m)
     query, cross_flat, after_cross, feed_rows, grads = cross(after_self, gains, wq, wo, memory, cotangent[0])
-    layer_output, norm_grad, pieces = feed(feed_rows, grads, feedup, feeddown, after_cross, subs)
-    grad_out, branch, sums_a, memory_grad, piece_q, piece_o = cross_back(
-        cotangent[0], norm_grad, after_cross, after_self, gains, query, cross_flat, memory, wq, wo, subs
+    layout = Layout(m, width, subs, groups)
+    part, norm_grad, pieces = feed(feed_rows, grads, feedup, feeddown, subs)
+    pieces = pieces.reshape(-1, layout.chunk, m)
+    grad_out, branch, sums_a, memory_grad, piece_q, piece_o, layer_output, summed, land = cross_back(
+        layout, cotangent[0], norm_grad, after_cross, after_self, gains, query, cross_flat, memory, wq, wo, part, pieces, subs
     )
-    frame_grad, sums_b, text_part, grad_qkv, grad_out_weight, grad_kv, grad_cq, grad_co = attend_back(
-        branch, triple, flat, sums, selfout, qkv, rows, frames[0], self_gains, grad_out, memory_grad, text_states[0], kv,
-        piece_q, piece_o, subs,
+    frame_grad, sums_b, text_part, grad_qkv, grad_out_weight, grad_kv, summed, land = attend_back(
+        layout, branch, triple, flat, sums, selfout, qkv, rows, frames[0], self_gains, grad_out, memory_grad,
+        text_states[0], kv, pieces, land, summed, subs,
     )
-    up, down, full_qkv, full_cq, full_kv, full_out, full_co, text_grad, vectors = total(
-        pieces, grad_qkv, grad_cq, grad_kv, grad_out_weight, grad_co, sums_a, sums_b, text_part, subs, groups
+    full_qkv, full_cq, full_kv, full_out, full_co, text_grad, vectors, summed = total(
+        layout, pieces, grad_qkv, grad_kv, grad_out_weight, piece_q, piece_o, sums_a, sums_b, text_part, land, summed,
+        subs, groups,
     )
+    down, up = summed.reshape(2, -1, m)
     return (
         layer_output[None],
         frame_grad[None],
         text_grad[None],
         vectors[4],
         vectors[5],
-        full_qkv.reshape(-1, 3, width),
-        full_out,
+        full_qkv.astype(F32).reshape(-1, 3, width),
+        full_out.astype(F32).reshape(-1, m),
         vectors[2],
         vectors[3],
-        full_cq,
-        full_kv.reshape(-1, 2, width),
-        full_co,
+        full_cq.astype(F32).reshape(-1, width),
+        full_kv.astype(F32).reshape(-1, 2, width),
+        full_co.astype(F32).reshape(-1, m),
         vectors[0],
         vectors[1],
-        up,
-        down,
+        up.astype(F32),
+        down.astype(F32),
     )
 
 

time: 641 us -> 537 us (0.84)
  Pallas kernels: 595 us -> 492 us
  local copies, waits for them, and re-layouts: 42.9 us -> 32.1 us
  other arithmetic: 1.25 us -> 10.6 us
    pallas_call x4, Pallas kernels: 461 us -> 358 us  [the longest x1 143 us: total(): pl.pallas_call(partial(total_kernel, layout), name='total', out_shape=[sh...]
    unnamed x29 -> x28, local copies, waits for them, and re-layouts: 26.3 us -> 16.4 us
where the time goes in v2:
time: 537 us; the launch traced here: 536 us
  Pallas kernels  492 us (92%)
  local copies, waits for them, and re-layouts  32.1 us (6%)
  other arithmetic  10.6 us (2%)
    pallas_call x1, Pallas kernels, total(): pl.pallas_call(partial(total_kernel, layout), name='total', out_shape=[sh...  143 us
    pallas_call x1, Pallas kernels, attend_back(): pl.pallas_call(partial(attend_back_kernel, layout), name='attend_back', o...  103 us
    pallas_call x1, Pallas kernels, attend(): pl.pallas_call(attend_kernel, name='attend', out_shape=[shape(4, n, local...  68.3 us
    pallas_call x1, Pallas kernels, feed(): pl.pallas_call(feed_kernel, name='feed', out_shape=[shape(4, n, m), shape...  65.1 us
    pallas_call x1, Pallas kernels, cross_back(): pl.pallas_call(partial(cross_back_kernel, layout), name='cross_back', out...  47.6 us
    pallas_call x1, Pallas kernels, enter(): pl.pallas_call(enter_kernel, name='enter', out_shape=[shape(4, n, m), sha...  36.8 us
    pallas_call x1, Pallas kernels, cross(): pl.pallas_call(cross_kernel, name='cross', out_shape=[shape(n, m), shape(...  29.2 us
    unnamed x28, local copies, waits for them, and re-layouts  16.4 us

profile of v2, /device:TPU:0, one launch (start us, length us, event | category | flops | bytes accessed | tf_op | source)
XLA Modules:
  0.0 536.0 jit_solution(12776597840814152245)
XLA Ops:
  0.6 0.7 stack.24.gain
  1.4 0.7 stack.25.bias
  2.1 0.7 stack.26
  2.8 0.7 stack.27
  3.5 0.7 stack.28
  4.2 0.7 stack.29
  4.9 0.6 pad_maximum_fusion.gains_in
  5.5 0.6 pad_maximum_fusion.1.gains_in
  6.1 3.5 copy.40
  9.7 4.3 copy.36
  13.9 3.7 copy.37.qkv.qkv_in
  17.6 36.8 %enter.1 = (bf16[4,256,1536]{2,1,0:T(8,128)(2,1)}, bf16[4,256,1152]{2,1,0:T(8,128)(2,1)}, bf16[4,64,768]{2,1,0:T(8,128)(2,1)}) custom-call(bf16[256,1536]{1,0:T(8,128)(2,1)} %bitcast.39, f32[1,1536]{1,0:T(1,128)} %copy-done.7, f32[1,1536]{1,0:T(1,128)} %copy-done.8, bf16[1536,1152]{1,0:T(8,128)(2,1)} %copy.37.qkv.qkv_in, bf16[64,1536]{1,0:T(8,128)(2,1)} %bitcast.49, ...), custom_call_target="tpu_custom_call" | custom-call | tf_op jit(solution)/shard_map/enter/pallas_call | solution.py:442
  54.4 68.3 %attend.1 = (bf16[4,256,384]{2,1,0:T(8,128)(2,1)}, f32[4,256,128]{2,1,0:T(8,128)}, f32[256,1536]{1,0:T(8,128)}, bf16[4,1536,384]{2,1,0:T(8,128)(2,1)}, bf16[4,384,1536]{2,1,0:T(8,128)(2,1)}) custom-call(bf16[4,256,1152]{2,1,0:T(8,128)(2,1)} %get-tuple-element.57.triple_in, bf16[384,1536]{1,0:T(8,128)(2,1)} %out_in.3, bf16[256,1536]{1,0:T(8,128)(2,1)} %bitcast.40, ...), custom_call_target="tpu_custom_call" | custom-call | tf_op jit(solution)/shard_map/attend/pallas_call | solution.py:619
  122.7 29.2 %cross.1 = (bf16[256,1536]{1,0:T(8,128)(2,1)}, bf16[256,1536]{1,0:T(8,128)(2,1)}, f32[256,1536]{1,0:T(8,128)}, bf16[256,1536]{1,0:T(8,128)(2,1)}, bf16[4,256,1536]{2,1,0:T(8,128)(2,1)}) custom-call(f32[256,1536]{1,0:T(8,128)} %get-tuple-element.58.after_in.self_in, f32[4,1536]{1,0:T(4,128)} %pad_maximum_fusion.gains_in, ...), custom_call_target="tpu_custom_call" | custom-call | tf_op jit(solution)/shard_map/cross/pallas_call | solution.py:752
  151.9 65.1 %feed.1 = (bf16[4,256,1536]{2,1,0:T(8,128)(2,1)}, bf16[256,1536]{1,0:T(8,128)(2,1)}, bf16[2,768,1536]{2,1,0:T(8,128)(2,1)}) custom-call(bf16[256,1536]{1,0:T(8,128)(2,1)} %get-tuple-element.62.rows_in, bf16[4,256,1536]{2,1,0:T(8,128)(2,1)} %get-tuple-element.63.grads_in, bf16[1536,1536]{1,0:T(8,128)(2,1)} %up_in.1, bf16[1536,1536]{1,0:T(8,128)(2,1)} %down_in.1), custom_call_target="tpu_custom_call" | custom-call | tf_op jit(solution)/shard_map/feed/pallas_call | solution.py:972
  217.1 47.6 %cross_back.1 = (f32[256,1536]{1,0:T(8,128)}, bf16[256,1536]{1,0:T(8,128)(2,1)}, f32[32,1536]{1,0:T(8,128)}, bf16[4,64,768]{2,1,0:T(8,128)(2,1)}, bf16[4,768,384...) custom-call(f32[256,1536]{1,0:T(8,128)} %bitcast.43, ...), custom_call_target="tpu_custom_call" | custom-call | tf_op jit(solution)/shard_map/cross_back/pallas_call | solution.py:1200
  264.7 102.8 %attend_back.1 = (f32[256,1536]{1,0:T(8,128)}, f32[16,1536]{1,0:T(8,128)}, f32[64,1536]{1,0:T(8,128)}, bf16[768,1152]{1,0:T(8,128)(2,1)}, bf16[192,1536]{1,0:T(8...) custom-call(bf16[256,1536]{1,0:T(8,128)(2,1)} %get-tuple-element.71., ...), custom_call_target="tpu_custom_call", output_to_operand_aliasing={{6}: (15, {})} | custom-call | tf_op jit(solution)/shard_map/attend_back/pallas_call | solution.py:1495
  367.5 142.5 %total.1 = (bf16[16,48,1152]{2,1,0:T(8,128)(2,1)}, bf16[16,48,384]{2,1,0:T(8,128)(2,1)}, bf16[16,48,768]{2,1,0:T(8,128)(2,1)}, bf16[4,48,1536]{2,1,0:T(8,128)(2,...) custom-call(bf16[32,48,1536]{2,1,0:T(8,128)(2,1)} %bitcast.31, ...), custom_call_target="tpu_custom_call", output_to_operand_aliasing={{7}: (10, {})} | custom-call | tf_op jit(solution)/shard_map/total/pallas_call | solution.py:1727
  510.1 1.7 slice_reduce_fusion
  511.8 2.2 bitcast_convert_fusion.3
  514.1 2.3 reshape.116
  516.4 1.8 bitcast_convert_fusion.2
  518.2 0.1 copy-done
  518.2 3.6 reshape.110
  521.8 4.5 copy.39
  526.3 0.3 fusion
  526.6 5.4 %bitcast_convert_fusion = (f32[768,1536]{1,0:T(8,128)}, f32[768,1536]{1,0:T(8,128)}) fusion(bf16[16,48,1536]{2,1,0:T(8,128)(2,1)S(1)} %get-tuple-element.136, bf16[16,48,1536]{2,1,0:T(8,128)(2,1)S(1)} %get-tuple-element.137), kind=kLoop, calls=%fused_computation | loop fusion | flops 2359296 | bytes 14155776 | tf_op jit(solution)/shard_map/convert_element_type | solution.py:1797
  532.0 1.1 copy.46
  533.1 0.8 copy-done.2
  534.0 1.1 copy.47
  535.1 0.1 copy-done.6
  535.2 0.7 copy.48
  (20 shorter events, 0.0 us)
Async XLA Ops:
  1.3 8.3 %copy-start.7 = (f32[1,1536]{1,0:T(1,128)}, f32[1,1536]{1,0:T(1,128)S(1)}, u32[]{:S(2)}) copy-start(f32[1,1536]{1,0:T(1,128)S(1)} %stack.24.gain) | copy-start | bytes 18436
  2.1 7.6 %copy-start.8 = (f32[1,1536]{1,0:T(1,128)}, f32[1,1536]{1,0:T(1,128)S(1)}, u32[]{:S(2)}) copy-start(f32[1,1536]{1,0:T(1,128)S(1)} %stack.25.bias) | copy-start | bytes 18436
  510.1 4.0 copy-start.3
  511.8 4.5 copy-start.4
  511.8 4.5 copy-start.5
  516.4 1.8 copy-start
  518.2 8.1 %slice-start = ((s8[4718592]{0:T(1024)(128)(4,1)}), s8[524288]{0:T(1024)(128)(4,1)S(1)}, s32[]{:S(2)}) async-start(s8[4718592]{0:T(1024)(128)(4,1)} %bitcast.32), calls=%async_computation | async-start | bytes 1048576
  521.8 4.5 slice-start.1
  526.6 5.4 %copy-start.1 = (f32[256,1536]{1,0:T(8,128)S(1)}, f32[256,1536]{1,0:T(8,128)}, u32[]{:S(2)}) copy-start(f32[256,1536]{1,0:T(8,128)} %get-tuple-element.70) | copy-start | bytes 4718596
  532.0 2.0 copy-start.2
  534.0 1.2 copy-start.6

commit v3 on v2

--- a/solution.py
+++ b/solution.py
@@ -330,9 +330,14 @@
         self.end = self.count + LAG * (groups - 1)
 
 
-def feed_outputs(layout, o_feed):
+def feed_outputs(layout, *halves):
     def outputs(c, block, store, act):
-        act(pltpu.make_async_copy(block, o_feed.at[c], store.at[c % RING, 0]))
+        count = layout.feed_count // 2
+        for i, half in enumerate(halves):
+
+            @pl.when(either(c >= i * count, c < (i + 1) * count))
+            def _(i=i, half=half):
+                act(pltpu.make_async_copy(block, half.at[c - i * count], store.at[c % RING, 0]))
 
     return outputs
 
@@ -356,20 +361,23 @@
 
 
 def enter_kernel(
-    frames, gain, bias, qkv, text, kv, o_rows, o_triple, o_memory,
-    v_frames, v_gain, v_bias, v_qkv, v_text, v_kv, rows, triple, memory, load, store, send, recv,
+    frames, gains, qkv, text, kv, o_rows, o_triple, o_memory,
+    v_frames, v_gains, v_qkv, v_text, v_kv, rows, triple, memory, load, store, send, recv,
 ):
     t, x, y, d = neighbours()
     loads = [
         pltpu.make_async_copy(a, b, load.at[i])
         for i, (a, b) in enumerate(
-            ((frames, v_frames), (gain, v_gain), (bias, v_bias), (qkv, v_qkv), (text, v_text), (kv, v_kv))
+            (
+                (frames, v_frames), (gains, v_gains), (text, v_text), (kv, v_kv),
+                *((qkv.at[i], v_qkv.at[:, pl.ds(i * qkv.shape[2], qkv.shape[2])]) for i in range(3)),
+            )
         )
     ]
     for copy in loads:
         copy.start()
     greet([{"tensor": x}, {"tensor": y}])
-    for copy in loads[:3]:
+    for copy in loads[:2]:
         copy.wait()
     count, width = v_qkv.shape
     block = 384
@@ -377,7 +385,7 @@
     def norm_block(i, carry):
         here = rows_at(i, 64)
         hat, _ = normed_rows(v_frames[here].astype(F32))
-        rows[t, here] = (hat * v_gain[...] + v_bias[...]).astype(BF)
+        rows[t, here] = (hat * v_gains[4:5] + v_gains[5:6]).astype(BF)
         return carry
 
     lax.fori_loop(0, v_frames.shape[0] // 64, norm_block, 0)
@@ -399,8 +407,8 @@
         b.start()
         return [a, b]
 
-    loads[4].wait()
-    loads[5].wait()
+    loads[2].wait()
+    loads[3].wait()
 
     def texts_step(j, carry):
         memory[t, :, cols(j, block)] = dot(v_text[...], v_kv[:, cols(j, block)]).astype(BF)
@@ -408,7 +416,8 @@
 
     lax.fori_loop(0, v_kv.shape[1] // block, texts_step, 0)
     texts.start()
-    loads[3].wait()
+    for copy in loads[4:]:
+        copy.wait()
     project(t)
     stores = put(0, t)
     gather.relay_x()
@@ -436,23 +445,23 @@
     last.wait()
 
 
-def enter(frames, gain, bias, qkv, text, kv):
+def enter(frames, gains, qkv, text, kv):
     n, m = frames.shape
-    width, texts, kvw = qkv.shape[1], text.shape[0], kv.shape[1]
+    width, texts, kvw = 3 * qkv.shape[2], text.shape[0], kv.shape[1]
     return pl.pallas_call(
         enter_kernel,
         name="enter",
         out_shape=[shape(4, n, m), shape(4, n, width), shape(4, texts, kvw)],
-        in_specs=[ANY] * 6,
+        in_specs=[ANY] * 5,
         out_specs=[ANY] * 3,
         scratch_shapes=[
-            pltpu.VMEM((n, m), frames.dtype), pltpu.VMEM((1, m), F32), pltpu.VMEM((1, m), F32),
-            pltpu.VMEM(qkv.shape, BF), pltpu.VMEM(text.shape, BF), pltpu.VMEM(kv.shape, BF),
+            pltpu.VMEM((n, m), frames.dtype), pltpu.VMEM(gains.shape, F32),
+            pltpu.VMEM((m, width), BF), pltpu.VMEM(text.shape, BF), pltpu.VMEM(kv.shape, BF),
             pltpu.VMEM((4, n, m), BF), pltpu.VMEM((4, n, width), BF), pltpu.VMEM((4, texts, kvw), BF),
-            dma(6), dma(9), dma(12), dma(12),
+            dma(7), dma(9), dma(12), dma(12),
         ],
         compiler_params=params(1),
-    )(frames, gain, bias, qkv, text, kv)
+    )(frames, gains, qkv, text, kv)
 
 
 def head_lanes(rows):
@@ -1009,7 +1018,7 @@
 def cross_back_kernel(
     layout,
     cot_in, norm_in, cross_in, self_in, gains_in, query_in, flat_in, memory_in, wq_in, wo_in, part_in, own_in,
-    o_out, o_branch, o_sums, o_memory, o_wq, o_wo, o_layer, o_feed, o_land,
+    o_out, o_branch, o_sums, o_memory, o_wq, o_wo, o_layer, o_down, o_land,
     cot, norm, after_cross, after_self, gains, query, flat, memory, wq, wo,
     branch, rows, query_grad, memory_grad, sums, whole_q, whole_o, land_q, land_o, piece_q, piece_o,
     norm_self, part, land_part, stage_part, own, land, ring, result, ring_send, ring_recv, ring_store,
@@ -1034,7 +1043,7 @@
     scatter = Scatter(part, land_part, stage_part, send, recv, 8 * (subs - 1))
     pump = Pump(
         own, land, ring, result, ring_send, ring_recv, ring_store, 0, layout.middle, layout.count,
-        feed_outputs(layout, o_feed),
+        feed_outputs(layout, o_down),
     )
     n, m = cot.shape
     width = wq.shape[2]
@@ -1202,7 +1211,7 @@
         name="cross_back",
         out_shape=[
             shape(n, m, kind=F32), shape(n, m), shape(32, m, kind=F32), shape(*memory.shape), shape(*part_q), shape(*part_o),
-            shape(n, m, kind=F32), shape(layout.feed_count, layout.chunk, m), shape(*held),
+            shape(n, m, kind=F32), shape(layout.feed_count // 2, layout.chunk, m), shape(*held),
         ],
         in_specs=[ANY] * 12,
         out_specs=[ANY] * 9,
@@ -1260,8 +1269,8 @@
 def attend_back_kernel(
     layout,
     branch_in, triple_in, flat_in, sums_in, out_in, qkv_in, rows_in, frames_in, gains_in, grad_in, memory_in, text_in, kv_in,
-    own_in, land_in, feed_in,
-    o_frames, o_sums, o_text, o_qkv, o_out, o_kv, o_feed, o_land,
+    own_in, land_in, down_in,
+    o_frames, o_sums, o_text, o_qkv, o_out, o_kv, o_down, o_up, o_land,
     branch, triple, flat, sums, out, qkv, rows, frames, gains, grad_out, memory, text, kv,
     land_m, stage_m,
     grad_heads, deltas, grads, grad_keys, grad_values, part, land, stage, whole_qkv, land_qkv, whole_out, land_out,
@@ -1273,7 +1282,8 @@
     subs = lax.axis_size("sub")
     names = (
         (branch_in, branch.at[t]), (out_in, out), (flat_in, flat), (triple_in, triple), (sums_in, sums),
-        (memory_in, memory), (own_in, own), (land_in, held), (qkv_in, qkv), (rows_in, rows),
+        (memory_in, memory), (own_in, own), (land_in, held),
+        *((qkv_in.at[i], qkv.at[:, pl.ds(i * qkv_in.shape[2], qkv_in.shape[2])]) for i in range(3)), (rows_in, rows),
         (text_in, text), (kv_in, kv), (frames_in, frames), (gains_in, gains), (grad_in, grad_out),
     )
     loads = [pltpu.make_async_copy(a, b, load.at[i]) for i, (a, b) in enumerate(names)]
@@ -1285,7 +1295,7 @@
     first, last = layout.middle, layout.later
     pump = Pump(
         own, held, ring, result, ring_send, ring_recv, ring_store, first, last, layout.count,
-        feed_outputs(layout, o_feed),
+        feed_outputs(layout, o_down, o_up),
     )
 
     def tick(k):
@@ -1362,7 +1372,7 @@
         return carry
 
     lax.fori_loop(0, 4, turn, 0)
-    for copy in loads[8:12]:
+    for copy in loads[8:14]:
         copy.wait()
 
     def finish_grads(i, carry):
@@ -1449,7 +1459,7 @@
         each.total(0, take, 16)
         stores.append(pltpu.make_async_copy(each.land.at[0, 0], output, store.at[slot]))
         stores[-1].start()
-    for copy in loads[12:]:
+    for copy in loads[14:]:
         copy.wait()
 
     def take_norm(here, total):
@@ -1460,7 +1470,7 @@
     def frame_block(i, carry):
         here = rows_at(i, 64)
         grad = part[t, here].astype(F32)
-        inner, terms = norm_back_block(grad, frames[here].astype(F32), gains[0:1])
+        inner, terms = norm_back_block(grad, frames[here].astype(F32), gains[4:5])
         grad_out[here] = grad_out[here] + inner
         return carry[0] + fold(terms), carry[1] + fold(grad)
 
@@ -1484,7 +1494,7 @@
 
 
 def attend_back(
-    layout, branch, triple, flat, sums, out, qkv, rows, frames, gains, grad, memory, text, kv, own, land, feed_sums, subs
+    layout, branch, triple, flat, sums, out, qkv, rows, frames, gains, grad, memory, text, kv, own, land, down, subs
 ):
     n, m = grad.shape
     width = triple.shape[2]
@@ -1497,13 +1507,13 @@
         name="attend_back",
         out_shape=[
             shape(n, m, kind=F32), shape(16, m, kind=F32), shape(texts, m, kind=F32), shape(m // subs, width),
-            shape(local // subs, m), shape(m // subs, kvw), shape(*feed_sums.shape), shape(*land.shape),
+            shape(local // subs, m), shape(m // subs, kvw), shape(*down.shape), shape(*down.shape), shape(*land.shape),
         ],
         in_specs=[ANY] * 16,
-        out_specs=[ANY] * 8,
+        out_specs=[ANY] * 9,
         input_output_aliases={15: 6},
         scratch_shapes=[
-            v((4, n, m), BF), v(triple.shape, BF), v(flat.shape, BF), v(sums.shape, F32), v(out.shape, BF), v(qkv.shape, BF),
+            v((4, n, m), BF), v(triple.shape, BF), v(flat.shape, BF), v(sums.shape, F32), v(out.shape, BF), v((m, width), BF),
             v(rows.shape, BF), v(frames.shape, frames.dtype), v(gains.shape, F32), v((n, m), F32), v(memory.shape, BF),
             v(text.shape, BF), v(kv.shape, BF),
             v((6, texts // 2, kvw), BF), v((2, texts // 2, kvw), BF),
@@ -1514,16 +1524,16 @@
             v((1, m, kvw), BF), v((1, subs - 1, m // subs, kvw), BF),
             v((texts, m), F32), v((16, m), F32), v((texts, kvw), BF),
             *pump_scratch(layout, layout.feed_count),
-            dma(15), dma(7), dma(count), dma(count),
+            dma(17), dma(7), dma(count), dma(count),
         ],
         compiler_params=params(6),
-    )(branch, triple, flat, sums, out, qkv, rows, frames, gains, grad, memory, text, kv, own, land, feed_sums)
+    )(branch, triple, flat, sums, out, qkv, rows, frames, gains, grad, memory, text, kv, own, land, down)
 
 
 def total_kernel(
     layout,
-    feed_in, qkv_in, kv_in, out_in, cross_q_in, cross_o_in, sums_a_in, sums_b_in, text_in, land_in, summed_in,
-    o_qkv, o_cq, o_kv, o_out, o_co, o_text, o_vectors, o_feed,
+    feed_in, qkv_in, kv_in, out_in, cross_q_in, cross_o_in, sums_a_in, sums_b_in, text_in, land_in, down_in, up_in,
+    o_qkv, o_cq, o_kv, o_out, o_co, o_text, o_vectors, o_down, o_up,
     own, held, ring, result, ring_send, ring_recv, ring_store,
     cross_q, cross_o, land_q, land_o, stage_q, stage_o,
     sums_a, sums_b, text, text_land, text_full, vectors, vectors_land, share, share_land, load, store, send, recv,
@@ -1537,9 +1547,44 @@
         r // chunk for r in (layout.qkv, layout.kv, layout.out, layout.cq, layout.co)
     )
     outs = layout.out_rows // chunk
+    def outputs(c, block, slots, act):
+        slot = c % RING
+
+        def region(begin, end, copies):
+            @pl.when(jnp.logical_and(c >= begin, c < end))
+            def _():
+                for i, (source, target) in enumerate(copies(c - begin)):
+                    act(pltpu.make_async_copy(source, target, slots.at[slot, i]))
+
+        def whole(output):
+            return lambda r: [(block, output.at[r])]
+
+        region(0, at_qkv // 2, whole(o_down))
+        region(at_qkv // 2, at_qkv, whole(o_up))
+        region(
+            at_qkv, at_kv,
+            lambda r: [
+                *((block.at[:, pl.ds(i * local, local)], o_qkv.at[i, r]) for i in range(3)),
+                (block.at[:, pl.ds(width, local)], o_qkv.at[r // quarter, 3 * quarter + r % quarter]),
+            ],
+        )
+        region(
+            at_kv, at_out,
+            lambda r: [
+                (block.at[:, pl.ds(2 * i * local, 2 * local)], o_kv.at[2 * i * quarter + r]) for i in range(2)
+            ],
+        )
+        region(at_out, at_cq, whole(o_out))
+        region(
+            at_cq, at_co,
+            lambda r: [(block.at[:, pl.ds(i * local, local)], o_cq.at[i * quarter + r]) for i in range(4)],
+        )
+        region(at_co, at_co + outs, whole(o_co))
+
+    fresh = max(0, layout.later - LAG * (groups - 1))
     pairs = [
         (land_in, held),
-        (feed_in, own.at[pl.ds(0, at_qkv)]),
+        (feed_in.at[pl.ds(fresh, at_qkv - fresh)], own.at[pl.ds(fresh, at_qkv - fresh)]),
         (qkv_in.at[pl.ds(0, 3 * quarter)], own.at[pl.ds(at_qkv, 3 * quarter), :, pl.ds(0, width)]),
     ]
     for i in range(3):
@@ -1549,6 +1594,7 @@
                 own.at[pl.ds(at_qkv + i * quarter, quarter), :, pl.ds(width, local)],
             )
         )
+    pairs += [(sums_a_in, sums_a), (sums_b_in, sums_b), (text_in, text), (cross_q_in, cross_q), (cross_o_in, cross_o)]
     for i in range(2):
         pairs.append(
             (
@@ -1556,10 +1602,7 @@
                 own.at[pl.ds(at_kv, 2 * quarter), :, pl.ds(2 * i * local, 2 * local)],
             )
         )
-    pairs += [
-        (out_in, own.at[pl.ds(at_out, outs)]),
-        (sums_a_in, sums_a), (sums_b_in, sums_b), (text_in, text), (cross_q_in, cross_q), (cross_o_in, cross_o),
-    ]
+    pairs.append((out_in, own.at[pl.ds(at_out, outs)]))
     loads = [pltpu.make_async_copy(a, b, load.at[i]) for i, (a, b) in enumerate(pairs)]
     for copy in loads:
         copy.start()
@@ -1569,7 +1612,21 @@
         + [{"sub": (s + k) % subs} for k in range(1, subs)]
         + [{"group": (g + k) % groups} for k in range(1, groups)]
     )
-    for copy in loads[1:]:
+    begin, end = layout.later, layout.end
+    loads[1].wait()
+    pump = Pump(own, held, ring, result, ring_send, ring_recv, ring_store, begin, end, layout.count, outputs)
+
+    def run(a, b):
+        def step(k, carry):
+            pump.step(k)
+            return carry
+
+        lax.fori_loop(a, b, step, 0)
+
+    for copy in loads[2:6]:
+        copy.wait()
+    run(begin, begin + 1)
+    for copy in loads[6:]:
         copy.wait()
     share_width = m // subs
     for i in range(6):
@@ -1612,53 +1669,7 @@
         each.along_x()
         each.along_y()
 
-    def outputs(c, block, slots, act):
-        slot = c % RING
-
-        def region(begin, end, copies):
-            @pl.when(jnp.logical_and(c >= begin, c < end))
-            def _():
-                for i, (source, target) in enumerate(copies(c - begin)):
-                    act(pltpu.make_async_copy(source, target, slots.at[slot, i]))
-
-        def whole(output):
-            return lambda r: [(block, output.at[r])]
-
-        region(layout.later - LAG * (groups - 1), at_qkv, lambda r: [(block, o_feed.at[c])])
-        region(
-            at_qkv, at_kv,
-            lambda r: [
-                (block.at[:, pl.ds(0, width)], o_qkv.at[r]),
-                (
-                    block.at[:, pl.ds(width, local)],
-                    o_qkv.at[3 * quarter + r % quarter, :, pl.ds(pl.multiple_of(r // quarter * local, local), local)],
-                ),
-            ],
-        )
-        region(
-            at_kv, at_out,
-            lambda r: [
-                (block.at[:, pl.ds(2 * i * local, 2 * local)], o_kv.at[2 * i * quarter + r]) for i in range(2)
-            ],
-        )
-        region(at_out, at_cq, whole(o_out))
-        region(
-            at_cq, at_co,
-            lambda r: [(block.at[:, pl.ds(i * local, local)], o_cq.at[i * quarter + r]) for i in range(4)],
-        )
-        region(at_co, at_co + outs, whole(o_co))
-
-    begin, end = layout.later, layout.end
-    pump = Pump(own, held, ring, result, ring_send, ring_recv, ring_store, begin, end, layout.count, outputs)
-
-    def run(a, b):
-        def step(k, carry):
-            pump.step(k)
-            return carry
-
-        lax.fori_loop(a, b, step, 0)
-
-    run(begin, begin + 3)
+    run(begin + 1, begin + 3)
     for copy in first:
         copy.wait_recv()
     for j in range(subs):
@@ -1717,7 +1728,7 @@
     vector_store.wait()
 
 
-def total(layout, pieces, qkv, kv, out, cross_q, cross_o, sums_a, sums_b, text, land, summed, subs, groups):
+def total(layout, pieces, qkv, kv, out, cross_q, cross_o, sums_a, sums_b, text, land, down, up, subs, groups):
     m, chunk = layout.m, layout.chunk
     v = pltpu.VMEM
     sems = 7 + subs + groups + 12
@@ -1728,12 +1739,12 @@
         partial(total_kernel, layout),
         name="total",
         out_shape=[
-            shape(*qkv.shape), shape(layout.piece // chunk, chunk, layout.local), shape(*kv.shape), shape(*out.shape),
-            shape(*out.shape), shape(*text.shape, kind=F32), shape(8, m // subs, kind=F32), shape(*summed.shape),
+            shape(3, *qkv.shape[:2], layout.local), shape(layout.piece // chunk, chunk, layout.local), shape(*kv.shape), shape(*out.shape),
+            shape(*out.shape), shape(*text.shape, kind=F32), shape(8, m // subs, kind=F32), shape(*down.shape), shape(*up.shape),
         ],
-        in_specs=[ANY] * 11,
-        out_specs=[ANY] * 8,
-        input_output_aliases={10: 7},
+        in_specs=[ANY] * 12,
+        out_specs=[ANY] * 9,
+        input_output_aliases={10: 7, 11: 8},
         scratch_shapes=[
             *pump_scratch(layout, layout.count),
             v(cross_q.shape, BF), v(cross_o.shape, BF),
@@ -1745,7 +1756,7 @@
             dma(14), dma(2), dma(sems), dma(sems),
         ],
         compiler_params=params(7),
-    )(pieces, qkv, kv, out, cross_q, cross_o, sums_a, sums_b, text, land, summed)
+    )(pieces, qkv, kv, out, cross_q, cross_o, sums_a, sums_b, text, land, down, up)
 
 
 def local(
@@ -1755,36 +1766,34 @@
     subs, groups = lax.axis_size("sub"), lax.axis_size("group")
     m = frames.shape[2]
     width = selfout.shape[0]
-    qkv = selfqkv.reshape(m, 3 * width)
+    qkv = selfqkv.transpose(1, 0, 2)
     kv = crosskv.reshape(m, 2 * width)
-    self_gains = jnp.stack([selfgain, selfbias])
-    gains = jnp.stack([crossgain, crossbias, feedgain, feedbias])
-    rows, triple, memory = enter(frames[0], self_gains[0:1], self_gains[1:2], qkv, text_states[0], kv)
+    gains = jnp.concatenate([crossgain, crossbias, feedgain, feedbias, selfgain, selfbias]).reshape(6, m)
+    rows, triple, memory = enter(frames[0], gains, qkv, text_states[0], kv)
     flat, sums, after_self, wq, wo = attend(triple, selfout, frames[0], crossquery, crossout, subs)
     wo = wo.reshape(4 * width, m)
     query, cross_flat, after_cross, feed_rows, grads = cross(after_self, gains, wq, wo, memory, cotangent[0])
     layout = Layout(m, width, subs, groups)
     part, norm_grad, pieces = feed(feed_rows, grads, feedup, feeddown, subs)
     pieces = pieces.reshape(-1, layout.chunk, m)
-    grad_out, branch, sums_a, memory_grad, piece_q, piece_o, layer_output, summed, land = cross_back(
+    grad_out, branch, sums_a, memory_grad, piece_q, piece_o, layer_output, down, land = cross_back(
         layout, cotangent[0], norm_grad, after_cross, after_self, gains, query, cross_flat, memory, wq, wo, part, pieces, subs
     )
-    frame_grad, sums_b, text_part, grad_qkv, grad_out_weight, grad_kv, summed, land = attend_back(
-        layout, branch, triple, flat, sums, selfout, qkv, rows, frames[0], self_gains, grad_out, memory_grad,
-        text_states[0], kv, pieces, land, summed, subs,
+    frame_grad, sums_b, text_part, grad_qkv, grad_out_weight, grad_kv, down, up, land = attend_back(
+        layout, branch, triple, flat, sums, selfout, qkv, rows, frames[0], gains, grad_out, memory_grad,
+        text_states[0], kv, pieces, land, down, subs,
     )
-    full_qkv, full_cq, full_kv, full_out, full_co, text_grad, vectors, summed = total(
-        layout, pieces, grad_qkv, grad_kv, grad_out_weight, piece_q, piece_o, sums_a, sums_b, text_part, land, summed,
+    full_qkv, full_cq, full_kv, full_out, full_co, text_grad, vectors, down, up = total(
+        layout, pieces, grad_qkv, grad_kv, grad_out_weight, piece_q, piece_o, sums_a, sums_b, text_part, land, down, up,
         subs, groups,
     )
-    down, up = summed.reshape(2, -1, m)
     return (
         layer_output[None],
         frame_grad[None],
         text_grad[None],
         vectors[4],
         vectors[5],
-        full_qkv.astype(F32).reshape(-1, 3, width),
+        full_qkv.astype(F32).reshape(3, -1, width).transpose(1, 0, 2),
         full_out.astype(F32).reshape(-1, m),
         vectors[2],
         vectors[3],
@@ -1793,8 +1802,8 @@
         full_co.astype(F32).reshape(-1, m),
         vectors[0],
         vectors[1],
-        up.astype(F32),
-        down.astype(F32),
+        up.astype(F32).reshape(-1, m),
+        down.astype(F32).reshape(-1, m),
     )
 
 

time: 537 us -> 522 us (0.972)
  local copies, waits for them, and re-layouts: 32.1 us -> 17.8 us
    reshape x2 -> x1, local copies, waits for them, and re-layouts: 7.23 us -> 0.63 us  [local(): jnp.concatenate([crossgain, crossbias, feedgain, feedbias, selfgain, self...]
    convert_element_type x1 -> x0, other arithmetic: 5.37 us -> none  [local(): down.astype(F32)]
    reshape x0 -> x1, other arithmetic: none -> 5.37 us  [local(): down.astype(F32).reshape(-1, m)]
    unnamed x28 -> x27, local copies, waits for them, and re-layouts: 16.4 us -> 12.5 us
where the time goes in v3:
time: 522 us; the launch traced here: 521 us
  Pallas kernels  491 us (94%)
  local copies, waits for them, and re-layouts  17.8 us (3%)
  other arithmetic  11.6 us (2%)
    pallas_call x1, Pallas kernels, total(): pl.pallas_call(partial(total_kernel, layout), name='total', out_shape=[sh...  141 us
    pallas_call x1, Pallas kernels, attend_back(): pl.pallas_call(partial(attend_back_kernel, layout), name='attend_back', o...  103 us
    pallas_call x1, Pallas kernels, attend(): pl.pallas_call(attend_kernel, name='attend', out_shape=[shape(4, n, local...  68.3 us
    pallas_call x1, Pallas kernels, feed(): pl.pallas_call(feed_kernel, name='feed', out_shape=[shape(4, n, m), shape...  65.1 us
    pallas_call x1, Pallas kernels, cross_back(): pl.pallas_call(partial(cross_back_kernel, layout), name='cross_back', out...  47 us
    pallas_call x1, Pallas kernels, enter(): pl.pallas_call(enter_kernel, name='enter', out_shape=[shape(4, n, m), sha...  36.9 us
    pallas_call x1, Pallas kernels, cross(): pl.pallas_call(cross_kernel, name='cross', out_shape=[shape(n, m), shape(...  29.3 us
    unnamed x27, local copies, waits for them, and re-layouts  12.5 us

profile of v3, /device:TPU:0, one launch (start us, length us, event | category | flops | bytes accessed | tf_op | source)
XLA Modules:
  0.0 521.2 jit_solution(4553556443669800466)
XLA Ops:
  0.7 0.7 constant_dynamic-update-slice_fusion.5
  1.4 0.7 constant_dynamic-update-slice_fusion.4
  2.1 0.7 constant_dynamic-update-slice_fusion.3
  2.8 0.7 constant_dynamic-update-slice_fusion.2
  3.5 0.7 constant_dynamic-update-slice_fusion.1
  4.2 0.7 constant_dynamic-update-slice_fusion
  4.9 0.6 reshape.93.gains.gains_in
  5.5 3.5 copy.35
  9.0 36.9 %enter.1 = (bf16[4,256,1536]{2,1,0:T(8,128)(2,1)}, bf16[4,256,1152]{2,1,0:T(8,128)(2,1)}, bf16[4,64,768]{2,1,0:T(8,128)(2,1)}) custom-call(bf16[256,1536]{1,0:T(8,128)(2,1)} %bitcast.43, f32[6,1536]{1,0:T(8,128)} %reshape.93.gains.gains_in, bf16[3,1536,384]{2,1,0:T(8,128)(2,1)} %bitcast.41, bf16[64,1536]{1,0:T(8,128)(2,1)} %bitcast.53, ...), custom_call_target="tpu_custom_call" | custom-call | tf_op jit(solution)/shard_map/enter/pallas_call | solution.py:451
  45.9 68.3 %attend.1 = (bf16[4,256,384]{2,1,0:T(8,128)(2,1)}, f32[4,256,128]{2,1,0:T(8,128)}, f32[256,1536]{1,0:T(8,128)}, bf16[4,1536,384]{2,1,0:T(8,128)(2,1)}, bf16[4,384,1536]{2,1,0:T(8,128)(2,1)}) custom-call(bf16[4,256,1152]{2,1,0:T(8,128)(2,1)} %get-tuple-element.59.triple_in, bf16[384,1536]{1,0:T(8,128)(2,1)} %out_in.3, bf16[256,1536]{1,0:T(8,128)(2,1)} %bitcast.44, ...), custom_call_target="tpu_custom_call" | custom-call | tf_op jit(solution)/shard_map/attend/pallas_call | solution.py:628
  114.2 29.3 %cross.1 = (bf16[256,1536]{1,0:T(8,128)(2,1)}, bf16[256,1536]{1,0:T(8,128)(2,1)}, f32[256,1536]{1,0:T(8,128)}, bf16[256,1536]{1,0:T(8,128)(2,1)}, bf16[4,256,1536]{2,1,0:T(8,128)(2,1)}) custom-call(f32[256,1536]{1,0:T(8,128)} %get-tuple-element.60.after_in.self_in, f32[6,1536]{1,0:T(8,128)} %reshape.93.gains.gains_in, ...), custom_call_target="tpu_custom_call" | custom-call | tf_op jit(solution)/shard_map/cross/pallas_call | solution.py:761
  143.5 65.1 %feed.1 = (bf16[4,256,1536]{2,1,0:T(8,128)(2,1)}, bf16[256,1536]{1,0:T(8,128)(2,1)}, bf16[2,768,1536]{2,1,0:T(8,128)(2,1)}) custom-call(bf16[256,1536]{1,0:T(8,128)(2,1)} %get-tuple-element.64.rows_in, bf16[4,256,1536]{2,1,0:T(8,128)(2,1)} %get-tuple-element.65.grads_in, bf16[1536,1536]{1,0:T(8,128)(2,1)} %up_in.1, bf16[1536,1536]{1,0:T(8,128)(2,1)} %down_in.1), custom_call_target="tpu_custom_call" | custom-call | tf_op jit(solution)/shard_map/feed/pallas_call | solution.py:981
  208.6 47.0 %cross_back.1 = (f32[256,1536]{1,0:T(8,128)}, bf16[256,1536]{1,0:T(8,128)(2,1)}, f32[32,1536]{1,0:T(8,128)}, bf16[4,64,768]{2,1,0:T(8,128)(2,1)}, bf16[4,768,384...) custom-call(f32[256,1536]{1,0:T(8,128)} %bitcast.47, ...), custom_call_target="tpu_custom_call" | custom-call | tf_op jit(solution)/shard_map/cross_back/pallas_call | solution.py:1209
  255.7 103.2 %attend_back.1 = (f32[256,1536]{1,0:T(8,128)}, f32[16,1536]{1,0:T(8,128)}, f32[64,1536]{1,0:T(8,128)}, bf16[768,1152]{1,0:T(8,128)(2,1)}, bf16[192,1536]{1,0:T(8...) custom-call(bf16[256,1536]{1,0:T(8,128)(2,1)} %get-tuple-element.73., ...), custom_call_target="tpu_custom_call", output_to_operand_aliasing={{6}: (15, {})} | custom-call | tf_op jit(solution)/shard_map/attend_back/pallas_call | solution.py:1505
  358.9 141.3 %total.1 = (bf16[3,16,48,384]{3,2,1,0:T(8,128)(2,1)}, bf16[16,48,384]{2,1,0:T(8,128)(2,1)}, bf16[16,48,768]{2,1,0:T(8,128)(2,1)}, bf16[4,48,1536]{2,1,0:T(8,128)...) custom-call(bf16[32,48,1536]{2,1,0:T(8,128)(2,1)} %bitcast.36, ...), custom_call_target="tpu_custom_call", output_to_operand_aliasing={{7}: (10, {}), {8}: (11, {})} | custom-call | tf_op jit(solution)/shard_map/total/pallas_call | solution.py:1738
  500.2 0.0 copy-start.5
  500.2 1.6 slice_reduce_fusion
  501.8 2.2 bitcast_convert_fusion.3
  504.1 0.0 copy-done.5
  504.1 2.3 reshape.118
  506.4 0.0 copy-done.6
  506.4 1.8 bitcast_convert_fusion.2
  508.1 0.1 copy-done.2
  508.2 2.2 convert_bitcast_fusion
  510.4 0.2 copy-done
  510.6 1.3 copy-done.1
  511.9 5.4 %bitcast_convert_fusion = (f32[768,1536]{1,0:T(8,128)}, f32[768,1536]{1,0:T(8,128)}) fusion(bf16[16,48,1536]{2,1,0:T(8,128)(2,1)S(1)} %copy-done, bf16[16,48,1536]{2,1,0:T(8,128)(2,1)S(1)} %copy-done.1), kind=kLoop, calls=%fused_computation.1 | loop fusion | flops 2359296 | bytes 14155776 | tf_op jit(solution)/shard_map/reshape | solution.py:1806
  517.2 1.1 copy.48
  518.4 0.8 copy-done.4
  519.2 1.1 copy.49
  520.4 0.1 copy-done.8
  520.4 0.7 copy.50
  (11 shorter events, 0.0 us)
Async XLA Ops:
  500.2 3.9 copy-start.5
  501.8 4.5 copy-start.6
  501.8 4.5 copy-start.7
  506.4 1.8 copy-start.2
  508.2 2.4 copy-start
  508.2 3.7 copy-start.1
  511.9 5.4 %copy-start.3 = (f32[256,1536]{1,0:T(8,128)S(1)}, f32[256,1536]{1,0:T(8,128)}, u32[]{:S(2)}) copy-start(f32[256,1536]{1,0:T(8,128)} %get-tuple-element.72) | copy-start | bytes 4718596
  517.2 2.0 copy-start.4
  519.2 1.2 copy-start.8

commit v4 on v3

--- a/solution.py
+++ b/solution.py
@@ -194,7 +194,7 @@
     return jax.ShapeDtypeStruct(dims, kind)
 
 
-LAG = 2
+LAG = 3
 RING = 4
 
 
@@ -309,28 +309,33 @@
                 self.outputs(f, self.result.at[f % RING], self.store, lambda copy: copy.wait())
 
 
+KV_TICKS, OUT_TICKS = 20, 28
+
+
 class Layout:
     def __init__(self, m, local, subs, groups):
         piece = m // subs
         self.m, self.piece, self.local = m, piece, local
         self.out_rows = local // subs
         self.chunk = 48
-        self.feed = 2 * piece
-        self.qkv = self.feed
-        self.kv = self.qkv + 3 * piece // 4
-        self.out = self.kv + piece // 2
-        self.cq = self.out + self.out_rows
-        self.co = self.cq + piece // 4
-        self.rows = self.co + self.out_rows
-        self.count = self.rows // self.chunk
-        self.feed_count = self.feed // self.chunk
+        quarter = piece // 4 // self.chunk
+        self.quarter = quarter
+        self.feed_count = 2 * piece // self.chunk
+        self.kv = self.feed_count
+        self.out = self.kv + 2 * quarter
+        self.qkv = self.out + self.out_rows // self.chunk
+        self.cq = self.qkv + 3 * quarter
+        self.co = self.cq + quarter
+        self.count = self.co + self.out_rows // self.chunk
         self.window = LAG * (groups + 1)
-        self.middle = min(10, self.feed_count // 3)
-        self.later = min(32, self.feed_count)
         self.end = self.count + LAG * (groups - 1)
-
-
-def feed_outputs(layout, *halves):
+        self.middle = min(12, self.feed_count // 3)
+        self.later = self.feed_count
+        if self.middle + KV_TICKS <= self.kv and self.middle + OUT_TICKS <= self.out:
+            self.later = self.middle + OUT_TICKS + 2
+
+
+def sum_outputs(layout, halves, text=None):
     def outputs(c, block, store, act):
         count = layout.feed_count // 2
         for i, half in enumerate(halves):
@@ -338,6 +343,15 @@
             @pl.when(either(c >= i * count, c < (i + 1) * count))
             def _(i=i, half=half):
                 act(pltpu.make_async_copy(block, half.at[c - i * count], store.at[c % RING, 0]))
+
+        if text is not None:
+
+            @pl.when(either(c >= layout.kv, c < layout.out))
+            def _():
+                for i in range(2):
+                    lanes = pl.ds(2 * i * layout.local, 2 * layout.local)
+                    target = text.at[2 * i * layout.quarter + c - layout.kv]
+                    act(pltpu.make_async_copy(block.at[:, lanes], target, store.at[c % RING, i]))
 
     return outputs
 
@@ -1017,14 +1031,13 @@
 
 def cross_back_kernel(
     layout,
-    cot_in, norm_in, cross_in, self_in, gains_in, query_in, flat_in, memory_in, wq_in, wo_in, part_in, own_in,
-    o_out, o_branch, o_sums, o_memory, o_wq, o_wo, o_layer, o_down, o_land,
+    cot_in, norm_in, cross_in, self_in, gains_in, query_in, flat_in, memory_in, wq_in, wo_in, own_in,
+    o_out, o_branch, o_sums, o_memory, o_wq, o_wo, o_down, o_land,
     cot, norm, after_cross, after_self, gains, query, flat, memory, wq, wo,
     branch, rows, query_grad, memory_grad, sums, whole_q, whole_o, land_q, land_o, piece_q, piece_o,
-    norm_self, part, land_part, stage_part, own, land, ring, result, ring_send, ring_recv, ring_store,
+    norm_self, own, land, ring, result, ring_send, ring_recv, ring_store,
     load, store, send, recv,
 ):
-    t, x, y, d = neighbours()
     s = lax.axis_index("sub")
     subs = lax.axis_size("sub")
     loads = [
@@ -1033,27 +1046,24 @@
             (
                 (cot_in, cot), (norm_in, norm), (cross_in, after_cross), (gains_in, gains), (wo_in, wo),
                 (query_in, query), (flat_in, flat), (memory_in, memory), (self_in, after_self), (wq_in, wq),
-                (part_in, part), (own_in, own),
+                (own_in.at[pl.ds(0, layout.middle)], own),
             )
         )
     ]
-    for copy in loads:
+    for copy in loads[10:] + loads[:10]:
         copy.start()
-    greet([{"tensor": x}, {"tensor": y}] + [{"sub": (s + k) % subs} for k in range(1, subs)] + group_ring())
-    scatter = Scatter(part, land_part, stage_part, send, recv, 8 * (subs - 1))
+    greet([{"sub": (s + k) % subs} for k in range(1, subs)] + group_ring())
     pump = Pump(
         own, land, ring, result, ring_send, ring_recv, ring_store, 0, layout.middle, layout.count,
-        feed_outputs(layout, o_down),
+        sum_outputs(layout, (o_down,)),
     )
     n, m = cot.shape
     width = wq.shape[2]
     texts = memory.shape[1]
-    for copy in (*loads[:4], *loads[10:]):
+    loads[10].wait()
+    pump.step(jnp.int32(0))
+    for copy in loads[:4]:
         copy.wait()
-    scatter.diagonal()
-    scatter.along_x()
-    scatter.along_y()
-    pump.step(jnp.int32(0))
     scale = HEAD ** (-0.5)
 
     def feed_block(i, carry):
@@ -1118,10 +1128,11 @@
     halves_q = Halves(whole_q, land_q, send, recv, 0)
     halves_o = Halves(whole_o, land_o, send, recv, 4 * (subs - 1))
 
-    scatter.relay()
-
     def weights(q, carry):
-        tick(q + 6)
+        @pl.when(q % 2 == 0)
+        def _():
+            tick(6 + q // 2)
+
 
         def grad_o(j, carry):
             whole_o[q, :, cols(j, 512)] = dot_c(flat[:, cols(q, width)], branch[:, cols(j, 512)]).astype(BF)
@@ -1143,6 +1154,10 @@
     loads[9].wait()
 
     def norm_grad(j, carry):
+        @pl.when(j % 3 == 0)
+        def _():
+            tick(8 + j // 3)
+
         here = rows_at(j, 256)
         total = jnp.zeros((n, 256), F32)
         for q in range(4):
@@ -1172,12 +1187,7 @@
     for copy in stores[1:]:
         copy.start()
 
-    def take_layer(here, total):
-        after_cross[here] = after_cross[here] + total
-
-    scatter.finish(take_layer, 64)
-    stores.append(pltpu.make_async_copy(after_cross, o_layer, store.at[6]))
-    stores[-1].start()
+    tick(jnp.int32(10))
     for halves, piece in ((halves_q, piece_q), (halves_o, piece_o)):
         for q in range(4):
 
@@ -1186,12 +1196,12 @@
 
             halves.total(q, take, 16)
     stores += [pltpu.make_async_copy(piece_q, o_wq, store.at[4]), pltpu.make_async_copy(piece_o, o_wo, store.at[5])]
-    for copy in stores[5:]:
+    for copy in stores[4:]:
         copy.start()
+    tick(jnp.int32(11))
     pump.drain()
-    stores.append(pltpu.make_async_copy(land, o_land, store.at[7]))
+    stores.append(pltpu.make_async_copy(land, o_land, store.at[6]))
     stores[-1].start()
-    scatter.drain()
     for q in range(4):
         halves_q.drain(q)
         halves_o.drain(q)
@@ -1199,11 +1209,10 @@
         copy.wait()
 
 
-def cross_back(layout, cot, norm, after_cross, after_self, gains, query, flat, memory, wq, wo, part, own, subs):
+def cross_back(layout, cot, norm, after_cross, after_self, gains, query, flat, memory, wq, wo, own, subs):
     n, m = cot.shape
     width = wq.shape[2]
-    count = 8 * (subs - 1) + 6
-    chunks = layout.feed_count
+    count = 8 * (subs - 1)
     held = (2, layout.window, layout.chunk, m)
     part_q, part_o = (4, m // subs, width), (4, width // subs, m)
     return pl.pallas_call(
@@ -1211,10 +1220,10 @@
         name="cross_back",
         out_shape=[
             shape(n, m, kind=F32), shape(n, m), shape(32, m, kind=F32), shape(*memory.shape), shape(*part_q), shape(*part_o),
-            shape(n, m, kind=F32), shape(layout.feed_count // 2, layout.chunk, m), shape(*held),
+            shape(layout.feed_count // 2, layout.chunk, m), shape(*held),
         ],
-        in_specs=[ANY] * 12,
-        out_specs=[ANY] * 9,
+        in_specs=[ANY] * 11,
+        out_specs=[ANY] * 8,
         scratch_shapes=[
             pltpu.VMEM((n, m), F32), pltpu.VMEM((n, m), BF), pltpu.VMEM((n, m), F32), pltpu.VMEM((n, m), F32),
             pltpu.VMEM(gains.shape, F32), pltpu.VMEM((n, m), BF), pltpu.VMEM((n, m), BF), pltpu.VMEM(memory.shape, BF),
@@ -1223,12 +1232,12 @@
             pltpu.VMEM((32, m), F32), pltpu.VMEM((4, m, width), BF), pltpu.VMEM((4, width, m), BF),
             pltpu.VMEM((4, subs - 1, m // subs, width), BF), pltpu.VMEM((4, subs - 1, width // subs, m), BF),
             pltpu.VMEM(part_q, BF), pltpu.VMEM(part_o, BF),
-            pltpu.VMEM((n, m), F32), pltpu.VMEM((4, n, m), BF), pltpu.VMEM((6, n // 2, m), BF), pltpu.VMEM((2, n // 2, m), BF),
-            *pump_scratch(layout, chunks),
-            dma(12), dma(8), dma(count), dma(count),
+            pltpu.VMEM((n, m), F32),
+            *pump_scratch(layout, layout.middle),
+            dma(11), dma(7), dma(count), dma(count),
         ],
         compiler_params=params(5),
-    )(cot, norm, after_cross, after_self, gains, query, flat, memory, wq, wo, part, own)
+    )(cot, norm, after_cross, after_self, gains, query, flat, memory, wq, wo, own)
 
 
 def attend_pair_back(p, triple, place, blocks, heads, grad_heads, deltas, sums, grads, grad_keys, grad_values):
@@ -1270,7 +1279,7 @@
     layout,
     branch_in, triple_in, flat_in, sums_in, out_in, qkv_in, rows_in, frames_in, gains_in, grad_in, memory_in, text_in, kv_in,
     own_in, land_in, down_in,
-    o_frames, o_sums, o_text, o_qkv, o_out, o_kv, o_down, o_up, o_land,
+    o_frames, o_sums, o_text, o_qkv, o_more, o_down, o_up, o_kv, o_land,
     branch, triple, flat, sums, out, qkv, rows, frames, gains, grad_out, memory, text, kv,
     land_m, stage_m,
     grad_heads, deltas, grads, grad_keys, grad_values, part, land, stage, whole_qkv, land_qkv, whole_out, land_out,
@@ -1282,7 +1291,7 @@
     subs = lax.axis_size("sub")
     names = (
         (branch_in, branch.at[t]), (out_in, out), (flat_in, flat), (triple_in, triple), (sums_in, sums),
-        (memory_in, memory), (own_in, own), (land_in, held),
+        (memory_in, memory), (own_in, own.at[pl.ds(0, layout.feed_count)]), (land_in, held),
         *((qkv_in.at[i], qkv.at[:, pl.ds(i * qkv_in.shape[2], qkv_in.shape[2])]) for i in range(3)), (rows_in, rows),
         (text_in, text), (kv_in, kv), (frames_in, frames), (gains_in, gains), (grad_in, grad_out),
     )
@@ -1295,7 +1304,7 @@
     first, last = layout.middle, layout.later
     pump = Pump(
         own, held, ring, result, ring_send, ring_recv, ring_store, first, last, layout.count,
-        feed_outputs(layout, o_down, o_up),
+        sum_outputs(layout, (o_down, o_up), o_kv),
     )
 
     def tick(k):
@@ -1409,6 +1418,7 @@
         return carry
 
     lax.fori_loop(0, 4, back, 0)
+    tick(16)
     scatter_m.relay()
 
     def take_m(here, total):
@@ -1425,6 +1435,7 @@
 
     lax.fori_loop(0, m // 384, grad_kv, 0)
     halves_kv.start(0)
+    tick(17)
 
     def grad_wout(j, carry):
         whole_out[0, :, cols(j, 512)] = dot_c(
@@ -1434,10 +1445,18 @@
 
     lax.fori_loop(0, m // 512, grad_wout, 0)
     halves_out.start(0)
-    scatter.relay()
+    tick(18)
+    chunk, half = layout.chunk, 2 * layout.quarter
+
+    def take_kv(here, total):
+        c = here.start // chunk
+        own[layout.kv + c % half, :, cols(c // half, 2 * local)] = total.astype(BF)
+
+    halves_kv.total(0, take_kv, chunk)
+    tick(19)
 
     def grad_wqkv(j, carry):
-        tick(16 + j)
+        tick(20 + j)
         turned = rows[:, :, cols(j, 256)].reshape(4 * n, 256)
 
         def inner(i, carry):
@@ -1451,14 +1470,24 @@
 
     lax.fori_loop(0, m // 256, grad_wqkv, 0)
     halves_qkv.start(0)
-    for each, output, slot in ((halves_kv, o_kv, 1), (halves_out, o_out, 2), (halves_qkv, o_qkv, 3)):
-
-        def take(here, total, each=each):
-            each.land[0, 0, here] = total.astype(BF)
-
-        each.total(0, take, 16)
-        stores.append(pltpu.make_async_copy(each.land.at[0, 0], output, store.at[slot]))
-        stores[-1].start()
+    tick(26)
+
+    def take_out(here, total):
+        own[layout.out + here.start // chunk] = total.astype(BF)
+
+    halves_out.total(0, take_out, chunk)
+    scatter.relay()
+    tick(27)
+
+    def take(here, total):
+        land_qkv[0, 0, here] = total.astype(BF)
+
+    halves_qkv.total(0, take, 16)
+    stores.append(pltpu.make_async_copy(land_qkv.at[0, 0], o_qkv, store.at[1]))
+    stores.append(pltpu.make_async_copy(own.at[pl.ds(layout.kv, layout.qkv - layout.kv)], o_more, store.at[2]))
+    for copy in stores[-2:]:
+        copy.start()
+    tick(28)
     for copy in loads[14:]:
         copy.wait()
 
@@ -1476,13 +1505,14 @@
 
     zero = jnp.zeros((8, m), F32)
     gain_sum, bias_sum = lax.fori_loop(0, n // 64, frame_block, (zero, zero))
+    tick(29)
     sums_out[0:8] = gain_sum
     sums_out[8:16] = bias_sum
-    stores += [pltpu.make_async_copy(grad_out, o_frames, store.at[4]), pltpu.make_async_copy(sums_out, o_sums, store.at[5])]
+    stores += [pltpu.make_async_copy(grad_out, o_frames, store.at[3]), pltpu.make_async_copy(sums_out, o_sums, store.at[4])]
     for copy in stores[-2:]:
         copy.start()
     pump.drain()
-    stores.append(pltpu.make_async_copy(held, o_land, store.at[6]))
+    stores.append(pltpu.make_async_copy(held, o_land, store.at[5]))
     stores[-1].start()
     gather.drain()
     for each in (scatter, scatter_m):
@@ -1507,11 +1537,12 @@
         name="attend_back",
         out_shape=[
             shape(n, m, kind=F32), shape(16, m, kind=F32), shape(texts, m, kind=F32), shape(m // subs, width),
-            shape(local // subs, m), shape(m // subs, kvw), shape(*down.shape), shape(*down.shape), shape(*land.shape),
+            shape(layout.qkv - layout.kv, layout.chunk, m), shape(*down.shape), shape(*down.shape),
+            shape(4 * layout.quarter, layout.chunk, kvw), shape(*land.shape),
         ],
         in_specs=[ANY] * 16,
         out_specs=[ANY] * 9,
-        input_output_aliases={15: 6},
+        input_output_aliases={15: 5},
         scratch_shapes=[
             v((4, n, m), BF), v(triple.shape, BF), v(flat.shape, BF), v(sums.shape, F32), v(out.shape, BF), v((m, width), BF),
             v(rows.shape, BF), v(frames.shape, frames.dtype), v(gains.shape, F32), v((n, m), F32), v(memory.shape, BF),
@@ -1523,8 +1554,8 @@
             v((1, local, m), BF), v((1, subs - 1, local // subs, m), BF),
             v((1, m, kvw), BF), v((1, subs - 1, m // subs, kvw), BF),
             v((texts, m), F32), v((16, m), F32), v((texts, kvw), BF),
-            *pump_scratch(layout, layout.feed_count),
-            dma(17), dma(7), dma(count), dma(count),
+            *pump_scratch(layout, layout.qkv),
+            dma(17), dma(6), dma(count), dma(count),
         ],
         compiler_params=params(6),
     )(branch, triple, flat, sums, out, qkv, rows, frames, gains, grad, memory, text, kv, own, land, down)
@@ -1532,21 +1563,19 @@
 
 def total_kernel(
     layout,
-    feed_in, qkv_in, kv_in, out_in, cross_q_in, cross_o_in, sums_a_in, sums_b_in, text_in, land_in, down_in, up_in,
-    o_qkv, o_cq, o_kv, o_out, o_co, o_text, o_vectors, o_down, o_up,
+    feed_in, qkv_in, more_in, cross_q_in, cross_o_in, sums_a_in, sums_b_in, text_in, land_in, part_in, after_in,
+    down_in, up_in, kv_in,
+    o_qkv, o_cq, o_out, o_co, o_text, o_vectors, o_layer, o_down, o_up, o_kv,
     own, held, ring, result, ring_send, ring_recv, ring_store,
-    cross_q, cross_o, land_q, land_o, stage_q, stage_o,
+    cross_q, cross_o, land_q, land_o, stage_q, stage_o, part, land_p, stage_p, after,
     sums_a, sums_b, text, text_land, text_full, vectors, vectors_land, share, share_land, load, store, send, recv,
 ):
     t, x, y, d = neighbours()
     s, subs = lax.axis_index("sub"), lax.axis_size("sub")
     g, groups = lax.axis_index("group"), lax.axis_size("group")
     chunk, m, local = layout.chunk, layout.m, layout.local
-    width, quarter = 3 * local, layout.piece // 4 // chunk
-    at_qkv, at_kv, at_out, at_cq, at_co = (
-        r // chunk for r in (layout.qkv, layout.kv, layout.out, layout.cq, layout.co)
-    )
-    outs = layout.out_rows // chunk
+    width, quarter = 3 * local, layout.quarter
+    at_kv, at_out, at_qkv, at_cq, at_co = layout.kv, layout.out, layout.qkv, layout.cq, layout.co
     def outputs(c, block, slots, act):
         slot = c % RING
 
@@ -1559,10 +1588,10 @@
         def whole(output):
             return lambda r: [(block, output.at[r])]
 
-        region(0, at_qkv // 2, whole(o_down))
-        region(at_qkv // 2, at_qkv, whole(o_up))
+        region(0, at_kv // 2, whole(o_down))
+        region(at_kv // 2, at_kv, whole(o_up))
         region(
-            at_qkv, at_kv,
+            at_qkv, at_cq,
             lambda r: [
                 *((block.at[:, pl.ds(i * local, local)], o_qkv.at[i, r]) for i in range(3)),
                 (block.at[:, pl.ds(width, local)], o_qkv.at[r // quarter, 3 * quarter + r % quarter]),
@@ -1574,17 +1603,18 @@
                 (block.at[:, pl.ds(2 * i * local, 2 * local)], o_kv.at[2 * i * quarter + r]) for i in range(2)
             ],
         )
-        region(at_out, at_cq, whole(o_out))
+        region(at_out, at_qkv, whole(o_out))
         region(
             at_cq, at_co,
             lambda r: [(block.at[:, pl.ds(i * local, local)], o_cq.at[i * quarter + r]) for i in range(4)],
         )
-        region(at_co, at_co + outs, whole(o_co))
+        region(at_co, layout.count, whole(o_co))
 
     fresh = max(0, layout.later - LAG * (groups - 1))
+    newer = max(fresh, at_kv)
     pairs = [
         (land_in, held),
-        (feed_in.at[pl.ds(fresh, at_qkv - fresh)], own.at[pl.ds(fresh, at_qkv - fresh)]),
+        (more_in.at[pl.ds(newer - at_kv, at_qkv - newer)], own.at[pl.ds(newer, at_qkv - newer)]),
         (qkv_in.at[pl.ds(0, 3 * quarter)], own.at[pl.ds(at_qkv, 3 * quarter), :, pl.ds(0, width)]),
     ]
     for i in range(3):
@@ -1594,15 +1624,13 @@
                 own.at[pl.ds(at_qkv + i * quarter, quarter), :, pl.ds(width, local)],
             )
         )
-    pairs += [(sums_a_in, sums_a), (sums_b_in, sums_b), (text_in, text), (cross_q_in, cross_q), (cross_o_in, cross_o)]
-    for i in range(2):
-        pairs.append(
-            (
-                kv_in.at[pl.ds(2 * i * quarter, 2 * quarter)],
-                own.at[pl.ds(at_kv, 2 * quarter), :, pl.ds(2 * i * local, 2 * local)],
-            )
-        )
-    pairs.append((out_in, own.at[pl.ds(at_out, outs)]))
+    if fresh < at_kv:
+        pairs.append((feed_in.at[pl.ds(fresh, at_kv - fresh)], own.at[pl.ds(fresh, at_kv - fresh)]))
+    early = len(pairs)
+    pairs += [
+        (sums_a_in, sums_a), (sums_b_in, sums_b), (text_in, text), (cross_q_in, cross_q), (cross_o_in, cross_o),
+        (part_in, part), (after_in, after),
+    ]
     loads = [pltpu.make_async_copy(a, b, load.at[i]) for i, (a, b) in enumerate(pairs)]
     for copy in loads:
         copy.start()
@@ -1613,7 +1641,6 @@
         + [{"group": (g + k) % groups} for k in range(1, groups)]
     )
     begin, end = layout.later, layout.end
-    loads[1].wait()
     pump = Pump(own, held, ring, result, ring_send, ring_recv, ring_store, begin, end, layout.count, outputs)
 
     def run(a, b):
@@ -1623,10 +1650,10 @@
 
         lax.fori_loop(a, b, step, 0)
 
-    for copy in loads[2:6]:
+    for copy in loads[1:early]:
         copy.wait()
     run(begin, begin + 1)
-    for copy in loads[6:]:
+    for copy in loads[early:]:
         copy.wait()
     share_width = m // subs
     for i in range(6):
@@ -1663,6 +1690,7 @@
     scatter_o = Scatter(cross_o, land_o, stage_o, send, recv, base + 6)
     for copy in first:
         copy.start()
+    scatter_p = Scatter(part, land_p, stage_p, send, recv, base + 12)
     for each in (scatter_q, scatter_o):
         each.diagonal()
     for each in (scatter_q, scatter_o):
@@ -1692,9 +1720,12 @@
         copy.start()
     relay = max(begin + 6, begin + (at_cq - begin) // 2)
     run(begin + 6, relay)
+    scatter_p.diagonal()
+    scatter_p.along_x()
+    scatter_p.along_y()
     for each in (scatter_q, scatter_o):
         each.relay()
-    finish = min(at_cq, relay + 8)
+    finish = at_cq
     run(relay, finish)
 
     def take_q(rows, value):
@@ -1710,7 +1741,17 @@
         own[at_co + rows.start // chunk, rows_at(rows.start % chunk // step, step)] = value.astype(BF)
 
     scatter_o.finish(take_o, step)
-    run(finish, end)
+    late = min(finish + 8, end)
+    run(finish, late)
+    scatter_p.relay()
+    run(late, end)
+
+    def take_layer(rows, value):
+        after[rows] = after[rows] + value
+
+    scatter_p.finish(take_layer, 64)
+    layer_store = pltpu.make_async_copy(after, o_layer, store.at[2])
+    layer_store.start()
     for copy in third:
         copy.wait_recv()
     total = share[1, 0]
@@ -1721,42 +1762,46 @@
     vector_store.start()
     for copy in second + third:
         copy.wait_send()
-    for each in (scatter_q, scatter_o):
+    for each in (scatter_q, scatter_o, scatter_p):
         each.drain()
     pump.drain()
+    layer_store.wait()
     text_store.wait()
     vector_store.wait()
 
 
-def total(layout, pieces, qkv, kv, out, cross_q, cross_o, sums_a, sums_b, text, land, down, up, subs, groups):
+def total(layout, pieces, qkv, more, cross_q, cross_o, sums_a, sums_b, text, land, part, after, down, up, kv, subs, groups):
     m, chunk = layout.m, layout.chunk
+    n = after.shape[0]
     v = pltpu.VMEM
-    sems = 7 + subs + groups + 12
-    tall = lambda a: a.reshape(-1, chunk, a.shape[1])
-    qkv, kv, out = tall(qkv), tall(kv), tall(out)
+    sems = 7 + subs + groups + 18
+    qkv = qkv.reshape(-1, chunk, qkv.shape[1])
     piece_q, piece_o = cross_q.shape[1:], cross_o.shape[1:]
+    out_shape = shape(layout.qkv - layout.out, chunk, m)
     return pl.pallas_call(
         partial(total_kernel, layout),
         name="total",
         out_shape=[
-            shape(3, *qkv.shape[:2], layout.local), shape(layout.piece // chunk, chunk, layout.local), shape(*kv.shape), shape(*out.shape),
-            shape(*out.shape), shape(*text.shape, kind=F32), shape(8, m // subs, kind=F32), shape(*down.shape), shape(*up.shape),
+            shape(3, *qkv.shape[:2], layout.local), shape(layout.piece // chunk, chunk, layout.local), out_shape, out_shape,
+            shape(*text.shape, kind=F32), shape(8, m // subs, kind=F32), shape(n, m, kind=F32),
+            shape(*down.shape), shape(*up.shape), shape(*kv.shape),
         ],
-        in_specs=[ANY] * 12,
-        out_specs=[ANY] * 9,
-        input_output_aliases={10: 7, 11: 8},
+        in_specs=[ANY] * 14,
+        out_specs=[ANY] * 10,
+        input_output_aliases={11: 7, 12: 8, 13: 9},
         scratch_shapes=[
             *pump_scratch(layout, layout.count),
             v(cross_q.shape, BF), v(cross_o.shape, BF),
             v((6, piece_q[0] // 2, piece_q[1]), BF), v((6, piece_o[0] // 2, piece_o[1]), BF),
             v((2, piece_q[0] // 2, piece_q[1]), BF), v((2, piece_o[0] // 2, piece_o[1]), BF),
+            v((4, n, m), BF), v((6, n // 2, m), BF), v((2, n // 2, m), BF), v((n, m), F32),
             v(sums_a.shape, F32), v(sums_b.shape, F32), v(text.shape, F32),
             v((3, text.shape[0] // 4, m), F32), v(text.shape, F32), v((subs, 8, m // subs), F32), v((3, subs, 8, m // subs), F32),
             v((3, subs, 8, m // subs), F32), v((subs - 1 + groups - 1, 8, m // subs), F32),
-            dma(14), dma(2), dma(sems), dma(sems),
+            dma(14), dma(3), dma(sems), dma(sems),
         ],
         compiler_params=params(7),
-    )(pieces, qkv, kv, out, cross_q, cross_o, sums_a, sums_b, text, land, down, up)
+    )(pieces, qkv, more, cross_q, cross_o, sums_a, sums_b, text, land, part, after, down, up, kv)
 
 
 def local(
@@ -1776,16 +1821,16 @@
     layout = Layout(m, width, subs, groups)
     part, norm_grad, pieces = feed(feed_rows, grads, feedup, feeddown, subs)
     pieces = pieces.reshape(-1, layout.chunk, m)
-    grad_out, branch, sums_a, memory_grad, piece_q, piece_o, layer_output, down, land = cross_back(
-        layout, cotangent[0], norm_grad, after_cross, after_self, gains, query, cross_flat, memory, wq, wo, part, pieces, subs
+    grad_out, branch, sums_a, memory_grad, piece_q, piece_o, down, land = cross_back(
+        layout, cotangent[0], norm_grad, after_cross, after_self, gains, query, cross_flat, memory, wq, wo, pieces, subs
     )
-    frame_grad, sums_b, text_part, grad_qkv, grad_out_weight, grad_kv, down, up, land = attend_back(
+    frame_grad, sums_b, text_part, grad_qkv, more, down, up, full_kv, land = attend_back(
         layout, branch, triple, flat, sums, selfout, qkv, rows, frames[0], gains, grad_out, memory_grad,
         text_states[0], kv, pieces, land, down, subs,
     )
-    full_qkv, full_cq, full_kv, full_out, full_co, text_grad, vectors, down, up = total(
-        layout, pieces, grad_qkv, grad_kv, grad_out_weight, piece_q, piece_o, sums_a, sums_b, text_part, land, down, up,
-        subs, groups,
+    full_qkv, full_cq, full_out, full_co, text_grad, vectors, layer_output, down, up, full_kv = total(
+        layout, pieces, grad_qkv, more, piece_q, piece_o, sums_a, sums_b, text_part, land, part, after_cross,
+        down, up, full_kv, subs, groups,
     )
     return (
         layer_output[None],

time: 522 us -> 510 us (0.977)
  Pallas kernels: 491 us -> 480 us
    pallas_call x1, Pallas kernels: 141 us -> 123 us  [total(): pl.pallas_call(partial(total_kernel, layout), name='total', out_shape=[sh...]
    pallas_call x1, Pallas kernels: 103 us -> 119 us  [attend_back(): pl.pallas_call(partial(attend_back_kernel, layout), name='attend_back', o...]
    pallas_call x1, Pallas kernels: 47 us -> 38.2 us  [cross_back(): pl.pallas_call(partial(cross_back_kernel, layout), name='cross_back', out...]
where the time goes in v4:
time: 510 us
  Pallas kernels  480 us (94%)
  local copies, waits for them, and re-layouts  17.8 us (3%)
  other arithmetic  11.6 us (2%)
    pallas_call x1, Pallas kernels, total(): pl.pallas_call(partial(total_kernel, layout), name='total', out_shape=[sh...  123 us
    pallas_call x1, Pallas kernels, attend_back(): pl.pallas_call(partial(attend_back_kernel, layout), name='attend_back', o...  119 us
    pallas_call x1, Pallas kernels, attend(): pl.pallas_call(attend_kernel, name='attend', out_shape=[shape(4, n, local...  68.3 us
    pallas_call x1, Pallas kernels, feed(): pl.pallas_call(feed_kernel, name='feed', out_shape=[shape(4, n, m), shape...  65.1 us
    pallas_call x1, Pallas kernels, cross_back(): pl.pallas_call(partial(cross_back_kernel, layout), name='cross_back', out...  38.2 us
    pallas_call x1, Pallas kernels, enter(): pl.pallas_call(enter_kernel, name='enter', out_shape=[shape(4, n, m), sha...  36.8 us
    pallas_call x1, Pallas kernels, cross(): pl.pallas_call(cross_kernel, name='cross', out_shape=[shape(n, m), shape(...  29.2 us
    unnamed x27, local copies, waits for them, and re-layouts  12.5 us

profile of v4, /device:TPU:0, one launch (start us, length us, event | category | flops | bytes accessed | tf_op | source)
XLA Modules:
  0.0 509.9 jit_solution(16647093039001540240)
XLA Ops:
  0.7 0.7 constant_dynamic-update-slice_fusion.5
  1.4 0.7 constant_dynamic-update-slice_fusion.4
  2.1 0.7 constant_dynamic-update-slice_fusion.3
  2.8 0.7 constant_dynamic-update-slice_fusion.2
  3.5 0.7 constant_dynamic-update-slice_fusion.1
  4.2 0.7 constant_dynamic-update-slice_fusion
  4.9 0.6 reshape.87.gains.gains_in
  5.5 3.5 copy.36
  9.0 36.8 %enter.1 = (bf16[4,256,1536]{2,1,0:T(8,128)(2,1)}, bf16[4,256,1152]{2,1,0:T(8,128)(2,1)}, bf16[4,64,768]{2,1,0:T(8,128)(2,1)}) custom-call(bf16[256,1536]{1,0:T(8,128)(2,1)} %bitcast.41, f32[6,1536]{1,0:T(8,128)} %reshape.87.gains.gains_in, bf16[3,1536,384]{2,1,0:T(8,128)(2,1)} %bitcast.39, bf16[64,1536]{1,0:T(8,128)(2,1)} %bitcast.50, ...), custom_call_target="tpu_custom_call" | custom-call | tf_op jit(solution)/shard_map/enter/pallas_call | solution.py:465
  45.9 68.3 %attend.1 = (bf16[4,256,384]{2,1,0:T(8,128)(2,1)}, f32[4,256,128]{2,1,0:T(8,128)}, f32[256,1536]{1,0:T(8,128)}, bf16[4,1536,384]{2,1,0:T(8,128)(2,1)}, bf16[4,384,1536]{2,1,0:T(8,128)(2,1)}) custom-call(bf16[4,256,1152]{2,1,0:T(8,128)(2,1)} %get-tuple-element.59.triple_in, bf16[384,1536]{1,0:T(8,128)(2,1)} %out_in.3, bf16[256,1536]{1,0:T(8,128)(2,1)} %bitcast.42, ...), custom_call_target="tpu_custom_call" | custom-call | tf_op jit(solution)/shard_map/attend/pallas_call | solution.py:642
  114.2 29.2 %cross.1 = (bf16[256,1536]{1,0:T(8,128)(2,1)}, bf16[256,1536]{1,0:T(8,128)(2,1)}, f32[256,1536]{1,0:T(8,128)}, bf16[256,1536]{1,0:T(8,128)(2,1)}, bf16[4,256,1536]{2,1,0:T(8,128)(2,1)}) custom-call(f32[256,1536]{1,0:T(8,128)} %get-tuple-element.60.after_in.self_in, f32[6,1536]{1,0:T(8,128)} %reshape.87.gains.gains_in, ...), custom_call_target="tpu_custom_call" | custom-call | tf_op jit(solution)/shard_map/cross/pallas_call | solution.py:775
  143.3 65.1 %feed.1 = (bf16[4,256,1536]{2,1,0:T(8,128)(2,1)}, bf16[256,1536]{1,0:T(8,128)(2,1)}, bf16[2,768,1536]{2,1,0:T(8,128)(2,1)}) custom-call(bf16[256,1536]{1,0:T(8,128)(2,1)} %get-tuple-element.64.rows_in, bf16[4,256,1536]{2,1,0:T(8,128)(2,1)} %get-tuple-element.65.grads_in, bf16[1536,1536]{1,0:T(8,128)(2,1)} %up_in.1, bf16[1536,1536]{1,0:T(8,128)(2,1)} %down_in.1), custom_call_target="tpu_custom_call" | custom-call | tf_op jit(solution)/shard_map/feed/pallas_call | solution.py:995
  208.5 38.2 %cross_back.1 = (f32[256,1536]{1,0:T(8,128)}, bf16[256,1536]{1,0:T(8,128)(2,1)}, f32[32,1536]{1,0:T(8,128)}, bf16[4,64,768]{2,1,0:T(8,128)(2,1)}, bf16[4,768,384...) custom-call(f32[256,1536]{1,0:T(8,128)} %bitcast.45, ...), custom_call_target="tpu_custom_call" | custom-call | tf_op jit(solution)/shard_map/cross_back/pallas_call | solution.py:1218
  246.7 119.5 %attend_back.1 = (f32[256,1536]{1,0:T(8,128)}, f32[16,1536]{1,0:T(8,128)}, f32[64,1536]{1,0:T(8,128)}, bf16[768,1152]{1,0:T(8,128)(2,1)}, bf16[12,48,1536]{2,1,0...) custom-call(bf16[256,1536]{1,0:T(8,128)(2,1)} %get-tuple-element.71., ...), custom_call_target="tpu_custom_call", output_to_operand_aliasing={{5}: (15, {})} | custom-call | tf_op jit(solution)/shard_map/attend_back/pallas_call | solution.py:1535
  366.2 122.7 %total.1 = (bf16[3,16,48,384]{3,2,1,0:T(8,128)(2,1)}, bf16[16,48,384]{2,1,0:T(8,128)(2,1)}, bf16[4,48,1536]{2,1,0:T(8,128)(2,1)}, bf16[4,48,1536]{2,1,0:T(8,128)...) custom-call(bf16[32,48,1536]{2,1,0:T(8,128)(2,1)} %bitcast.34, ...), custom_call_target="tpu_custom_call", output_to_operand_aliasing={{7}: (11, {}), {8}: (12, {}), {9}: (13, {})} | custom-call | tf_op jit(solution)/shard_map/total/pallas_call | solution.py:1781
  488.9 0.0 copy-start.2
  488.9 1.6 slice_reduce_fusion
  490.6 2.2 bitcast_convert_fusion.3
  492.8 0.0 copy-done.2
  492.8 2.3 reshape.110
  495.1 0.0 copy-done.6
  495.1 1.8 bitcast_convert_fusion.2
  496.9 0.1 copy-done.3
  497.0 2.2 convert_bitcast_fusion
  499.2 0.2 copy-done
  499.3 1.3 copy-done.1
  500.6 5.4 %bitcast_convert_fusion = (f32[768,1536]{1,0:T(8,128)}, f32[768,1536]{1,0:T(8,128)}) fusion(bf16[16,48,1536]{2,1,0:T(8,128)(2,1)S(1)} %copy-done, bf16[16,48,1536]{2,1,0:T(8,128)(2,1)S(1)} %copy-done.1), kind=kLoop, calls=%fused_computation.1 | loop fusion | flops 2359296 | bytes 14155776 | tf_op jit(solution)/shard_map/reshape | solution.py:1851
  506.0 1.1 copy.50
  507.1 0.8 copy-done.4
  508.0 1.1 copy.51
  509.1 0.1 copy-done.8
  509.2 0.7 copy.52
  (11 shorter events, 0.0 us)
Async XLA Ops:
  488.9 3.9 copy-start.2
  490.6 4.5 copy-start.6
  490.6 4.5 copy-start.7
  495.1 1.8 copy-start.3
  496.9 2.4 copy-start
  496.9 3.7 copy-start.1
  500.6 5.4 %copy-start.5 = (f32[256,1536]{1,0:T(8,128)S(1)}, f32[256,1536]{1,0:T(8,128)}, u32[]{:S(2)}) copy-start(f32[256,1536]{1,0:T(8,128)} %get-tuple-element.91) | copy-start | bytes 4718596
  506.0 2.0 copy-start.4
  508.0 1.2 copy-start.8

commit v5 on v4

--- a/solution.py
+++ b/solution.py
@@ -1453,6 +1453,7 @@
         own[layout.kv + c % half, :, cols(c // half, 2 * local)] = total.astype(BF)
 
     halves_kv.total(0, take_kv, chunk)
+    scatter.relay()
     tick(19)
 
     def grad_wqkv(j, carry):
@@ -1476,7 +1477,6 @@
         own[layout.out + here.start // chunk] = total.astype(BF)
 
     halves_out.total(0, take_out, chunk)
-    scatter.relay()
     tick(27)
 
     def take(here, total):
@@ -1628,7 +1628,7 @@
         pairs.append((feed_in.at[pl.ds(fresh, at_kv - fresh)], own.at[pl.ds(fresh, at_kv - fresh)]))
     early = len(pairs)
     pairs += [
-        (sums_a_in, sums_a), (sums_b_in, sums_b), (text_in, text), (cross_q_in, cross_q), (cross_o_in, cross_o),
+        (cross_q_in, cross_q), (cross_o_in, cross_o), (sums_a_in, sums_a), (sums_b_in, sums_b), (text_in, text),
         (part_in, part), (after_in, after),
     ]
     loads = [pltpu.make_async_copy(a, b, load.at[i]) for i, (a, b) in enumerate(pairs)]
@@ -1653,7 +1653,7 @@
     for copy in loads[1:early]:
         copy.wait()
     run(begin, begin + 1)
-    for copy in loads[early:]:
+    for copy in loads[early:-2]:
         copy.wait()
     share_width = m // subs
     for i in range(6):
@@ -1693,7 +1693,6 @@
     scatter_p = Scatter(part, land_p, stage_p, send, recv, base + 12)
     for each in (scatter_q, scatter_o):
         each.diagonal()
-    for each in (scatter_q, scatter_o):
         each.along_x()
         each.along_y()
 
@@ -1718,33 +1717,31 @@
     text_store.start()
     for copy in third:
         copy.start()
-    relay = max(begin + 6, begin + (at_cq - begin) // 2)
-    run(begin + 6, relay)
+    scatter_q.relay()
+    scatter_o.relay()
+    loads[-2].wait()
+    loads[-1].wait()
     scatter_p.diagonal()
     scatter_p.along_x()
     scatter_p.along_y()
-    for each in (scatter_q, scatter_o):
-        each.relay()
-    finish = at_cq
-    run(relay, finish)
+    run(begin + 6, at_cq)
 
     def take_q(rows, value):
         row = rows.start
-        part = row // (quarter * chunk)
-        c = row // chunk - part * quarter
-        own[at_cq + c, :, pl.ds(pl.multiple_of(part * local, local), local)] = value.astype(BF)
+        c = row // chunk
+        own[at_cq + c % quarter, :, cols(c // quarter, local)] = value.astype(BF)
 
     scatter_q.finish(take_q, chunk)
+    run(at_cq, at_co)
     step = min(chunk, scatter_o.half)
 
     def take_o(rows, value):
         own[at_co + rows.start // chunk, rows_at(rows.start % chunk // step, step)] = value.astype(BF)
 
     scatter_o.finish(take_o, step)
-    late = min(finish + 8, end)
-    run(finish, late)
+    run(at_co, layout.count)
     scatter_p.relay()
-    run(late, end)
+    run(layout.count, end)
 
     def take_layer(rows, value):
         after[rows] = after[rows] + value

time: 510 us -> 509 us (level)
  no operation moved by 1% of the time
where the time goes in v5:
time: 509 us
  Pallas kernels  479 us (94%)
  local copies, waits for them, and re-layouts  17.8 us (3%)
  other arithmetic  11.6 us (2%)
    pallas_call x1, Pallas kernels, total(): pl.pallas_call(partial(total_kernel, layout), name='total', out_shape=[sh...  121 us
    pallas_call x1, Pallas kernels, attend_back(): pl.pallas_call(partial(attend_back_kernel, layout), name='attend_back', o...  119 us
    pallas_call x1, Pallas kernels, attend(): pl.pallas_call(attend_kernel, name='attend', out_shape=[shape(4, n, local...  68.3 us
    pallas_call x1, Pallas kernels, feed(): pl.pallas_call(feed_kernel, name='feed', out_shape=[shape(4, n, m), shape...  65.1 us
    pallas_call x1, Pallas kernels, cross_back(): pl.pallas_call(partial(cross_back_kernel, layout), name='cross_back', out...  38.2 us
    pallas_call x1, Pallas kernels, enter(): pl.pallas_call(enter_kernel, name='enter', out_shape=[shape(4, n, m), sha...  36.8 us
    pallas_call x1, Pallas kernels, cross(): pl.pallas_call(cross_kernel, name='cross', out_shape=[shape(n, m), shape(...  29.2 us
    unnamed x27, local copies, waits for them, and re-layouts  12.5 us

profile of v5, /device:TPU:0, one launch (start us, length us, event | category | flops | bytes accessed | tf_op | source)
XLA Modules:
  0.0 508.7 jit_solution(7326246219756861280)
XLA Ops:
  0.7 0.7 constant_dynamic-update-slice_fusion.5
  1.4 0.7 constant_dynamic-update-slice_fusion.4
  2.1 0.7 constant_dynamic-update-slice_fusion.3
  2.8 0.7 constant_dynamic-update-slice_fusion.2
  3.5 0.7 constant_dynamic-update-slice_fusion.1
  4.2 0.7 constant_dynamic-update-slice_fusion
  4.9 0.6 reshape.87.gains.gains_in
  5.5 3.5 copy.36
  9.0 36.8 %enter.1 = (bf16[4,256,1536]{2,1,0:T(8,128)(2,1)}, bf16[4,256,1152]{2,1,0:T(8,128)(2,1)}, bf16[4,64,768]{2,1,0:T(8,128)(2,1)}) custom-call(bf16[256,1536]{1,0:T(8,128)(2,1)} %bitcast.41, f32[6,1536]{1,0:T(8,128)} %reshape.87.gains.gains_in, bf16[3,1536,384]{2,1,0:T(8,128)(2,1)} %bitcast.39, bf16[64,1536]{1,0:T(8,128)(2,1)} %bitcast.50, ...), custom_call_target="tpu_custom_call" | custom-call | tf_op jit(solution)/shard_map/enter/pallas_call | solution.py:465
  45.9 68.3 %attend.1 = (bf16[4,256,384]{2,1,0:T(8,128)(2,1)}, f32[4,256,128]{2,1,0:T(8,128)}, f32[256,1536]{1,0:T(8,128)}, bf16[4,1536,384]{2,1,0:T(8,128)(2,1)}, bf16[4,384,1536]{2,1,0:T(8,128)(2,1)}) custom-call(bf16[4,256,1152]{2,1,0:T(8,128)(2,1)} %get-tuple-element.59.triple_in, bf16[384,1536]{1,0:T(8,128)(2,1)} %out_in.3, bf16[256,1536]{1,0:T(8,128)(2,1)} %bitcast.42, ...), custom_call_target="tpu_custom_call" | custom-call | tf_op jit(solution)/shard_map/attend/pallas_call | solution.py:642
  114.2 29.2 %cross.1 = (bf16[256,1536]{1,0:T(8,128)(2,1)}, bf16[256,1536]{1,0:T(8,128)(2,1)}, f32[256,1536]{1,0:T(8,128)}, bf16[256,1536]{1,0:T(8,128)(2,1)}, bf16[4,256,1536]{2,1,0:T(8,128)(2,1)}) custom-call(f32[256,1536]{1,0:T(8,128)} %get-tuple-element.60.after_in.self_in, f32[6,1536]{1,0:T(8,128)} %reshape.87.gains.gains_in, ...), custom_call_target="tpu_custom_call" | custom-call | tf_op jit(solution)/shard_map/cross/pallas_call | solution.py:775
  143.3 65.1 %feed.1 = (bf16[4,256,1536]{2,1,0:T(8,128)(2,1)}, bf16[256,1536]{1,0:T(8,128)(2,1)}, bf16[2,768,1536]{2,1,0:T(8,128)(2,1)}) custom-call(bf16[256,1536]{1,0:T(8,128)(2,1)} %get-tuple-element.64.rows_in, bf16[4,256,1536]{2,1,0:T(8,128)(2,1)} %get-tuple-element.65.grads_in, bf16[1536,1536]{1,0:T(8,128)(2,1)} %up_in.1, bf16[1536,1536]{1,0:T(8,128)(2,1)} %down_in.1), custom_call_target="tpu_custom_call" | custom-call | tf_op jit(solution)/shard_map/feed/pallas_call | solution.py:995
  208.5 38.2 %cross_back.1 = (f32[256,1536]{1,0:T(8,128)}, bf16[256,1536]{1,0:T(8,128)(2,1)}, f32[32,1536]{1,0:T(8,128)}, bf16[4,64,768]{2,1,0:T(8,128)(2,1)}, bf16[4,768,384...) custom-call(f32[256,1536]{1,0:T(8,128)} %bitcast.45, ...), custom_call_target="tpu_custom_call" | custom-call | tf_op jit(solution)/shard_map/cross_back/pallas_call | solution.py:1218
  246.7 119.5 %attend_back.1 = (f32[256,1536]{1,0:T(8,128)}, f32[16,1536]{1,0:T(8,128)}, f32[64,1536]{1,0:T(8,128)}, bf16[768,1152]{1,0:T(8,128)(2,1)}, bf16[12,48,1536]{2,1,0...) custom-call(bf16[256,1536]{1,0:T(8,128)(2,1)} %get-tuple-element.71., ...), custom_call_target="tpu_custom_call", output_to_operand_aliasing={{5}: (15, {})} | custom-call | tf_op jit(solution)/shard_map/attend_back/pallas_call | solution.py:1535
  366.2 121.5 %total.1 = (bf16[3,16,48,384]{3,2,1,0:T(8,128)(2,1)}, bf16[16,48,384]{2,1,0:T(8,128)(2,1)}, bf16[4,48,1536]{2,1,0:T(8,128)(2,1)}, bf16[4,48,1536]{2,1,0:T(8,128)...) custom-call(bf16[32,48,1536]{2,1,0:T(8,128)(2,1)} %bitcast.34, ...), custom_call_target="tpu_custom_call", output_to_operand_aliasing={{7}: (11, {}), {8}: (12, {}), {9}: (13, {})} | custom-call | tf_op jit(solution)/shard_map/total/pallas_call | solution.py:1778
  487.7 0.0 copy-start.2
  487.7 1.6 slice_reduce_fusion
  489.3 2.2 bitcast_convert_fusion.3
  491.6 0.0 copy-done.2
  491.6 2.3 reshape.110
  493.8 0.0 copy-done.6
  493.8 1.8 bitcast_convert_fusion.2
  495.6 0.1 copy-done.3
  495.7 2.2 convert_bitcast_fusion
  497.9 0.2 copy-done
  498.1 1.3 copy-done.1
  499.3 5.4 %bitcast_convert_fusion = (f32[768,1536]{1,0:T(8,128)}, f32[768,1536]{1,0:T(8,128)}) fusion(bf16[16,48,1536]{2,1,0:T(8,128)(2,1)S(1)} %copy-done, bf16[16,48,1536]{2,1,0:T(8,128)(2,1)S(1)} %copy-done.1), kind=kLoop, calls=%fused_computation.1 | loop fusion | flops 2359296 | bytes 14155776 | tf_op jit(solution)/shard_map/reshape | solution.py:1848
  504.7 1.1 copy.50
  505.9 0.8 copy-done.4
  506.7 1.1 copy.51
  507.8 0.1 copy-done.8
  507.9 0.7 copy.52
  (11 shorter events, 0.0 us)
Async XLA Ops:
  487.7 3.9 copy-start.2
  489.3 4.5 copy-start.6
  489.3 4.5 copy-start.7
  493.8 1.8 copy-start.3
  495.7 2.4 copy-start
  495.7 3.7 copy-start.1
  499.3 5.4 %copy-start.5 = (f32[256,1536]{1,0:T(8,128)S(1)}, f32[256,1536]{1,0:T(8,128)}, u32[]{:S(2)}) copy-start(f32[256,1536]{1,0:T(8,128)} %get-tuple-element.91) | copy-start | bytes 4718596
  504.7 2.0 copy-start.4
  506.7 1.2 copy-start.8

commit v6 on v5

--- a/solution.py
+++ b/solution.py
@@ -194,7 +194,7 @@
     return jax.ShapeDtypeStruct(dims, kind)
 
 
-LAG = 3
+LAG = 2
 RING = 4
 
 
@@ -239,14 +239,24 @@
 
                 @pl.when(place > 0)
                 def _():
-                    before = self.land[way, c % self.window].astype(F32)
-                    self.ring[way, c % RING] = (self.own[c].astype(F32) + before).astype(BF)
+                    self.fill(self.ring.at[way, c % RING], (self.own.at[c], self.land.at[way, c % self.window]))
 
                 @pl.when(place == 0)
                 def _():
-                    self.ring[way, c % RING] = self.own[c]
+                    self.fill(self.ring.at[way, c % RING], (self.own.at[c],))
 
                 self.copy(way, c).start()
+
+    def fill(self, target, terms):
+        def block(i, carry):
+            here = rows_at(i, 48)
+            value = terms[0][here].astype(F32)
+            for term in terms[1:]:
+                value = value + term[here].astype(F32)
+            target[here] = value.astype(BF)
+            return carry
+
+        lax.fori_loop(0, target.shape[0] // 48, block, 0)
 
     def finished(self, k):
         far = jnp.maximum(self.g, self.n - 1 - self.g)
@@ -263,21 +273,20 @@
             def _():
                 self.outputs(f - RING, self.result.at[f % RING], self.store, lambda copy: copy.wait())
 
-            mine = self.own[f].astype(F32)
             slot, held = f % RING, f % self.window
+            mine, target = self.own.at[f], self.result.at[slot]
 
             @pl.when(either(self.g > 0, self.g < self.n - 1))
             def _():
-                both = self.land[0, held].astype(F32) + self.land[1, held].astype(F32)
-                self.result[slot] = (mine + both).astype(BF)
+                self.fill(target, (mine, self.land.at[0, held], self.land.at[1, held]))
 
             @pl.when(self.g == 0)
             def _():
-                self.result[slot] = (mine + self.land[1, held].astype(F32)).astype(BF)
+                self.fill(target, (mine, self.land.at[1, held]))
 
             @pl.when(self.g == self.n - 1)
             def _():
-                self.result[slot] = (mine + self.land[0, held].astype(F32)).astype(BF)
+                self.fill(target, (mine, self.land.at[0, held]))
 
             self.outputs(f, self.result.at[slot], self.store, lambda copy: copy.start())
 
@@ -309,7 +318,7 @@
                 self.outputs(f, self.result.at[f % RING], self.store, lambda copy: copy.wait())
 
 
-KV_TICKS, OUT_TICKS = 20, 28
+KV_TICKS, OUT_TICKS = 10, 14
 
 
 class Layout:
@@ -317,7 +326,7 @@
         piece = m // subs
         self.m, self.piece, self.local = m, piece, local
         self.out_rows = local // subs
-        self.chunk = 48
+        self.chunk = 96 if piece % 384 == 0 and self.out_rows % 96 == 0 else 48
         quarter = piece // 4 // self.chunk
         self.quarter = quarter
         self.feed_count = 2 * piece // self.chunk
@@ -327,9 +336,9 @@
         self.cq = self.qkv + 3 * quarter
         self.co = self.cq + quarter
         self.count = self.co + self.out_rows // self.chunk
-        self.window = LAG * (groups + 1)
+        self.window = LAG * groups
         self.end = self.count + LAG * (groups - 1)
-        self.middle = min(12, self.feed_count // 3)
+        self.middle = min(6, self.feed_count // 2 - 2)
         self.later = self.feed_count
         if self.middle + KV_TICKS <= self.kv and self.middle + OUT_TICKS <= self.out:
             self.later = self.middle + OUT_TICKS + 2
@@ -1095,12 +1104,15 @@
     def tick(k):
         @pl.when(k < middle)
         def _():
-            pump.step(k)
+            pump.step(jnp.int32(k))
 
     tick(jnp.int32(1))
 
     def quarter(q, carry):
-        tick(q + 2)
+        @pl.when(q % 2 == 1)
+        def _():
+            tick(2 + q // 2)
+
         grad_heads = dot_t(branch[...], wo[rows_at(q, width)]).astype(BF)
         whole_q_cols = cols(q, width)
         query_grad_block = []
@@ -1129,10 +1141,6 @@
     halves_o = Halves(whole_o, land_o, send, recv, 4 * (subs - 1))
 
     def weights(q, carry):
-        @pl.when(q % 2 == 0)
-        def _():
-            tick(6 + q // 2)
-
 
         def grad_o(j, carry):
             whole_o[q, :, cols(j, 512)] = dot_c(flat[:, cols(q, width)], branch[:, cols(j, 512)]).astype(BF)
@@ -1153,11 +1161,9 @@
         halves_o.start(q)
     loads[9].wait()
 
+    tick(4)
+
     def norm_grad(j, carry):
-        @pl.when(j % 3 == 0)
-        def _():
-            tick(8 + j // 3)
-
         here = rows_at(j, 256)
         total = jnp.zeros((n, 256), F32)
         for q in range(4):
@@ -1187,7 +1193,7 @@
     for copy in stores[1:]:
         copy.start()
 
-    tick(jnp.int32(10))
+    tick(5)
     for halves, piece in ((halves_q, piece_q), (halves_o, piece_o)):
         for q in range(4):
 
@@ -1198,7 +1204,6 @@
     stores += [pltpu.make_async_copy(piece_q, o_wq, store.at[4]), pltpu.make_async_copy(piece_o, o_wo, store.at[5])]
     for copy in stores[4:]:
         copy.start()
-    tick(jnp.int32(11))
     pump.drain()
     stores.append(pltpu.make_async_copy(land, o_land, store.at[6]))
     stores[-1].start()
@@ -1310,7 +1315,7 @@
     def tick(k):
         @pl.when(k + first < last)
         def _():
-            pump.step(k + first)
+            pump.step(jnp.int32(k + first))
 
     n, m = grad_out.shape
     width = triple.shape[2]
@@ -1366,7 +1371,12 @@
         deltas[place] = lax.fori_loop(0, heads // 2, delta, jnp.zeros((n, 128), F32))
 
         def pair(p, carry):
-            tick(i * (heads // 2) + p)
+            turns = i * (heads // 2) + p
+
+            @pl.when(turns % 2 == 0)
+            def _():
+                tick(turns // 2)
+
             for blocks in range(1, 5):
 
                 @pl.when(place == blocks - 1)
@@ -1401,7 +1411,10 @@
             return carry
 
         lax.fori_loop(0, m // 512, step, 0)
-        tick(12 + i)
+
+        @pl.when(i % 2 == 0)
+        def _():
+            tick(6 + i // 2)
 
         @pl.when(i == 0)
         def _():
@@ -1418,7 +1431,7 @@
         return carry
 
     lax.fori_loop(0, 4, back, 0)
-    tick(16)
+    tick(8)
     scatter_m.relay()
 
     def take_m(here, total):
@@ -1435,7 +1448,6 @@
 
     lax.fori_loop(0, m // 384, grad_kv, 0)
     halves_kv.start(0)
-    tick(17)
 
     def grad_wout(j, carry):
         whole_out[0, :, cols(j, 512)] = dot_c(
@@ -1445,7 +1457,7 @@
 
     lax.fori_loop(0, m // 512, grad_wout, 0)
     halves_out.start(0)
-    tick(18)
+    tick(9)
     chunk, half = layout.chunk, 2 * layout.quarter
 
     def take_kv(here, total):
@@ -1454,10 +1466,12 @@
 
     halves_kv.total(0, take_kv, chunk)
     scatter.relay()
-    tick(19)
 
     def grad_wqkv(j, carry):
-        tick(20 + j)
+        @pl.when(j % 2 == 0)
+        def _():
+            tick(10 + j // 2)
+
         turned = rows[:, :, cols(j, 256)].reshape(4 * n, 256)
 
         def inner(i, carry):
@@ -1471,13 +1485,12 @@
 
     lax.fori_loop(0, m // 256, grad_wqkv, 0)
     halves_qkv.start(0)
-    tick(26)
+    tick(13)
 
     def take_out(here, total):
         own[layout.out + here.start // chunk] = total.astype(BF)
 
     halves_out.total(0, take_out, chunk)
-    tick(27)
 
     def take(here, total):
         land_qkv[0, 0, here] = total.astype(BF)
@@ -1487,7 +1500,7 @@
     stores.append(pltpu.make_async_copy(own.at[pl.ds(layout.kv, layout.qkv - layout.kv)], o_more, store.at[2]))
     for copy in stores[-2:]:
         copy.start()
-    tick(28)
+    tick(14)
     for copy in loads[14:]:
         copy.wait()
 
@@ -1505,7 +1518,7 @@
 
     zero = jnp.zeros((8, m), F32)
     gain_sum, bias_sum = lax.fori_loop(0, n // 64, frame_block, (zero, zero))
-    tick(29)
+    tick(15)
     sums_out[0:8] = gain_sum
     sums_out[8:16] = bias_sum
     stores += [pltpu.make_async_copy(grad_out, o_frames, store.at[3]), pltpu.make_async_copy(sums_out, o_sums, store.at[4])]
@@ -1696,7 +1709,7 @@
         each.along_x()
         each.along_y()
 
-    run(begin + 1, begin + 3)
+    run(begin + 1, begin + 2)
     for copy in first:
         copy.wait_recv()
     for j in range(subs):
@@ -1706,7 +1719,7 @@
         copy.wait_send()
     for copy in second:
         copy.start()
-    run(begin + 3, begin + 6)
+    run(begin + 2, begin + 3)
     for copy in second:
         copy.wait_recv()
     total = share[0, s]
@@ -1724,7 +1737,7 @@
     scatter_p.diagonal()
     scatter_p.along_x()
     scatter_p.along_y()
-    run(begin + 6, at_cq)
+    run(begin + 3, at_cq)
 
     def take_q(rows, value):
         row = rows.start

time: 509 us -> 508 us (level)
    pallas_call x1, Pallas kernels: 38.2 us -> 46.1 us  [cross_back(): pl.pallas_call(partial(cross_back_kernel, layout), name='cross_back', out...]
    pallas_call x1, Pallas kernels: 121 us -> 115 us  [total(): pl.pallas_call(partial(total_kernel, layout), name='total', out_shape=[sh...]
where the time goes in v6:
time: 508 us; the launch traced here: 507 us
  Pallas kernels  477 us (94%)
  local copies, waits for them, and re-layouts  17.8 us (4%)
  other arithmetic  11.6 us (2%)
    pallas_call x1, Pallas kernels, attend_back(): pl.pallas_call(partial(attend_back_kernel, layout), name='attend_back', o...  117 us
    pallas_call x1, Pallas kernels, total(): pl.pallas_call(partial(total_kernel, layout), name='total', out_shape=[sh...  115 us
    pallas_call x1, Pallas kernels, attend(): pl.pallas_call(attend_kernel, name='attend', out_shape=[shape(4, n, local...  68.3 us
    pallas_call x1, Pallas kernels, feed(): pl.pallas_call(feed_kernel, name='feed', out_shape=[shape(4, n, m), shape...  65.1 us
    pallas_call x1, Pallas kernels, cross_back(): pl.pallas_call(partial(cross_back_kernel, layout), name='cross_back', out...  46.1 us
    pallas_call x1, Pallas kernels, enter(): pl.pallas_call(enter_kernel, name='enter', out_shape=[shape(4, n, m), sha...  36.8 us
    pallas_call x1, Pallas kernels, cross(): pl.pallas_call(cross_kernel, name='cross', out_shape=[shape(n, m), shape(...  29.2 us
    unnamed x27, local copies, waits for them, and re-layouts  12.5 us

profile of v6, /device:TPU:0, one launch (start us, length us, event | category | flops | bytes accessed | tf_op | source)
XLA Modules:
  0.0 507.3 jit_solution(5432815674515537005)
XLA Ops:
  0.7 0.7 constant_dynamic-update-slice_fusion.5
  1.4 0.7 constant_dynamic-update-slice_fusion.4
  2.1 0.7 constant_dynamic-update-slice_fusion.3
  2.8 0.7 constant_dynamic-update-slice_fusion.2
  3.5 0.7 constant_dynamic-update-slice_fusion.1
  4.2 0.7 constant_dynamic-update-slice_fusion
  4.9 0.6 reshape.87.gains.gains_in
  5.5 3.5 copy.36
  9.0 36.8 %enter.1 = (bf16[4,256,1536]{2,1,0:T(8,128)(2,1)}, bf16[4,256,1152]{2,1,0:T(8,128)(2,1)}, bf16[4,64,768]{2,1,0:T(8,128)(2,1)}) custom-call(bf16[256,1536]{1,0:T(8,128)(2,1)} %bitcast.41, f32[6,1536]{1,0:T(8,128)} %reshape.87.gains.gains_in, bf16[3,1536,384]{2,1,0:T(8,128)(2,1)} %bitcast.39, bf16[64,1536]{1,0:T(8,128)(2,1)} %bitcast.50, ...), custom_call_target="tpu_custom_call" | custom-call | tf_op jit(solution)/shard_map/enter/pallas_call | solution.py:474
  45.9 68.3 %attend.1 = (bf16[4,256,384]{2,1,0:T(8,128)(2,1)}, f32[4,256,128]{2,1,0:T(8,128)}, f32[256,1536]{1,0:T(8,128)}, bf16[4,1536,384]{2,1,0:T(8,128)(2,1)}, bf16[4,384,1536]{2,1,0:T(8,128)(2,1)}) custom-call(bf16[4,256,1152]{2,1,0:T(8,128)(2,1)} %get-tuple-element.59.triple_in, bf16[384,1536]{1,0:T(8,128)(2,1)} %out_in.3, bf16[256,1536]{1,0:T(8,128)(2,1)} %bitcast.42, ...), custom_call_target="tpu_custom_call" | custom-call | tf_op jit(solution)/shard_map/attend/pallas_call | solution.py:651
  114.2 29.2 %cross.1 = (bf16[256,1536]{1,0:T(8,128)(2,1)}, bf16[256,1536]{1,0:T(8,128)(2,1)}, f32[256,1536]{1,0:T(8,128)}, bf16[256,1536]{1,0:T(8,128)(2,1)}, bf16[4,256,1536]{2,1,0:T(8,128)(2,1)}) custom-call(f32[256,1536]{1,0:T(8,128)} %get-tuple-element.60.after_in.self_in, f32[6,1536]{1,0:T(8,128)} %reshape.87.gains.gains_in, ...), custom_call_target="tpu_custom_call" | custom-call | tf_op jit(solution)/shard_map/cross/pallas_call | solution.py:784
  143.4 65.1 %feed.1 = (bf16[4,256,1536]{2,1,0:T(8,128)(2,1)}, bf16[256,1536]{1,0:T(8,128)(2,1)}, bf16[2,768,1536]{2,1,0:T(8,128)(2,1)}) custom-call(bf16[256,1536]{1,0:T(8,128)(2,1)} %get-tuple-element.64.rows_in, bf16[4,256,1536]{2,1,0:T(8,128)(2,1)} %get-tuple-element.65.grads_in, bf16[1536,1536]{1,0:T(8,128)(2,1)} %up_in.1, bf16[1536,1536]{1,0:T(8,128)(2,1)} %down_in.1), custom_call_target="tpu_custom_call" | custom-call | tf_op jit(solution)/shard_map/feed/pallas_call | solution.py:1004
  208.5 46.1 %cross_back.1 = (f32[256,1536]{1,0:T(8,128)}, bf16[256,1536]{1,0:T(8,128)(2,1)}, f32[32,1536]{1,0:T(8,128)}, bf16[4,64,768]{2,1,0:T(8,128)(2,1)}, bf16[4,768,384...) custom-call(f32[256,1536]{1,0:T(8,128)} %bitcast.45, ...), custom_call_target="tpu_custom_call" | custom-call | tf_op jit(solution)/shard_map/cross_back/pallas_call | solution.py:1223
  254.6 116.8 %attend_back.1 = (f32[256,1536]{1,0:T(8,128)}, f32[16,1536]{1,0:T(8,128)}, f32[64,1536]{1,0:T(8,128)}, bf16[768,1152]{1,0:T(8,128)(2,1)}, bf16[6,96,1536]{2,1,0:...) custom-call(bf16[256,1536]{1,0:T(8,128)(2,1)} %get-tuple-element.71., ...), custom_call_target="tpu_custom_call", output_to_operand_aliasing={{5}: (15, {})} | custom-call | tf_op jit(solution)/shard_map/attend_back/pallas_call | solution.py:1548
  371.4 114.9 %total.1 = (bf16[3,8,96,384]{3,2,1,0:T(8,128)(2,1)}, bf16[8,96,384]{2,1,0:T(8,128)(2,1)}, bf16[2,96,1536]{2,1,0:T(8,128)(2,1)}, bf16[2,96,1536]{2,1,0:T(8,128)(2...) custom-call(bf16[16,96,1536]{2,1,0:T(8,128)(2,1)} %bitcast.34, ...), custom_call_target="tpu_custom_call", output_to_operand_aliasing={{7}: (11, {}), {8}: (12, {}), {9}: (13, {})} | custom-call | tf_op jit(solution)/shard_map/total/pallas_call | solution.py:1791
  486.3 0.0 copy-start.2
  486.3 1.6 slice_reduce_fusion
  488.0 2.2 bitcast_convert_fusion.3
  490.2 0.0 copy-done.2
  490.2 2.3 reshape.110
  492.5 0.0 copy-done.6
  492.5 1.8 bitcast_convert_fusion.2
  494.3 0.1 copy-done.3
  494.3 2.2 convert_bitcast_fusion
  496.5 0.2 copy-done
  496.7 1.3 copy-done.1
  498.0 5.4 %bitcast_convert_fusion = (f32[768,1536]{1,0:T(8,128)}, f32[768,1536]{1,0:T(8,128)}) fusion(bf16[8,96,1536]{2,1,0:T(8,128)(2,1)S(1)} %copy-done, bf16[8,96,1536]{2,1,0:T(8,128)(2,1)S(1)} %copy-done.1), kind=kLoop, calls=%fused_computation.1 | loop fusion | flops 2359296 | bytes 14155776 | tf_op jit(solution)/shard_map/reshape | solution.py:1861
  503.4 1.1 copy.50
  504.5 0.8 copy-done.4
  505.3 1.1 copy.51
  506.5 0.1 copy-done.8
  506.6 0.7 copy.52
  (11 shorter events, 0.0 us)
Async XLA Ops:
  486.3 3.9 copy-start.2
  488.0 4.5 copy-start.6
  488.0 4.5 copy-start.7
  492.5 1.8 copy-start.3
  494.3 2.4 copy-start
  494.3 3.7 copy-start.1
  498.0 5.4 %copy-start.5 = (f32[256,1536]{1,0:T(8,128)S(1)}, f32[256,1536]{1,0:T(8,128)}, u32[]{:S(2)}) copy-start(f32[256,1536]{1,0:T(8,128)} %get-tuple-element.91) | copy-start | bytes 4718596
  503.4 2.0 copy-start.4
  505.3 1.2 copy-start.8

commit v7 on v6

--- a/solution.py
+++ b/solution.py
@@ -529,6 +529,7 @@
     t, x, y, d = neighbours()
     s = lax.axis_index("sub")
     subs = lax.axis_size("sub")
+    g, groups = lax.axis_index("group"), lax.axis_size("group")
     n = triple.shape[1]
     m = v_out.shape[1]
     heads = v_out.shape[0] // HEAD
@@ -543,18 +544,25 @@
     greet(
         [{"tensor": x}, {"tensor": y}]
         + [{"sub": (s + k) % subs} for k in range(1, subs)]
+        + [{"group": (g + k) % groups} for k in range(1, groups)]
     )
     scatter = Scatter(part, land, stage, send, recv, 0)
     gathers = []
     for i, (weight, full) in enumerate(((wq, o_wq), (wo, o_wo))):
         piece = weight.shape[0] // subs
-        first, second = split(piece)
+        strips = groups if i == 0 and piece % (32 * groups) == 0 else 1
+        strip = piece // strips
+        first, second = split(strip)
         offset = pl.multiple_of(s * piece, piece)
+        begin = pl.multiple_of(offset + (g * strip if strips > 1 else 0), strip)
         halves = (
-            pl.ds(offset, first.size),
-            pl.ds(pl.multiple_of(offset + first.size, 16), second.size),
+            pl.ds(begin, first.size),
+            pl.ds(pl.multiple_of(begin + first.size, 16), second.size),
         )
         gathers.append((Gather(weight, full, send, recv, 6 + 6 * i, halves), full, pl.ds(offset, piece)))
+        if i == 0:
+            mine = pl.ds(begin, strip)
+            spread = [(j, k) for j in range(3) for k in range(1, groups)] if strips > 1 else []
 
     def shared(i, j, k):
         _, full, piece = gathers[i]
@@ -566,8 +574,16 @@
             device_id={"sub": (s + k) % subs}, device_id_type=MESH,
         )
 
-    for gather, _, _ in gathers:
-        gather.start()
+    def stripped(j, k):
+        place = (x, y, d)[j]
+        slot = 18 + 6 * (subs - 1) + j * (groups - 1) + k - 1
+        return pltpu.make_async_remote_copy(
+            o_wq.at[place, mine], o_wq.at[place, mine], send.at[slot], recv.at[slot],
+            device_id={"group": (g + k) % groups}, device_id_type=MESH,
+        )
+
+    (query_gather, _, _), (out_gather, _, _) = gathers
+    query_gather.start()
     for copy in loads[:2]:
         copy.wait()
 
@@ -575,6 +591,21 @@
         far_y = 1 - i // 2
         far_x = 1 - i % 2
         place = (t // 2 + far_y - 2 * (t // 2) * far_y) * 2 + (t % 2 + far_x - 2 * (t % 2) * far_x)
+
+        @pl.when(i == 1)
+        def _():
+            query_gather.relay_x()
+            query_gather.relay_y()
+            out_gather.start()
+
+        @pl.when(i == 2)
+        def _():
+            query_gather.have_x()
+            query_gather.have_y()
+            query_gather.have_d()
+            for j, k in spread:
+                stripped(j, k).start()
+
         for blocks in range(1, 5):
 
             @pl.when(place == blocks - 1)
@@ -602,9 +633,8 @@
         return carry
 
     lax.fori_loop(0, 4, one, 0)
-    for gather, _, _ in gathers:
-        gather.relay_x()
-        gather.relay_y()
+    out_gather.relay_x()
+    out_gather.relay_y()
     stores = [
         pltpu.make_async_copy(flat, o_flat, store.at[0]),
         pltpu.make_async_copy(sums, o_sums, store.at[1]),
@@ -618,13 +648,6 @@
     for copy in stores:
         copy.start()
     scatter.relay()
-    for i, (gather, _, _) in enumerate(gathers):
-        gather.have_x()
-        gather.have_y()
-        gather.have_d()
-        for j in range(3):
-            for k in range(1, subs):
-                shared(i, j, k).start()
     loads[2].wait()
 
     def take(rows, total):
@@ -633,7 +656,20 @@
     scatter.finish(take, 64)
     last = pltpu.make_async_copy(after, o_after, store.at[4])
     last.start()
+    out_gather.have_x()
+    out_gather.have_y()
+    out_gather.have_d()
+    for j in range(3):
+        for k in range(1, subs):
+            shared(1, j, k).start()
+    for j, k in spread:
+        stripped(j, k).wait_recv()
+    for j in range(3):
+        for k in range(1, subs):
+            shared(0, j, k).start()
     scatter.drain()
+    for j, k in spread:
+        stripped(j, k).wait_send()
     for i, (gather, _, _) in enumerate(gathers):
         gather.drain()
         for j in range(3):
@@ -644,10 +680,10 @@
     last.wait()
 
 
-def attend(triple, out, frames, wq, wo, subs):
+def attend(triple, out, frames, wq, wo, subs, groups):
     _, n, width = triple.shape
     local, m = out.shape
-    extra = 18 + 6 * (subs - 1)
+    extra = 18 + 6 * (subs - 1) + 3 * (groups - 1)
     return pl.pallas_call(
         attend_kernel,
         name="attend",
@@ -1825,7 +1861,7 @@
     kv = crosskv.reshape(m, 2 * width)
     gains = jnp.concatenate([crossgain, crossbias, feedgain, feedbias, selfgain, selfbias]).reshape(6, m)
     rows, triple, memory = enter(frames[0], gains, qkv, text_states[0], kv)
-    flat, sums, after_self, wq, wo = attend(triple, selfout, frames[0], crossquery, crossout, subs)
+    flat, sums, after_self, wq, wo = attend(triple, selfout, frames[0], crossquery, crossout, subs, groups)
     wo = wo.reshape(4 * width, m)
     query, cross_flat, after_cross, feed_rows, grads = cross(after_self, gains, wq, wo, memory, cotangent[0])
     layout = Layout(m, width, subs, groups)

time: 508 us -> 502 us (0.988)
  Pallas kernels: 477 us -> 471 us
    pallas_call x1, Pallas kernels: 68.3 us -> 61.6 us  [attend(): pl.pallas_call(attend_kernel, name='attend', out_shape=[shape(4, n, local...]
where the time goes in v7:
time: 502 us; the launch traced here: 501 us
  Pallas kernels  471 us (94%)
  local copies, waits for them, and re-layouts  17.8 us (4%)
  other arithmetic  11.6 us (2%)
    pallas_call x1, Pallas kernels, attend_back(): pl.pallas_call(partial(attend_back_kernel, layout), name='attend_back', o...  116 us
    pallas_call x1, Pallas kernels, total(): pl.pallas_call(partial(total_kernel, layout), name='total', out_shape=[sh...  115 us
    pallas_call x1, Pallas kernels, feed(): pl.pallas_call(feed_kernel, name='feed', out_shape=[shape(4, n, m), shape...  65.7 us
    pallas_call x1, Pallas kernels, attend(): pl.pallas_call(attend_kernel, name='attend', out_shape=[shape(4, n, local...  61.6 us
    pallas_call x1, Pallas kernels, cross_back(): pl.pallas_call(partial(cross_back_kernel, layout), name='cross_back', out...  44.9 us
    pallas_call x1, Pallas kernels, enter(): pl.pallas_call(enter_kernel, name='enter', out_shape=[shape(4, n, m), sha...  36.8 us
    pallas_call x1, Pallas kernels, cross(): pl.pallas_call(cross_kernel, name='cross', out_shape=[shape(n, m), shape(...  30.6 us
    unnamed x27, local copies, waits for them, and re-layouts  12.5 us

profile of v7, /device:TPU:0, one launch (start us, length us, event | category | flops | bytes accessed | tf_op | source)
XLA Modules:
  0.0 501.2 jit_solution(10506076916585911781)
XLA Ops:
  0.7 0.7 constant_dynamic-update-slice_fusion.5
  1.4 0.7 constant_dynamic-update-slice_fusion.4
  2.1 0.7 constant_dynamic-update-slice_fusion.3
  2.8 0.7 constant_dynamic-update-slice_fusion.2
  3.5 0.7 constant_dynamic-update-slice_fusion.1
  4.2 0.7 constant_dynamic-update-slice_fusion
  4.9 0.6 reshape.87.gains.gains_in
  5.5 3.5 copy.36
  9.0 36.8 %enter.1 = (bf16[4,256,1536]{2,1,0:T(8,128)(2,1)}, bf16[4,256,1152]{2,1,0:T(8,128)(2,1)}, bf16[4,64,768]{2,1,0:T(8,128)(2,1)}) custom-call(bf16[256,1536]{1,0:T(8,128)(2,1)} %bitcast.41, f32[6,1536]{1,0:T(8,128)} %reshape.87.gains.gains_in, bf16[3,1536,384]{2,1,0:T(8,128)(2,1)} %bitcast.39, bf16[64,1536]{1,0:T(8,128)(2,1)} %bitcast.50, ...), custom_call_target="tpu_custom_call" | custom-call | tf_op jit(solution)/shard_map/enter/pallas_call | solution.py:474
  45.9 61.6 %attend.1 = (bf16[4,256,384]{2,1,0:T(8,128)(2,1)}, f32[4,256,128]{2,1,0:T(8,128)}, f32[256,1536]{1,0:T(8,128)}, bf16[4,1536,384]{2,1,0:T(8,128)(2,1)}, bf16[4,384,1536]{2,1,0:T(8,128)(2,1)}) custom-call(bf16[4,256,1152]{2,1,0:T(8,128)(2,1)} %get-tuple-element.59.triple_in, bf16[384,1536]{1,0:T(8,128)(2,1)} %out_in.3, bf16[256,1536]{1,0:T(8,128)(2,1)} %bitcast.42, ...), custom_call_target="tpu_custom_call" | custom-call | tf_op jit(solution)/shard_map/attend/pallas_call | solution.py:687
  107.5 30.6 %cross.1 = (bf16[256,1536]{1,0:T(8,128)(2,1)}, bf16[256,1536]{1,0:T(8,128)(2,1)}, f32[256,1536]{1,0:T(8,128)}, bf16[256,1536]{1,0:T(8,128)(2,1)}, bf16[4,256,1536]{2,1,0:T(8,128)(2,1)}) custom-call(f32[256,1536]{1,0:T(8,128)} %get-tuple-element.60.after_in.self_in, f32[6,1536]{1,0:T(8,128)} %reshape.87.gains.gains_in, ...), custom_call_target="tpu_custom_call" | custom-call | tf_op jit(solution)/shard_map/cross/pallas_call | solution.py:820
  138.1 65.7 %feed.1 = (bf16[4,256,1536]{2,1,0:T(8,128)(2,1)}, bf16[256,1536]{1,0:T(8,128)(2,1)}, bf16[2,768,1536]{2,1,0:T(8,128)(2,1)}) custom-call(bf16[256,1536]{1,0:T(8,128)(2,1)} %get-tuple-element.64.rows_in, bf16[4,256,1536]{2,1,0:T(8,128)(2,1)} %get-tuple-element.65.grads_in, bf16[1536,1536]{1,0:T(8,128)(2,1)} %up_in.1, bf16[1536,1536]{1,0:T(8,128)(2,1)} %down_in.1), custom_call_target="tpu_custom_call" | custom-call | tf_op jit(solution)/shard_map/feed/pallas_call | solution.py:1040
  203.8 44.9 %cross_back.1 = (f32[256,1536]{1,0:T(8,128)}, bf16[256,1536]{1,0:T(8,128)(2,1)}, f32[32,1536]{1,0:T(8,128)}, bf16[4,64,768]{2,1,0:T(8,128)(2,1)}, bf16[4,768,384...) custom-call(f32[256,1536]{1,0:T(8,128)} %bitcast.45, ...), custom_call_target="tpu_custom_call" | custom-call | tf_op jit(solution)/shard_map/cross_back/pallas_call | solution.py:1259
  248.7 116.4 %attend_back.1 = (f32[256,1536]{1,0:T(8,128)}, f32[16,1536]{1,0:T(8,128)}, f32[64,1536]{1,0:T(8,128)}, bf16[768,1152]{1,0:T(8,128)(2,1)}, bf16[6,96,1536]{2,1,0:...) custom-call(bf16[256,1536]{1,0:T(8,128)(2,1)} %get-tuple-element.71., ...), custom_call_target="tpu_custom_call", output_to_operand_aliasing={{5}: (15, {})} | custom-call | tf_op jit(solution)/shard_map/attend_back/pallas_call | solution.py:1584
  365.1 115.1 %total.1 = (bf16[3,8,96,384]{3,2,1,0:T(8,128)(2,1)}, bf16[8,96,384]{2,1,0:T(8,128)(2,1)}, bf16[2,96,1536]{2,1,0:T(8,128)(2,1)}, bf16[2,96,1536]{2,1,0:T(8,128)(2...) custom-call(bf16[16,96,1536]{2,1,0:T(8,128)(2,1)} %bitcast.34, ...), custom_call_target="tpu_custom_call", output_to_operand_aliasing={{7}: (11, {}), {8}: (12, {}), {9}: (13, {})} | custom-call | tf_op jit(solution)/shard_map/total/pallas_call | solution.py:1827
  480.2 0.0 copy-start.2
  480.2 1.6 slice_reduce_fusion
  481.9 2.2 bitcast_convert_fusion.3
  484.1 0.0 copy-done.2
  484.1 2.3 reshape.110
  486.4 0.0 copy-done.6
  486.4 1.8 bitcast_convert_fusion.2
  488.2 0.1 copy-done.3
  488.2 2.2 convert_bitcast_fusion
  490.4 0.2 copy-done
  490.6 1.3 copy-done.1
  491.9 5.4 %bitcast_convert_fusion = (f32[768,1536]{1,0:T(8,128)}, f32[768,1536]{1,0:T(8,128)}) fusion(bf16[8,96,1536]{2,1,0:T(8,128)(2,1)S(1)} %copy-done, bf16[8,96,1536]{2,1,0:T(8,128)(2,1)S(1)} %copy-done.1), kind=kLoop, calls=%fused_computation.1 | loop fusion | flops 2359296 | bytes 14155776 | tf_op jit(solution)/shard_map/reshape | solution.py:1897
  497.3 1.1 copy.50
  498.4 0.8 copy-done.4
  499.2 1.1 copy.51
  500.4 0.1 copy-done.8
  500.5 0.7 copy.52
  (11 shorter events, 0.0 us)
Async XLA Ops:
  480.2 3.9 copy-start.2
  481.9 4.5 copy-start.6
  481.9 4.5 copy-start.7
  486.4 1.8 copy-start.3
  488.2 2.4 copy-start
  488.2 3.7 copy-start.1
  491.9 5.4 %copy-start.5 = (f32[256,1536]{1,0:T(8,128)S(1)}, f32[256,1536]{1,0:T(8,128)}, u32[]{:S(2)}) copy-start(f32[256,1536]{1,0:T(8,128)} %get-tuple-element.91) | copy-start | bytes 4718596
  497.3 2.0 copy-start.4
  499.2 1.2 copy-start.8

commit v8 on v7

--- a/solution.py
+++ b/solution.py
@@ -1390,6 +1390,7 @@
         @pl.when(i == 2)
         def _():
             gather.have_y()
+            scatter_m.relay()
 
         @pl.when(i == 3)
         def _():
@@ -1468,7 +1469,6 @@
 
     lax.fori_loop(0, 4, back, 0)
     tick(8)
-    scatter_m.relay()
 
     def take_m(here, total):
         sum_m[here] = total.astype(BF)
@@ -1756,6 +1756,28 @@
     for copy in second:
         copy.start()
     run(begin + 2, begin + 3)
+    scatter_q.relay()
+    scatter_o.relay()
+    loads[-2].wait()
+    loads[-1].wait()
+    scatter_p.diagonal()
+    scatter_p.along_x()
+    scatter_p.along_y()
+    run(begin + 3, at_cq)
+
+    def take_q(rows, value):
+        row = rows.start
+        c = row // chunk
+        own[at_cq + c % quarter, :, cols(c // quarter, local)] = value.astype(BF)
+
+    scatter_q.finish(take_q, chunk)
+    run(at_cq, at_co)
+    step = min(chunk, scatter_o.half)
+
+    def take_o(rows, value):
+        own[at_co + rows.start // chunk, rows_at(rows.start % chunk // step, step)] = value.astype(BF)
+
+    scatter_o.finish(take_o, step)
     for copy in second:
         copy.wait_recv()
     total = share[0, s]
@@ -1766,28 +1788,6 @@
     text_store.start()
     for copy in third:
         copy.start()
-    scatter_q.relay()
-    scatter_o.relay()
-    loads[-2].wait()
-    loads[-1].wait()
-    scatter_p.diagonal()
-    scatter_p.along_x()
-    scatter_p.along_y()
-    run(begin + 3, at_cq)
-
-    def take_q(rows, value):
-        row = rows.start
-        c = row // chunk
-        own[at_cq + c % quarter, :, cols(c // quarter, local)] = value.astype(BF)
-
-    scatter_q.finish(take_q, chunk)
-    run(at_cq, at_co)
-    step = min(chunk, scatter_o.half)
-
-    def take_o(rows, value):
-        own[at_co + rows.start // chunk, rows_at(rows.start % chunk // step, step)] = value.astype(BF)
-
-    scatter_o.finish(take_o, step)
     run(at_co, layout.count)
     scatter_p.relay()
     run(layout.count, end)

time: 502 us -> 492 us (0.980)
  Pallas kernels: 471 us -> 462 us
    pallas_call x1, Pallas kernels: 115 us -> 106 us  [total(): pl.pallas_call(partial(total_kernel, layout), name='total', out_shape=[sh...]
where the time goes in v8:
time: 492 us
  Pallas kernels  462 us (94%)
  local copies, waits for them, and re-layouts  17.8 us (4%)
  other arithmetic  11.6 us (2%)
    pallas_call x1, Pallas kernels, attend_back(): pl.pallas_call(partial(attend_back_kernel, layout), name='attend_back', o...  116 us
    pallas_call x1, Pallas kernels, total(): pl.pallas_call(partial(total_kernel, layout), name='total', out_shape=[sh...  106 us
    pallas_call x1, Pallas kernels, feed(): pl.pallas_call(feed_kernel, name='feed', out_shape=[shape(4, n, m), shape...  65.7 us
    pallas_call x1, Pallas kernels, attend(): pl.pallas_call(attend_kernel, name='attend', out_shape=[shape(4, n, local...  61.6 us
    pallas_call x1, Pallas kernels, cross_back(): pl.pallas_call(partial(cross_back_kernel, layout), name='cross_back', out...  44.9 us
    pallas_call x1, Pallas kernels, enter(): pl.pallas_call(enter_kernel, name='enter', out_shape=[shape(4, n, m), sha...  36.8 us
    pallas_call x1, Pallas kernels, cross(): pl.pallas_call(cross_kernel, name='cross', out_shape=[shape(n, m), shape(...  30.6 us
    unnamed x27, local copies, waits for them, and re-layouts  12.5 us

profile of v8, /device:TPU:0, one launch (start us, length us, event | category | flops | bytes accessed | tf_op | source)
XLA Modules:
  0.0 491.9 jit_solution(3219501357450499138)
XLA Ops:
  0.7 0.7 constant_dynamic-update-slice_fusion.5
  1.4 0.7 constant_dynamic-update-slice_fusion.4
  2.1 0.7 constant_dynamic-update-slice_fusion.3
  2.8 0.7 constant_dynamic-update-slice_fusion.2
  3.5 0.7 constant_dynamic-update-slice_fusion.1
  4.2 0.7 constant_dynamic-update-slice_fusion
  4.9 0.6 reshape.87.gains.gains_in
  5.5 3.5 copy.36
  9.0 36.8 %enter.1 = (bf16[4,256,1536]{2,1,0:T(8,128)(2,1)}, bf16[4,256,1152]{2,1,0:T(8,128)(2,1)}, bf16[4,64,768]{2,1,0:T(8,128)(2,1)}) custom-call(bf16[256,1536]{1,0:T(8,128)(2,1)} %bitcast.41, f32[6,1536]{1,0:T(8,128)} %reshape.87.gains.gains_in, bf16[3,1536,384]{2,1,0:T(8,128)(2,1)} %bitcast.39, bf16[64,1536]{1,0:T(8,128)(2,1)} %bitcast.50, ...), custom_call_target="tpu_custom_call" | custom-call | tf_op jit(solution)/shard_map/enter/pallas_call | solution.py:474
  45.9 61.6 %attend.1 = (bf16[4,256,384]{2,1,0:T(8,128)(2,1)}, f32[4,256,128]{2,1,0:T(8,128)}, f32[256,1536]{1,0:T(8,128)}, bf16[4,1536,384]{2,1,0:T(8,128)(2,1)}, bf16[4,384,1536]{2,1,0:T(8,128)(2,1)}) custom-call(bf16[4,256,1152]{2,1,0:T(8,128)(2,1)} %get-tuple-element.59.triple_in, bf16[384,1536]{1,0:T(8,128)(2,1)} %out_in.3, bf16[256,1536]{1,0:T(8,128)(2,1)} %bitcast.42, ...), custom_call_target="tpu_custom_call" | custom-call | tf_op jit(solution)/shard_map/attend/pallas_call | solution.py:687
  107.5 30.6 %cross.1 = (bf16[256,1536]{1,0:T(8,128)(2,1)}, bf16[256,1536]{1,0:T(8,128)(2,1)}, f32[256,1536]{1,0:T(8,128)}, bf16[256,1536]{1,0:T(8,128)(2,1)}, bf16[4,256,1536]{2,1,0:T(8,128)(2,1)}) custom-call(f32[256,1536]{1,0:T(8,128)} %get-tuple-element.60.after_in.self_in, f32[6,1536]{1,0:T(8,128)} %reshape.87.gains.gains_in, ...), custom_call_target="tpu_custom_call" | custom-call | tf_op jit(solution)/shard_map/cross/pallas_call | solution.py:820
  138.1 65.7 %feed.1 = (bf16[4,256,1536]{2,1,0:T(8,128)(2,1)}, bf16[256,1536]{1,0:T(8,128)(2,1)}, bf16[2,768,1536]{2,1,0:T(8,128)(2,1)}) custom-call(bf16[256,1536]{1,0:T(8,128)(2,1)} %get-tuple-element.64.rows_in, bf16[4,256,1536]{2,1,0:T(8,128)(2,1)} %get-tuple-element.65.grads_in, bf16[1536,1536]{1,0:T(8,128)(2,1)} %up_in.1, bf16[1536,1536]{1,0:T(8,128)(2,1)} %down_in.1), custom_call_target="tpu_custom_call" | custom-call | tf_op jit(solution)/shard_map/feed/pallas_call | solution.py:1040
  203.8 44.9 %cross_back.1 = (f32[256,1536]{1,0:T(8,128)}, bf16[256,1536]{1,0:T(8,128)(2,1)}, f32[32,1536]{1,0:T(8,128)}, bf16[4,64,768]{2,1,0:T(8,128)(2,1)}, bf16[4,768,384...) custom-call(f32[256,1536]{1,0:T(8,128)} %bitcast.45, ...), custom_call_target="tpu_custom_call" | custom-call | tf_op jit(solution)/shard_map/cross_back/pallas_call | solution.py:1259
  248.7 116.4 %attend_back.1 = (f32[256,1536]{1,0:T(8,128)}, f32[16,1536]{1,0:T(8,128)}, f32[64,1536]{1,0:T(8,128)}, bf16[768,1152]{1,0:T(8,128)(2,1)}, bf16[6,96,1536]{2,1,0:...) custom-call(bf16[256,1536]{1,0:T(8,128)(2,1)} %get-tuple-element.71., ...), custom_call_target="tpu_custom_call", output_to_operand_aliasing={{5}: (15, {})} | custom-call | tf_op jit(solution)/shard_map/attend_back/pallas_call | solution.py:1584
  365.1 105.8 %total.1 = (bf16[3,8,96,384]{3,2,1,0:T(8,128)(2,1)}, bf16[8,96,384]{2,1,0:T(8,128)(2,1)}, bf16[2,96,1536]{2,1,0:T(8,128)(2,1)}, bf16[2,96,1536]{2,1,0:T(8,128)(2...) custom-call(bf16[16,96,1536]{2,1,0:T(8,128)(2,1)} %bitcast.34, ...), custom_call_target="tpu_custom_call", output_to_operand_aliasing={{7}: (11, {}), {8}: (12, {}), {9}: (13, {})} | custom-call | tf_op jit(solution)/shard_map/total/pallas_call | solution.py:1827
  470.9 0.0 copy-start.2
  470.9 1.6 slice_reduce_fusion
  472.5 2.2 bitcast_convert_fusion.3
  474.7 0.0 copy-done.2
  474.7 2.3 reshape.110
  477.0 0.0 copy-done.6
  477.0 1.8 bitcast_convert_fusion.2
  478.8 0.1 copy-done.3
  478.9 2.2 convert_bitcast_fusion
  481.1 0.2 copy-done
  481.2 1.3 copy-done.1
  482.5 5.4 %bitcast_convert_fusion = (f32[768,1536]{1,0:T(8,128)}, f32[768,1536]{1,0:T(8,128)}) fusion(bf16[8,96,1536]{2,1,0:T(8,128)(2,1)S(1)} %copy-done, bf16[8,96,1536]{2,1,0:T(8,128)(2,1)S(1)} %copy-done.1), kind=kLoop, calls=%fused_computation.1 | loop fusion | flops 2359296 | bytes 14155776 | tf_op jit(solution)/shard_map/reshape | solution.py:1897
  487.9 1.1 copy.50
  489.0 0.8 copy-done.4
  489.9 1.1 copy.51
  491.0 0.1 copy-done.8
  491.1 0.7 copy.52
  (11 shorter events, 0.0 us)
Async XLA Ops:
  470.9 3.9 copy-start.2
  472.5 4.5 copy-start.6
  472.5 4.5 copy-start.7
  477.0 1.8 copy-start.3
  478.9 2.4 copy-start
  478.9 3.7 copy-start.1
  482.5 5.4 %copy-start.5 = (f32[256,1536]{1,0:T(8,128)S(1)}, f32[256,1536]{1,0:T(8,128)}, u32[]{:S(2)}) copy-start(f32[256,1536]{1,0:T(8,128)} %get-tuple-element.91) | copy-start | bytes 4718596
  487.9 2.0 copy-start.4
  489.9 1.2 copy-start.8

commit v9 on v8

--- a/solution.py
+++ b/solution.py
@@ -596,15 +596,19 @@
         def _():
             query_gather.relay_x()
             query_gather.relay_y()
-            out_gather.start()
-
-        @pl.when(i == 2)
-        def _():
             query_gather.have_x()
             query_gather.have_y()
+            for j, k in spread:
+                if j < 2:
+                    stripped(j, k).start()
+            out_gather.start()
+
+        @pl.when(i == 2)
+        def _():
             query_gather.have_d()
             for j, k in spread:
-                stripped(j, k).start()
+                if j == 2:
+                    stripped(j, k).start()
 
         for blocks in range(1, 5):
 
@@ -1537,6 +1541,7 @@
     for copy in stores[-2:]:
         copy.start()
     tick(14)
+    tick(15)
     for copy in loads[14:]:
         copy.wait()
 
@@ -1554,7 +1559,6 @@
 
     zero = jnp.zeros((8, m), F32)
     gain_sum, bias_sum = lax.fori_loop(0, n // 64, frame_block, (zero, zero))
-    tick(15)
     sums_out[0:8] = gain_sum
     sums_out[8:16] = bias_sum
     stores += [pltpu.make_async_copy(grad_out, o_frames, store.at[3]), pltpu.make_async_copy(sums_out, o_sums, store.at[4])]

time: 492 us -> 492 us (level)
  no operation moved by 1% of the time
where the time goes in v9:
time: 492 us
  Pallas kernels  462 us (94%)
  local copies, waits for them, and re-layouts  17.8 us (4%)
  other arithmetic  11.6 us (2%)
    pallas_call x1, Pallas kernels, attend_back(): pl.pallas_call(partial(attend_back_kernel, layout), name='attend_back', o...  116 us
    pallas_call x1, Pallas kernels, total(): pl.pallas_call(partial(total_kernel, layout), name='total', out_shape=[sh...  106 us
    pallas_call x1, Pallas kernels, feed(): pl.pallas_call(feed_kernel, name='feed', out_shape=[shape(4, n, m), shape...  65.7 us
    pallas_call x1, Pallas kernels, attend(): pl.pallas_call(attend_kernel, name='attend', out_shape=[shape(4, n, local...  61.6 us
    pallas_call x1, Pallas kernels, cross_back(): pl.pallas_call(partial(cross_back_kernel, layout), name='cross_back', out...  44.9 us
    pallas_call x1, Pallas kernels, enter(): pl.pallas_call(enter_kernel, name='enter', out_shape=[shape(4, n, m), sha...  36.8 us
    pallas_call x1, Pallas kernels, cross(): pl.pallas_call(cross_kernel, name='cross', out_shape=[shape(n, m), shape(...  30.6 us
    unnamed x27, local copies, waits for them, and re-layouts  12.5 us

profile of v9, /device:TPU:0, one launch (start us, length us, event | category | flops | bytes accessed | tf_op | source)
XLA Modules:
  0.0 491.9 jit_solution(17383831501897152141)
XLA Ops:
  0.7 0.7 constant_dynamic-update-slice_fusion.5
  1.4 0.7 constant_dynamic-update-slice_fusion.4
  2.1 0.7 constant_dynamic-update-slice_fusion.3
  2.8 0.7 constant_dynamic-update-slice_fusion.2
  3.5 0.7 constant_dynamic-update-slice_fusion.1
  4.2 0.7 constant_dynamic-update-slice_fusion
  4.9 0.6 reshape.87.gains.gains_in
  5.5 3.5 copy.36
  9.0 36.8 %enter.1 = (bf16[4,256,1536]{2,1,0:T(8,128)(2,1)}, bf16[4,256,1152]{2,1,0:T(8,128)(2,1)}, bf16[4,64,768]{2,1,0:T(8,128)(2,1)}) custom-call(bf16[256,1536]{1,0:T(8,128)(2,1)} %bitcast.41, f32[6,1536]{1,0:T(8,128)} %reshape.87.gains.gains_in, bf16[3,1536,384]{2,1,0:T(8,128)(2,1)} %bitcast.39, bf16[64,1536]{1,0:T(8,128)(2,1)} %bitcast.50, ...), custom_call_target="tpu_custom_call" | custom-call | tf_op jit(solution)/shard_map/enter/pallas_call | solution.py:474
  45.9 61.6 %attend.1 = (bf16[4,256,384]{2,1,0:T(8,128)(2,1)}, f32[4,256,128]{2,1,0:T(8,128)}, f32[256,1536]{1,0:T(8,128)}, bf16[4,1536,384]{2,1,0:T(8,128)(2,1)}, bf16[4,384,1536]{2,1,0:T(8,128)(2,1)}) custom-call(bf16[4,256,1152]{2,1,0:T(8,128)(2,1)} %get-tuple-element.59.triple_in, bf16[384,1536]{1,0:T(8,128)(2,1)} %out_in.3, bf16[256,1536]{1,0:T(8,128)(2,1)} %bitcast.42, ...), custom_call_target="tpu_custom_call" | custom-call | tf_op jit(solution)/shard_map/attend/pallas_call | solution.py:691
  107.5 30.6 %cross.1 = (bf16[256,1536]{1,0:T(8,128)(2,1)}, bf16[256,1536]{1,0:T(8,128)(2,1)}, f32[256,1536]{1,0:T(8,128)}, bf16[256,1536]{1,0:T(8,128)(2,1)}, bf16[4,256,1536]{2,1,0:T(8,128)(2,1)}) custom-call(f32[256,1536]{1,0:T(8,128)} %get-tuple-element.60.after_in.self_in, f32[6,1536]{1,0:T(8,128)} %reshape.87.gains.gains_in, ...), custom_call_target="tpu_custom_call" | custom-call | tf_op jit(solution)/shard_map/cross/pallas_call | solution.py:824
  138.1 65.7 %feed.1 = (bf16[4,256,1536]{2,1,0:T(8,128)(2,1)}, bf16[256,1536]{1,0:T(8,128)(2,1)}, bf16[2,768,1536]{2,1,0:T(8,128)(2,1)}) custom-call(bf16[256,1536]{1,0:T(8,128)(2,1)} %get-tuple-element.64.rows_in, bf16[4,256,1536]{2,1,0:T(8,128)(2,1)} %get-tuple-element.65.grads_in, bf16[1536,1536]{1,0:T(8,128)(2,1)} %up_in.1, bf16[1536,1536]{1,0:T(8,128)(2,1)} %down_in.1), custom_call_target="tpu_custom_call" | custom-call | tf_op jit(solution)/shard_map/feed/pallas_call | solution.py:1044
  203.8 44.9 %cross_back.1 = (f32[256,1536]{1,0:T(8,128)}, bf16[256,1536]{1,0:T(8,128)(2,1)}, f32[32,1536]{1,0:T(8,128)}, bf16[4,64,768]{2,1,0:T(8,128)(2,1)}, bf16[4,768,384...) custom-call(f32[256,1536]{1,0:T(8,128)} %bitcast.45, ...), custom_call_target="tpu_custom_call" | custom-call | tf_op jit(solution)/shard_map/cross_back/pallas_call | solution.py:1263
  248.7 116.4 %attend_back.1 = (f32[256,1536]{1,0:T(8,128)}, f32[16,1536]{1,0:T(8,128)}, f32[64,1536]{1,0:T(8,128)}, bf16[768,1152]{1,0:T(8,128)(2,1)}, bf16[6,96,1536]{2,1,0:...) custom-call(bf16[256,1536]{1,0:T(8,128)(2,1)} %get-tuple-element.71., ...), custom_call_target="tpu_custom_call", output_to_operand_aliasing={{5}: (15, {})} | custom-call | tf_op jit(solution)/shard_map/attend_back/pallas_call | solution.py:1588
  365.1 105.8 %total.1 = (bf16[3,8,96,384]{3,2,1,0:T(8,128)(2,1)}, bf16[8,96,384]{2,1,0:T(8,128)(2,1)}, bf16[2,96,1536]{2,1,0:T(8,128)(2,1)}, bf16[2,96,1536]{2,1,0:T(8,128)(2...) custom-call(bf16[16,96,1536]{2,1,0:T(8,128)(2,1)} %bitcast.34, ...), custom_call_target="tpu_custom_call", output_to_operand_aliasing={{7}: (11, {}), {8}: (12, {}), {9}: (13, {})} | custom-call | tf_op jit(solution)/shard_map/total/pallas_call | solution.py:1831
  470.9 0.0 copy-start.2
  470.9 1.6 slice_reduce_fusion
  472.5 2.2 bitcast_convert_fusion.3
  474.7 0.0 copy-done.2
  474.7 2.3 reshape.110
  477.0 0.0 copy-done.6
  477.0 1.8 bitcast_convert_fusion.2
  478.8 0.1 copy-done.3
  478.9 2.2 convert_bitcast_fusion
  481.1 0.2 copy-done
  481.2 1.3 copy-done.1
  482.5 5.4 %bitcast_convert_fusion = (f32[768,1536]{1,0:T(8,128)}, f32[768,1536]{1,0:T(8,128)}) fusion(bf16[8,96,1536]{2,1,0:T(8,128)(2,1)S(1)} %copy-done, bf16[8,96,1536]{2,1,0:T(8,128)(2,1)S(1)} %copy-done.1), kind=kLoop, calls=%fused_computation.1 | loop fusion | flops 2359296 | bytes 14155776 | tf_op jit(solution)/shard_map/reshape | solution.py:1901
  487.9 1.1 copy.50
  489.0 0.8 copy-done.4
  489.9 1.1 copy.51
  491.0 0.1 copy-done.8
  491.1 0.7 copy.52
  (11 shorter events, 0.0 us)
Async XLA Ops:
  470.9 3.9 copy-start.2
  472.5 4.5 copy-start.6
  472.5 4.5 copy-start.7
  477.0 1.8 copy-start.3
  478.9 2.4 copy-start
  478.9 3.7 copy-start.1
  482.5 5.4 %copy-start.5 = (f32[256,1536]{1,0:T(8,128)S(1)}, f32[256,1536]{1,0:T(8,128)}, u32[]{:S(2)}) copy-start(f32[256,1536]{1,0:T(8,128)} %get-tuple-element.91) | copy-start | bytes 4718596
  487.9 2.0 copy-start.4
  489.9 1.2 copy-start.8
